TPU v7x, 32 devices: a whole 2x2x4 slice. The times are simulated.
32 devices in a mesh: gx: 4 (over y, x), gy: 8 (over z, core).
Axes of the slice: x: 2, y: 2, z: 4, core: 2. Of those that a mesh axis runs over, the one named last changes fastest.
Arguments:
- density: float32 [32, 32, 128], P('gx', 'gy'), may hold values from -5 to 5
- susceptibility: float32 [32, 32, 128], P('gx', 'gy'), may hold values from -5 to 5
- station_cell: int32 [2, 1024], P(None, 'gx'), may hold values from 0 to 1023
- station_line: int32 [2, 1024], P(None, 'gx'), may hold values from 0 to 255, as said below
- observed: float32 [2, 1024], P(None, 'gx'), may hold values from -3 to 3
- data_weight: float32 [2, 1024], P(None, 'gx'), may hold values from 0.5 to 2
- trial_steps: float32 [8], replicated, may hold values from 0.05 to 0.5
Outputs:
- data_gradient: float32 [2, 32, 32, 128], P(None, 'gx', 'gy')
- cross_force: float32 [2, 32, 32, 128], P(None, 'gx', 'gy')
- weighted_residual: float32 [2, 1024], P(None, 'gx')
- trial_values: float32 [8], replicated
Inputs may be any that keep to these rules, and one draw needn't show every extreme that they name: `station_line`: one or more survey lines hold no station of either field.
All inputs are finite; a program needn't handle non-finite values. Where the computation divides by a largest or mean magnitude, that divisor is 1e-20 or more.
Results may differ from a plain program's by a relative error of at most 0.0003.
Values sent between devices are 32-bit elements; how exact they have to be, the bound alone decides.
No kernel may reach another device: no remote copies, remote signals or barrier semaphores. Data moves between devices by JAX's collectives and lax.ppermute only.
A program may use at most 64 MiB of HBM per device.

v0:
```python
import math

import jax
import jax.numpy as jnp
from jax import lax
from jax.sharding import PartitionSpec as P

LINES = 256


cell_depth = 2.0
lift = 1.0
coupling_scale = 0.05
highest = lax.Precision.HIGHEST


def extended_2(block, sides, width):
    for axis, dim in sides:
        count = lax.axis_size(axis)
        forward = [(i, i + 1) for i in range(count - 1)]
        backward = [(target, source) for source, target in forward]
        low = lax.ppermute(
            lax.slice_in_dim(block, block.shape[dim] - width, None, axis=dim), axis, forward
        )
        high = lax.ppermute(lax.slice_in_dim(block, 0, width, axis=dim), axis, backward)
        block = jnp.concatenate([low, block, high], axis=dim)
    return block


def kernel_tile(field, station_x, station_y, cell_x, cell_y, depth):
    gap_x = station_x[:, None] - cell_x[None, :]
    gap_y = station_y[:, None] - cell_y[None, :]
    depth_row = depth[None, :]
    radius_sq = gap_x * gap_x + gap_y * gap_y + depth_row * depth_row
    inverse = lax.rsqrt(radius_sq)
    cube = inverse * inverse * inverse
    if field == 0:
        return depth_row * cube
    return (3.0 * depth_row * depth_row - radius_sq) * cube * inverse * inverse


def cell_coords(anchor_x, anchor_y, width, layers, start, count):
    position = start + jnp.arange(count, dtype=jnp.int32)
    cell_x = (anchor_x + position // (width * layers)).astype(jnp.float32)
    cell_y = (anchor_y + position // layers % width).astype(jnp.float32)
    depth = ((position % layers).astype(jnp.float32) + 0.5) * cell_depth + lift
    return (cell_x, cell_y, depth)


def to_blocks(values, size):
    return jnp.swapaxes(values.reshape(2, -1, size), 0, 1)


def forward_part(models, anchor_x, anchor_y, station_x, station_y):
    rows, width, layers = (models.shape[1], models.shape[2], models.shape[3])
    cells = rows * width * layers
    flat = models.reshape(2, cells)
    cell_block = math.gcd(cells, 2048)
    station_block = math.gcd(station_x.shape[1], 64)

    def forward_station_turn(pair):
        block_x, block_y = pair

        def forward_cell_turn(index, total):
            start = index * cell_block
            cell_x, cell_y, depth = cell_coords(
                anchor_x, anchor_y, width, layers, start, cell_block
            )
            piece = lax.dynamic_slice_in_dim(flat, start, cell_block, 1)
            rows_out = [
                jnp.dot(
                    kernel_tile(field, block_x[field], block_y[field], cell_x, cell_y, depth),
                    piece[field],
                    precision=highest,
                )
                for field in range(2)
            ]
            return total + jnp.stack(rows_out)

        return lax.fori_loop(
            0, cells // cell_block, forward_cell_turn, jnp.zeros((2, station_block), jnp.float32)
        )

    parts = lax.map(
        forward_station_turn,
        (to_blocks(station_x, station_block), to_blocks(station_y, station_block)),
    )
    return jnp.swapaxes(parts, 0, 1).reshape(2, -1)


def adjoint_part(source, anchor_x, anchor_y, rows, width, layers, station_x, station_y):
    cells = rows * width * layers
    cell_block = math.gcd(cells, 2048)
    station_block = math.gcd(station_x.shape[1], 64)

    def adjoint_cell_turn(index):
        start = index * cell_block
        cell_x, cell_y, depth = cell_coords(anchor_x, anchor_y, width, layers, start, cell_block)

        def cell_station_turn(turn, total):
            first = turn * station_block
            block_x = lax.dynamic_slice_in_dim(station_x, first, station_block, 1)
            block_y = lax.dynamic_slice_in_dim(station_y, first, station_block, 1)
            block_source = lax.dynamic_slice_in_dim(source, first, station_block, 1)
            rows_out = [
                jnp.dot(
                    block_source[field],
                    kernel_tile(field, block_x[field], block_y[field], cell_x, cell_y, depth),
                    precision=highest,
                )
                for field in range(2)
            ]
            return total + jnp.stack(rows_out)

        return lax.fori_loop(
            0,
            station_x.shape[1] // station_block,
            cell_station_turn,
            jnp.zeros((2, cell_block), jnp.float32),
        )

    parts = lax.map(adjoint_cell_turn, jnp.arange(cells // cell_block, dtype=jnp.int32))
    return jnp.swapaxes(parts, 0, 1).reshape(2, rows, width, layers)


def cross_terms(extended, start_x, start_y, total_x, total_y):
    rows = extended.shape[1] - 1
    width = extended.shape[2] - 1
    global_x = start_x - 1 + jnp.arange(rows, dtype=jnp.int32)
    global_y = start_y - 1 + jnp.arange(width, dtype=jnp.int32)
    mask_x = (global_x < total_x - 1).astype(jnp.float32)[:, None, None]
    mask_y = (global_y < total_y - 1).astype(jnp.float32)[None, :, None]
    valid = ((global_x >= 0)[:, None] & (global_y >= 0)[None, :]).astype(jnp.float32)[:, :, None]

    def diffs(field):
        base = field[:-1, :-1, :]
        along_x = (field[1:, :-1, :] - base) * mask_x
        along_y = (field[:-1, 1:, :] - base) * mask_y
        along_z = jnp.concatenate(
            [base[:, :, 1:] - base[:, :, :-1], jnp.zeros_like(base[:, :, :1])], axis=2
        )
        return (along_x, along_y, along_z)

    first_x, first_y, first_z = diffs(extended[0])
    second_x, second_y, second_z = diffs(extended[1])
    part_one = first_y * second_z - first_z * second_y
    part_two = first_z * second_x - first_x * second_z
    part_three = first_x * second_y - first_y * second_x
    return (part_one * part_one + part_two * part_two + part_three * part_three) * valid


def line_totals(values, lines):
    labels = jnp.arange(LINES, dtype=jnp.int32)
    onehot = (lines[:, :, None] == labels).astype(jnp.float32)
    local = jnp.einsum("fs,fsl->fl", values, onehot, precision=highest)
    return lax.psum(local, "gx")


def spread_table(table, lines):
    labels = jnp.arange(LINES, dtype=jnp.int32)
    onehot = (lines[:, :, None] == labels).astype(jnp.float32)
    return jnp.einsum("fl,fsl->fs", table, onehot, precision=highest)


def faces(fields):
    return extended_2(fields, (("gx", 1), ("gy", 2)), 1)


def body(density, susceptibility, station_cell, station_line, observed, data_weight, trial_steps):
    rows, width, layers = density.shape
    groups = lax.axis_size("gx")
    columns = lax.axis_size("gy")
    total_x = rows * groups
    total_y = width * columns
    own_count = station_cell.shape[1]
    total_stations = own_count * groups
    anchor_x = lax.axis_index("gx") * rows
    anchor_y = lax.axis_index("gy") * width
    models = jnp.stack([density, susceptibility])
    own_x = (station_cell // total_y).astype(jnp.float32)
    own_y = (station_cell % total_y).astype(jnp.float32)
    coupling = coupling_scale * total_stations / (total_x * total_y * layers)

    def energies(extended):
        squares = cross_terms(extended, anchor_x, anchor_y, total_x, total_y)
        return (0.5 * jnp.sum(squares), 0.5 * jnp.sum(squares[1:, 1:]))

    extended = faces(models)
    (rim_energy, model_energy), rim_grad = jax.value_and_grad(energies, has_aux=True)(extended)
    cross_force = rim_grad[:, 1:-1, 1:-1, :]

    def fold_forward(piece, start):
        return forward_part(piece, start, anchor_y, own_x, own_y)

    def column_data(fields):
        partial_value = fold_forward(lax.all_gather(fields, "gx", axis=1, tiled=True), jnp.int32(0))
        return lax.psum(partial_value, "gy")

    predicted = column_data(models)
    misfit = predicted - observed
    both_lines = jnp.concatenate([station_line, station_line])
    first_totals = line_totals(jnp.concatenate([misfit, jnp.ones_like(misfit)]), both_lines)
    counts = jnp.maximum(first_totals[2:], 1.0)
    residual = misfit - spread_table(first_totals[:2] / counts, station_line)
    weighted_residual = data_weight * residual
    source = data_weight * weighted_residual
    source = source - spread_table(line_totals(source, station_line) / counts, station_line)
    data_gradient = jnp.swapaxes(
        lax.psum_scatter(
            jnp.swapaxes(
                adjoint_part(
                    source,
                    jnp.int32(0),
                    anchor_y,
                    lax.axis_size("gx") * rows,
                    width,
                    layers,
                    own_x,
                    own_y,
                ),
                0,
                1,
            ),
            "gx",
            scatter_dimension=0,
            tiled=True,
        ),
        0,
        1,
    )
    gradient = data_gradient + coupling * cross_force
    peak = lax.pmax(jnp.max(jnp.abs(gradient)), ("gx", "gy")) + 1e-06
    direction = gradient / peak
    extended_direction = faces(direction)
    image = column_data(direction)
    change = image - spread_table(line_totals(image, station_line) / counts, station_line)
    shares = []
    for trial in range(trial_steps.shape[0]):
        step = trial_steps[trial]
        moved = data_weight * (residual - step * change)
        data_value = 0.5 * jnp.sum(moved * moved)
        own_extended = extended - step * extended_direction
        shares.append(
            data_value / columns
            + coupling
            * (
                0.5
                * jnp.sum(cross_terms(own_extended, anchor_x, anchor_y, total_x, total_y)[1:, 1:])
            )
        )
    trial_values = lax.psum(jnp.stack(shares), ("gx", "gy")) / (2 * total_stations)
    return (data_gradient, cross_force, weighted_residual, trial_values)


def solution(mesh):
    placed = (
        P("gx", "gy", None),
        P("gx", "gy", None),
        P(None, "gx"),
        P(None, "gx"),
        P(None, "gx"),
        P(None, "gx"),
        P(),
    )
    return jax.shard_map(
        body,
        mesh=mesh,
        in_specs=placed,
        out_specs=(P(None, "gx", "gy", None), P(None, "gx", "gy", None), P(None, "gx"), P()),
        check_vma=False,
    )
```

profile of v0, /device:TPU:0, one launch (start us, length us, event | category | flops | bytes accessed | tf_op | source)
XLA Modules:
  0.0 424.1 jit_solution(3316433478356458403)
XLA Ops:
  8.0 4.9 %collective-permute-start = (f32[2,1,4,128]{3,2,1,0:T(4,128)S(1)}, f32[2,1,4,128]{3,2,1,0:T(4,128)S(1)}, u32[]{:S(2)}, u32[]{:S(2)}) collective-permute-start(f32[2,1,4,128]{3,2,1,0:T(4,128)S(1)} %get-tuple-element.1306), channel_id=1, source_target_pairs={{0,8},{8,16},{16,24},{1,9},{9,17},{17,25},{2,10},{10,18},{18,26},{... | collective-permute-start | bytes 12296 | tf_op jit(solution)/shard_map/ppermute | solution.py:22
  14.2 10.6 %all_gather.6 = f32[2,32,4,128]{3,2,1,0:T(4,128)S(1)} all-gather(f32[2,8,4,128]{3,2,1,0:T(4,128)S(1)} %pad_maximum_fusion.2), channel_id=1, replica_groups=mesh['gx'=4,'gy'=8] {'gx'}, dimensions={1}, use_global_device_ids=true | all-gather | bytes 163840 | tf_op jit(solution)/shard_map/all_gather | solution.py:196
  25.7 53.3 %while.116 = (s32[]{:T(128)}, f32[4,2,64]{2,1,0:T(2,128)S(1)}, f32[4,2,64]{2,1,0:T(2,128)S(1)}, f32[4,2,64]{2,1,0:T(2,128)S(1)}, s32[]{:T(128)}, /*index=5*/f32[...) while((s32[]{:T(128)}, f32[4,2,64]{2,1,0:T(2,128)S(1)}, ...), condition=%wide.region_3.4_spmd, body=%wide.region_0.3_spmd.sunk | while | flops 6052234 | bytes 133554 | solution.py:84
  25.7 13.3 %while.121 = (s32[]{:T(128)}, f32[2,64]{1,0:T(2,128)S(1)}, f32[2,64]{1,0:T(2,128)S(1)}, f32[2,64]{1,0:T(2,128)S(1)}, s32[]{:T(128)}, /*index=5*/f32[2,16384]{1,0...) while((s32[]{:T(128)}, f32[2,64]{1,0:T(2,128)S(1)}, ...), condition=%wide.region_2.2_spmd.clone, body=%wide.region_1.1_spmd.clone.sunk | while | flops 6052232 | bytes 129229 | solution.py:80
  39.0 13.3 %while.121 = (s32[]{:T(128)}, f32[2,64]{1,0:T(2,128)S(1)}, f32[2,64]{1,0:T(2,128)S(1)}, f32[2,64]{1,0:T(2,128)S(1)}, s32[]{:T(128)}, /*index=5*/f32[2,16384]{1,0...) while((s32[]{:T(128)}, f32[2,64]{1,0:T(2,128)S(1)}, ...), condition=%wide.region_2.2_spmd.clone, body=%wide.region_1.1_spmd.clone.sunk | while | flops 6052232 | bytes 129229 | solution.py:80
  52.4 13.3 %while.121 = (s32[]{:T(128)}, f32[2,64]{1,0:T(2,128)S(1)}, f32[2,64]{1,0:T(2,128)S(1)}, f32[2,64]{1,0:T(2,128)S(1)}, s32[]{:T(128)}, /*index=5*/f32[2,16384]{1,0...) while((s32[]{:T(128)}, f32[2,64]{1,0:T(2,128)S(1)}, ...), condition=%wide.region_2.2_spmd.clone, body=%wide.region_1.1_spmd.clone.sunk | while | flops 6052232 | bytes 129229 | solution.py:80
  65.7 13.3 %while.121 = (s32[]{:T(128)}, f32[2,64]{1,0:T(2,128)S(1)}, f32[2,64]{1,0:T(2,128)S(1)}, f32[2,64]{1,0:T(2,128)S(1)}, s32[]{:T(128)}, /*index=5*/f32[2,16384]{1,0...) while((s32[]{:T(128)}, f32[2,64]{1,0:T(2,128)S(1)}, ...), condition=%wide.region_2.2_spmd.clone, body=%wide.region_1.1_spmd.clone.sunk | while | flops 6052232 | bytes 129229 | solution.py:80
  79.1 14.1 %psum.42 = f32[2,256]{1,0:T(2,128)S(1)} all-reduce(f32[2,256]{1,0:T(2,128)S(1)} %reshape.283), channel_id=1, replica_groups=mesh['gx'=4,'gy'=8] {'gy'}, use_global_device_ids=true, to_apply=%region_4.5 | all-reduce | flops 512 | bytes 4096 | tf_op jit(solution)/shard_map/psum | solution.py:197
  94.4 8.9 %psum.43 = f32[4,256]{1,0:T(4,128)S(1)} all-reduce(f32[4,256]{1,0:T(4,128)S(1)} %bitcast.234), channel_id=1, replica_groups=mesh['gx'=4,'gy'=8] {'gx'}, use_global_device_ids=true, to_apply=%region_5.6 | all-reduce | flops 1024 | bytes 8192 | tf_op jit(solution)/shard_map/psum | solution.py:156
  104.9 8.3 %psum.44 = f32[2,256]{1,0:T(2,128)S(1)} all-reduce(f32[2,256]{1,0:T(2,128)S(1)} %bitcast.238), channel_id=1, replica_groups=mesh['gx'=4,'gy'=8] {'gx'}, use_global_device_ids=true, to_apply=%region_6.7 | all-reduce | flops 512 | bytes 4096 | tf_op jit(solution)/shard_map/psum | solution.py:156
  113.6 60.8 %while.118 = (s32[]{:T(128)}, f32[8,2,2048]{2,1,0:T(2,128)S(1)}, s32[8]{0:T(128)S(1)}, s32[]{:T(128)}, f32[2,256]{1,0:T(2,128)S(1)}, /*index=5*/f32[2,256]{1,0:T...) while((s32[]{:T(128)}, f32[8,2,2048]{2,1,0:T(2,128)S(1)}, ...), condition=%wide.region_10.11_spmd, body=%wide.region_7.10_spmd.sunk | while | flops 6064138 | bytes 213438 | solution.py:122
  114.9 6.3 %while.122 = (s32[]{:T(128)}, f32[2,2048]{1,0:T(2,128)S(1)}, f32[2,256]{1,0:T(2,128)S(1)}, f32[2,256]{1,0:T(2,128)S(1)}, f32[2,256]{1,0:T(2,128)S(1)}, /*index=5...) while((s32[]{:T(128)}, f32[2,2048]{1,0:T(2,128)S(1)}, ...), condition=%wide.region_9.9_spmd.clone.clone.clone, body=%wide.region_8.8_spmd.clone.clone.clone.sunk | while | flops 6064135 | bytes 180413 | solution.py:115
  122.5 6.3 %while.122 = (s32[]{:T(128)}, f32[2,2048]{1,0:T(2,128)S(1)}, f32[2,256]{1,0:T(2,128)S(1)}, f32[2,256]{1,0:T(2,128)S(1)}, f32[2,256]{1,0:T(2,128)S(1)}, /*index=5...) while((s32[]{:T(128)}, f32[2,2048]{1,0:T(2,128)S(1)}, ...), condition=%wide.region_9.9_spmd.clone.clone.clone, body=%wide.region_8.8_spmd.clone.clone.clone.sunk | while | flops 6064135 | bytes 180413 | solution.py:115
  130.1 6.3 %while.122 = (s32[]{:T(128)}, f32[2,2048]{1,0:T(2,128)S(1)}, f32[2,256]{1,0:T(2,128)S(1)}, f32[2,256]{1,0:T(2,128)S(1)}, f32[2,256]{1,0:T(2,128)S(1)}, /*index=5...) while((s32[]{:T(128)}, f32[2,2048]{1,0:T(2,128)S(1)}, ...), condition=%wide.region_9.9_spmd.clone.clone.clone, body=%wide.region_8.8_spmd.clone.clone.clone.sunk | while | flops 6064135 | bytes 180413 | solution.py:115
  137.7 6.3 %while.122 = (s32[]{:T(128)}, f32[2,2048]{1,0:T(2,128)S(1)}, f32[2,256]{1,0:T(2,128)S(1)}, f32[2,256]{1,0:T(2,128)S(1)}, f32[2,256]{1,0:T(2,128)S(1)}, /*index=5...) while((s32[]{:T(128)}, f32[2,2048]{1,0:T(2,128)S(1)}, ...), condition=%wide.region_9.9_spmd.clone.clone.clone, body=%wide.region_8.8_spmd.clone.clone.clone.sunk | while | flops 6064135 | bytes 180413 | solution.py:115
  145.3 6.3 %while.122 = (s32[]{:T(128)}, f32[2,2048]{1,0:T(2,128)S(1)}, f32[2,256]{1,0:T(2,128)S(1)}, f32[2,256]{1,0:T(2,128)S(1)}, f32[2,256]{1,0:T(2,128)S(1)}, /*index=5...) while((s32[]{:T(128)}, f32[2,2048]{1,0:T(2,128)S(1)}, ...), condition=%wide.region_9.9_spmd.clone.clone.clone, body=%wide.region_8.8_spmd.clone.clone.clone.sunk | while | flops 6064135 | bytes 180413 | solution.py:115
  152.9 6.3 %while.122 = (s32[]{:T(128)}, f32[2,2048]{1,0:T(2,128)S(1)}, f32[2,256]{1,0:T(2,128)S(1)}, f32[2,256]{1,0:T(2,128)S(1)}, f32[2,256]{1,0:T(2,128)S(1)}, /*index=5...) while((s32[]{:T(128)}, f32[2,2048]{1,0:T(2,128)S(1)}, ...), condition=%wide.region_9.9_spmd.clone.clone.clone, body=%wide.region_8.8_spmd.clone.clone.clone.sunk | while | flops 6064135 | bytes 180413 | solution.py:115
  160.5 6.3 %while.122 = (s32[]{:T(128)}, f32[2,2048]{1,0:T(2,128)S(1)}, f32[2,256]{1,0:T(2,128)S(1)}, f32[2,256]{1,0:T(2,128)S(1)}, f32[2,256]{1,0:T(2,128)S(1)}, /*index=5...) while((s32[]{:T(128)}, f32[2,2048]{1,0:T(2,128)S(1)}, ...), condition=%wide.region_9.9_spmd.clone.clone.clone, body=%wide.region_8.8_spmd.clone.clone.clone.sunk | while | flops 6064135 | bytes 180413 | solution.py:115
  168.1 6.3 %while.122 = (s32[]{:T(128)}, f32[2,2048]{1,0:T(2,128)S(1)}, f32[2,256]{1,0:T(2,128)S(1)}, f32[2,256]{1,0:T(2,128)S(1)}, f32[2,256]{1,0:T(2,128)S(1)}, /*index=5...) while((s32[]{:T(128)}, f32[2,2048]{1,0:T(2,128)S(1)}, ...), condition=%wide.region_9.9_spmd.clone.clone.clone, body=%wide.region_8.8_spmd.clone.clone.clone.sunk | while | flops 6064135 | bytes 180413 | solution.py:115
  181.4 33.5 %all-reduce.34.cloned.1.call-done = f32[32,2,4,128]{3,2,0,1:T(4,128)} async-done(((f32[32,2,4,128]{3,2,0,1:T(4,128)}), f32[32,2,4,128]{3,2,0,1:T(4,128)}) %all-reduce.34.cloned.1.call-update) | async-done | bytes 131088
  216.3 39.4 %pmax.7 = f32[]{:T(128)} all-reduce(f32[]{:T(128)} %get-tuple-element.1187), channel_id=1, replica_groups=mesh['gx'=4,'gy'=8] {'gx','gy'}, use_global_device_ids=true, to_apply=%region_13.14 | all-reduce | flops 1 | bytes 8 | tf_op jit(solution)/shard_map/pmax | solution.py:232
  256.5 9.5 %all_gather.7 = f32[2,32,4,128]{3,2,1,0:T(4,128)S(1)} all-gather(f32[2,8,4,128]{3,2,1,0:T(4,128)S(1)} %broadcast_divide_fusion), channel_id=1, replica_groups=mesh['gx'=4,'gy'=8] {'gx'}, dimensions={1}, use_global_device_ids=true | all-gather | bytes 163840 | tf_op jit(solution)/shard_map/all_gather | solution.py:196
  266.0 3.4 collective-permute-start.4
  270.7 53.4 %while.120 = (s32[]{:T(128)}, f32[4,2,64]{2,1,0:T(2,128)S(1)}, f32[4,2,64]{2,1,0:T(2,128)S(1)}, f32[4,2,64]{2,1,0:T(2,128)S(1)}, s32[]{:T(128)}, /*index=5*/f32[...) while((s32[]{:T(128)}, f32[4,2,64]{2,1,0:T(2,128)S(1)}, ...), condition=%wide.region_17.18_spmd, body=%wide.region_14.17_spmd.sunk | while | flops 6052234 | bytes 133554 | solution.py:84
  270.8 13.3 %while.123 = (s32[]{:T(128)}, f32[2,64]{1,0:T(2,128)S(1)}, f32[2,64]{1,0:T(2,128)S(1)}, f32[2,64]{1,0:T(2,128)S(1)}, s32[]{:T(128)}, /*index=5*/f32[2,16384]{1,0...) while((s32[]{:T(128)}, f32[2,64]{1,0:T(2,128)S(1)}, ...), condition=%wide.region_16.16_spmd.clone, body=%wide.region_15.15_spmd.clone.sunk | while | flops 6052232 | bytes 129229 | solution.py:80
  284.1 13.3 %while.123 = (s32[]{:T(128)}, f32[2,64]{1,0:T(2,128)S(1)}, f32[2,64]{1,0:T(2,128)S(1)}, f32[2,64]{1,0:T(2,128)S(1)}, s32[]{:T(128)}, /*index=5*/f32[2,16384]{1,0...) while((s32[]{:T(128)}, f32[2,64]{1,0:T(2,128)S(1)}, ...), condition=%wide.region_16.16_spmd.clone, body=%wide.region_15.15_spmd.clone.sunk | while | flops 6052232 | bytes 129229 | solution.py:80
  297.5 13.3 %while.123 = (s32[]{:T(128)}, f32[2,64]{1,0:T(2,128)S(1)}, f32[2,64]{1,0:T(2,128)S(1)}, f32[2,64]{1,0:T(2,128)S(1)}, s32[]{:T(128)}, /*index=5*/f32[2,16384]{1,0...) while((s32[]{:T(128)}, f32[2,64]{1,0:T(2,128)S(1)}, ...), condition=%wide.region_16.16_spmd.clone, body=%wide.region_15.15_spmd.clone.sunk | while | flops 6052232 | bytes 129229 | solution.py:80
  310.8 13.3 %while.123 = (s32[]{:T(128)}, f32[2,64]{1,0:T(2,128)S(1)}, f32[2,64]{1,0:T(2,128)S(1)}, f32[2,64]{1,0:T(2,128)S(1)}, s32[]{:T(128)}, /*index=5*/f32[2,16384]{1,0...) while((s32[]{:T(128)}, f32[2,64]{1,0:T(2,128)S(1)}, ...), condition=%wide.region_16.16_spmd.clone, body=%wide.region_15.15_spmd.clone.sunk | while | flops 6052232 | bytes 129229 | solution.py:80
  324.2 13.6 %psum.45 = f32[2,256]{1,0:T(2,128)S(1)} all-reduce(f32[2,256]{1,0:T(2,128)S(1)} %reshape.286), channel_id=1, replica_groups=mesh['gx'=4,'gy'=8] {'gy'}, use_global_device_ids=true, to_apply=%region_18.19 | all-reduce | flops 512 | bytes 4096 | tf_op jit(solution)/shard_map/psum | solution.py:197
  338.1 10.1 %psum.46 = f32[2,256]{1,0:T(2,128)S(1)} all-reduce(f32[2,256]{1,0:T(2,128)S(1)} %bitcast.239), channel_id=1, replica_groups=mesh['gx'=4,'gy'=8] {'gx'}, use_global_device_ids=true, to_apply=%region_19.20 | all-reduce | flops 512 | bytes 4096 | tf_op jit(solution)/shard_map/psum | solution.py:156
  351.2 5.7 %multiply_reduce_fusion.8 = (f32[]{:T(128)}, f32[]{:T(128)}, f32[]{:T(128)}, f32[]{:T(128)}, f32[]{:T(128)}, /*index=5*/f32[]{:T(128)}, f32[]{:T(128)}, f32[]{:T(128)}) fusion(f32[2,256]{1,0:T(2,128)S(1)} %copy-done.5, f32[2,256]{1,0:T(2,128)S(1)} %get-tuple-element.1211, f32[]{:T(128)} %bitcast.61, f32[]{:T(128)} %bitcast.53, f32[]{:T(128)} %bitcast.49, ...), kind=kLoop, calls=%fused_computation.436 | loop fusion | flops 20984 | bytes 8256 | tf_op jit(solution)/shard_map/reduce_sum | solution.py:241
  376.7 40.0 %psum.47 = f32[8]{0:T(128)S(1)} all-reduce(f32[8]{0:T(128)S(1)} %stack.131), channel_id=1, replica_groups=mesh['gx'=4,'gy'=8] {'gx','gy'}, use_global_device_ids=true, to_apply=%region_36.37 | all-reduce | flops 8 | bytes 64 | tf_op jit(solution)/shard_map/psum | solution.py:251
  (951 shorter events, 186.4 us)
Async XLA Ops:
  7.2 207.8 %all-reduce.34.cloned.1.call-start = ((), (), s32[]{:S(2)}) async-start(), calls=%async_computation | async-start | bytes 262144
  7.2 6.9 %copy-start = (f32[8,4,128]{2,1,0:T(4,128)S(1)}, f32[8,4,128]{2,1,0:T(4,128)}, u32[]{:S(2)}) copy-start(f32[8,4,128]{2,1,0:T(4,128)} %param.19) | copy-start | bytes 49156
  7.2 6.9 %copy-start.1 = (f32[8,4,128]{2,1,0:T(4,128)S(1)}, f32[8,4,128]{2,1,0:T(4,128)}, u32[]{:S(2)}) copy-start(f32[8,4,128]{2,1,0:T(4,128)} %param.20) | copy-start | bytes 49156
  8.0 167.5 %collective-permute-start = (f32[2,1,4,128]{3,2,1,0:T(4,128)S(1)}, f32[2,1,4,128]{3,2,1,0:T(4,128)S(1)}, u32[]{:S(2)}, u32[]{:S(2)}) collective-permute-start(f32[2,1,4,128]{3,2,1,0:T(4,128)S(1)} %get-tuple-element.1306), channel_id=1, source_target_pairs={{0,8},{8,16},{16,24},{1,9},{9,17},{17,25},{2,10},{10,18},{18,26},{... | collective-permute-start | bytes 12296 | tf_op jit(solution)/shard_map/ppermute | solution.py:22
  12.9 162.7 %collective-permute-start.1 = (f32[2,1,4,128]{3,2,1,0:T(4,128)S(1)}, f32[2,1,4,128]{3,2,1,0:T(4,128)S(1)}, u32[]{:S(2)}, u32[]{:S(2)}) collective-permute-start(f32[2,1,4,128]{3,2,1,0:T(4,128)S(1)} %get-tuple-element.1307), channel_id=1, source_target_pairs={{8,0},{16,8},{24,16},{9,1},{17,9},{25,17},{10,2},{18,10},{26,18},{... | collective-permute-start | bytes 12296 | tf_op jit(solution)/shard_map/ppermute | solution.py:25
  24.8 0.7 copy-start.6
  79.1 14.1 %copy-start.7 = (f32[2,256]{1,0:T(2,128)S(1)}, f32[2,256]{1,0:T(2,128)}, u32[]{:S(2)}) copy-start(f32[2,256]{1,0:T(2,128)} %param.23) | copy-start | bytes 6148
  93.2 0.7 copy-start.8
  103.3 0.7 copy-start.5
  175.6 2.6 copy-start.4
  175.6 5.3 %collective-permute-start.2 = (f32[2,10,1,128]{3,2,1,0:T(1,128)S(1)}, f32[2,10,1,128]{3,2,1,0:T(1,128)S(1)}, u32[]{:S(2)}, u32[]{:S(2)}) collective-permute-start(f32[2,10,1,128]{3,2,1,0:T(1,128)S(1)} %get-tuple-element.1302), channel_id=1, source_target_pairs={{0,1},{1,2},{2,3},{3,4},{4,5},{5,6},{6,7},{8,9},{9,10},{10,11},{11... | collective-permute-start | bytes 30728 | tf_op jit(solution)/shard_map/ppermute | solution.py:22
  176.9 4.0 collective-permute-start.3
  178.9 0.7 copy-start.9
  216.3 40.1 %copy-start.2 = (f32[2,8,4,128]{3,2,1,0:T(4,128)}, f32[2,8,4,128]{3,2,1,0:T(4,128)S(1)}, u32[]{:S(2)}) copy-start(f32[2,8,4,128]{3,2,1,0:T(4,128)S(1)} %get-tuple-element.1188) | copy-start | bytes 98308
  216.3 40.1 %copy-start.3 = (f32[2,8,4,128]{3,2,1,0:T(4,128)}, f32[2,8,4,128]{3,2,1,0:T(4,128)S(1)}, u32[]{:S(2)}) copy-start(f32[2,8,4,128]{3,2,1,0:T(4,128)S(1)} %get-tuple-element.1189) | copy-start | bytes 98308
  266.0 82.6 %collective-permute-start.4 = (f32[2,1,4,128]{3,2,1,0:T(4,128)S(1)}, f32[2,1,4,128]{3,2,1,0:T(4,128)S(1)}, u32[]{:S(2)}, u32[]{:S(2)}) collective-permute-start(f32[2,1,4,128]{3,2,1,0:T(4,128)S(1)} %get-tuple-element.1304), channel_id=1, source_target_pairs={{0,8},{8,16},{16,24},{1,9},{9,17},{17,25},{2,10},{10,18},{18,26},{... | collective-permute-start | bytes 12296 | tf_op jit(solution)/shard_map/ppermute | solution.py:22
  269.3 79.3 %collective-permute-start.5 = (f32[2,1,4,128]{3,2,1,0:T(4,128)S(1)}, f32[2,1,4,128]{3,2,1,0:T(4,128)S(1)}, u32[]{:S(2)}, u32[]{:S(2)}) collective-permute-start(f32[2,1,4,128]{3,2,1,0:T(4,128)S(1)} %get-tuple-element.1305), channel_id=1, source_target_pairs={{8,0},{16,8},{24,16},{9,1},{17,9},{25,17},{10,2},{18,10},{26,18},{... | collective-permute-start | bytes 12296 | tf_op jit(solution)/shard_map/ppermute | solution.py:25
  348.6 13.2 %collective-permute-start.6 = (f32[2,10,1,128]{3,2,1,0:T(1,128)S(1)}, f32[2,10,1,128]{3,2,1,0:T(1,128)S(1)}, u32[]{:S(2)}, u32[]{:S(2)}) collective-permute-start(f32[2,10,1,128]{3,2,1,0:T(1,128)S(1)} %get-tuple-element.1300), channel_id=1, source_target_pairs={{0,1},{1,2},{2,3},{3,4},{4,5},{5,6},{6,7},{8,9},{9,10},{10,11},{11... | collective-permute-start | bytes 30728 | tf_op jit(solution)/shard_map/ppermute | solution.py:22
  349.9 11.9 %collective-permute-start.7 = (f32[2,10,1,128]{3,2,1,0:T(1,128)S(1)}, f32[2,10,1,128]{3,2,1,0:T(1,128)S(1)}, u32[]{:S(2)}, u32[]{:S(2)}) collective-permute-start(f32[2,10,1,128]{3,2,1,0:T(1,128)S(1)} %get-tuple-element.1301), channel_id=1, source_target_pairs={{1,0},{2,1},{3,2},{4,3},{5,4},{6,5},{7,6},{9,8},{10,9},{11,10},{12... | collective-permute-start | bytes 30728 | tf_op jit(solution)/shard_map/ppermute | solution.py:25
Sparse Core Ops, SparseCore 0:
  175.5 39.4 all-reduce.33
where the time goes:
time: 426 us; the launch traced here: 424 us
  blocking collectives  155 us (36%)
  matrix products  140 us (33%)
  waiting for transfers between devices  33.6 us (8%)
  other arithmetic  28.7 us (7%)
  between operations  26 us (6%)
  starting transfers between devices  16 us (4%)
  local copies, waits for them, and re-layouts  15.6 us (4%)
  loops' own time  9.71 us (2%)
    dot_general x128, matrix products, forward_cell_turn(): jnp.dot(kernel_tile(field, block_x[field], block_y[field], cell_x, cell_y...  97.5 us
    dot_general x64, matrix products, cell_station_turn(): jnp.dot(block_source[field], kernel_tile(field, block_x[field], block_y[f...  40.2 us
    psum x1, blocking collectives, body(): lax.psum(jnp.stack(shares), ('gx', 'gy')) / (2 * total_stations)  40 us
    pmax x1, blocking collectives, body(): peak = lax.pmax(jnp.max(jnp.abs(gradient)), ('gx', 'gy')) + 1e-06  39.4 us
    unnamed x2, waiting for transfers between devices  33.6 us
    psum x2, blocking collectives, column_data(): return lax.psum(partial_value, 'gy')  27.7 us
    psum x3, blocking collectives, line_totals(): return lax.psum(local, 'gx')  27.3 us
    all_gather x2, blocking collectives, column_data(): lax.all_gather(fields, 'gx', axis=1, tiled=True)  20.1 us
  transfers between devices with their start and end apart: 9, of which 1 were waited for; matrix products, arithmetic and copies ran while one was open for 40% of the time, Pallas kernels for 0%

commit v1 on v0

v1 whole, which is shorter than its diff:
```python
import jax
import jax.numpy as jnp
from jax import lax
from jax.sharding import PartitionSpec as P

LINES = 256

cell_depth = 2.0
lift = 1.0
coupling_scale = 0.05
highest = lax.Precision.HIGHEST


def extended(block, low, high):
    for axis, dim in (("gx", 1), ("gy", 2)):
        count = lax.axis_size(axis)
        forward = [(i, i + 1) for i in range(count - 1)]
        backward = [(target, source) for source, target in forward]
        size = block.shape[dim]
        before = lax.ppermute(
            lax.slice_in_dim(block, size - low, None, axis=dim), axis, forward
        )
        after = lax.ppermute(lax.slice_in_dim(block, 0, high, axis=dim), axis, backward)
        block = jnp.concatenate([before, block, after], axis=dim)
    return block


def tables(first_x, first_y, rows, width, layers):
    shape = (rows, width, layers)
    gap_x = (first_x + lax.broadcasted_iota(jnp.int32, shape, 0)).astype(jnp.float32)
    gap_y = (first_y + lax.broadcasted_iota(jnp.int32, shape, 1)).astype(jnp.float32)
    depth = (
        lax.broadcasted_iota(jnp.int32, shape, 2).astype(jnp.float32) + 0.5
    ) * cell_depth + lift
    radius_sq = gap_x * gap_x + gap_y * gap_y + depth * depth
    inverse = lax.rsqrt(radius_sq)
    cube = inverse * inverse * inverse
    gravity = depth * cube
    magnetic = (3.0 * depth * depth - radius_sq) * cube * inverse * inverse
    return jnp.stack([gravity, magnetic])


def masks(rows, width, start_x, start_y, total_x, total_y):
    global_x = start_x + jnp.arange(rows, dtype=jnp.int32)
    global_y = start_y + jnp.arange(width, dtype=jnp.int32)
    mask_x = ((global_x >= 0) & (global_x < total_x - 1)).astype(jnp.float32)[:, None, None]
    mask_y = ((global_y >= 0) & (global_y < total_y - 1)).astype(jnp.float32)[None, :, None]
    valid = (global_x >= 0)[:, None] & (global_y >= 0)[None, :]
    valid = valid & (global_x < total_x)[:, None] & (global_y < total_y)[None, :]
    return (mask_x, mask_y, valid.astype(jnp.float32)[:, :, None])


def differences(field, mask_x, mask_y):
    base = field[:-1, :-1, :]
    along_x = (field[1:, :-1, :] - base) * mask_x
    along_y = (field[:-1, 1:, :] - base) * mask_y
    along_z = jnp.concatenate(
        [base[:, :, 1:] - base[:, :, :-1], jnp.zeros_like(base[:, :, :1])], axis=2
    )
    return (along_x, along_y, along_z)


def cross(a, b):
    return (
        a[1] * b[2] - a[2] * b[1],
        a[2] * b[0] - a[0] * b[2],
        a[0] * b[1] - a[1] * b[0],
    )


def inner(a, b):
    return a[0] * b[0] + a[1] * b[1] + a[2] * b[2]


def adjoint_differences(force, mask_x, mask_y):
    fx = force[0] * mask_x
    fy = force[1] * mask_y
    fz = force[2]
    keep = lax.broadcasted_iota(jnp.int32, fz.shape, 2) < fz.shape[2] - 1
    fz = jnp.where(keep, fz, 0.0)
    lower = jnp.concatenate([jnp.zeros_like(fz[:, :, :1]), fz[:, :, :-1]], axis=2)
    return (
        (fx[:-1, 1:] - fx[1:, 1:]) + (fy[1:, :-1] - fy[1:, 1:]) + (lower - fz)[1:, 1:]
    )


def from_all(values):
    count = lax.axis_size("gx") * lax.axis_size("gy")
    copies = jnp.broadcast_to(values[None], (count,) + values.shape)
    return lax.all_to_all(copies, ("gx", "gy"), 0, 0, tiled=True)


def everywhere(values):
    return jnp.sum(from_all(values), axis=0)


def all_groups(values):
    groups = lax.axis_size("gx")
    group = lax.axis_index("gx")
    pieces = jnp.stack(
        [values]
        + [
            lax.ppermute(values, "gx", [(i, (i + hop) % groups) for i in range(groups)])
            for hop in range(1, groups)
        ]
    )
    return jnp.concatenate(
        [
            lax.dynamic_index_in_dim(pieces, (group - turn) % groups, 0, keepdims=False)
            for turn in range(groups)
        ],
        axis=1,
    )


def body(density, susceptibility, station_cell, station_line, observed, data_weight, trial_steps):
    rows, width, layers = density.shape
    groups = lax.axis_size("gx")
    columns = lax.axis_size("gy")
    total_x = rows * groups
    total_y = width * columns
    stations = station_cell.shape[1] * groups
    group = lax.axis_index("gx")
    anchor_x = group * rows
    anchor_y = lax.axis_index("gy") * width
    coupling = coupling_scale * stations / (total_x * total_y * layers)
    models = jnp.stack([density, susceptibility])

    packed = jnp.concatenate(
        [
            station_cell.astype(jnp.float32),
            station_line.astype(jnp.float32),
            observed,
            data_weight,
        ]
    )
    packed = all_groups(packed)
    cells = packed[0:2].astype(jnp.int32)
    lines = packed[2:4].astype(jnp.int32)
    observed = packed[4:6]
    weight = packed[6:8]
    hot_x = (cells // total_y)[:, :, None] == jnp.arange(total_x, dtype=jnp.int32)
    hot_y = (cells % total_y)[:, :, None] == jnp.arange(total_y, dtype=jnp.int32)
    hot_x = hot_x.astype(jnp.float32)
    hot_y = hot_y.astype(jnp.float32)
    same = (lines[:, :, None] == lines[:, None, :]).astype(jnp.bfloat16)
    counts = jnp.sum(same.astype(jnp.float32), axis=2)

    def parts_of(values):
        first = lax.reduce_precision(values, 8, 7)
        rest = values - first
        second = lax.reduce_precision(rest, 8, 7)
        return jnp.stack([first, second, rest - second], axis=1).astype(jnp.bfloat16)

    def level(values):
        sums = jnp.einsum(
            "fct,fts->fcs", parts_of(values), same, preferred_element_type=jnp.float32
        )
        return values - jnp.sum(sums, axis=1) / jnp.maximum(counts, 1.0)

    def at_stations(surface):
        picked = jnp.einsum("fsy,fxy->fsx", hot_y, surface, precision=highest)
        return jnp.sum(picked * hot_x, axis=2)

    span_x = total_x + rows
    span_y = -(-(total_y + width) // 8) * 8
    table = tables(-rows - anchor_x, -width - anchor_y, span_x, span_y, layers)
    flat = table.reshape(2, span_x * span_y, layers)

    def forward(fields):
        by_offset = jnp.einsum(
            "fck,fpk->fcp", fields.reshape(2, rows * width, layers), flat, precision=highest
        ).reshape(2, rows, width, span_x, span_y)
        over_x = sum(
            lax.slice_in_dim(by_offset[:, i], rows - i, rows - i + total_x, axis=2)
            for i in range(rows)
        )
        return sum(
            lax.slice_in_dim(over_x[:, j], width - j, width - j + total_y, axis=2)
            for j in range(width)
        )

    def adjoint(surface):
        padded = jnp.pad(
            surface, ((0, 0), (rows, rows), (width, span_y - total_y))
        )
        shifted = jnp.stack(
            [
                padded[:, i : i + span_x, j : j + span_y]
                for i in range(rows + 1)
                for j in range(width + 1)
            ],
            axis=1,
        )
        return jnp.einsum(
            "fcp,fpk->fck",
            shifted.reshape(2, (rows + 1) * (width + 1), span_x * span_y),
            flat,
            precision=highest,
        ).reshape(2, rows + 1, width + 1, layers)

    wide = extended(models, 1, 2)
    mask_x, mask_y, valid = masks(
        rows + 2, width + 2, anchor_x - 1, anchor_y - 1, total_x, total_y
    )
    a = differences(wide[0], mask_x, mask_y)
    b = differences(wide[1], mask_x, mask_y)
    t = tuple(part * valid for part in cross(a, b))
    pull_a = cross(b, t)
    pull_b = cross(t, a)
    force = jnp.stack(
        [
            adjoint_differences(pull_a, mask_x, mask_y),
            adjoint_differences(pull_b, mask_x, mask_y),
        ]
    )
    cross_force = force[:, :rows, :width]

    surface_shape = (2, total_x, total_y)
    predicted = everywhere(forward(models).reshape(-1, 128)).reshape(surface_shape)
    predicted = at_stations(predicted)
    residual = level(predicted - observed)
    weighted = weight * residual
    source = level(weight * weighted)
    surface = jnp.einsum("fsx,fsy->fxy", hot_x * source[:, :, None], hot_y, precision=highest)
    data_wide = adjoint(surface)
    data_gradient = data_wide[:, :rows, :width]
    gradient_wide = data_wide + coupling * force
    gradient = gradient_wide[:, :rows, :width]

    image_part = forward(gradient)
    own_a = tuple(part[1:-1, 1:-1] for part in a)
    own_b = tuple(part[1:-1, 1:-1] for part in b)
    own_t = tuple(part[1:-1, 1:-1] for part in t)
    own_mask = (mask_x[1:-1], mask_y[:, 1:-1])
    da = differences(gradient_wide[0], *own_mask)
    db = differences(gradient_wide[1], *own_mask)
    t1 = tuple(-(p + q) for p, q in zip(cross(da, own_b), cross(own_a, db)))
    t2 = cross(da, db)
    powers = jnp.stack(
        [
            jnp.sum(inner(own_t, own_t)),
            2.0 * jnp.sum(inner(own_t, t1)),
            jnp.sum(inner(t1, t1) + 2.0 * inner(own_t, t2)),
            2.0 * jnp.sum(inner(t1, t2)),
            jnp.sum(inner(t2, t2)),
        ]
    )
    surface_size = 2 * total_x * total_y
    tail = jnp.concatenate([powers, jnp.max(jnp.abs(gradient))[None]])
    sent = jnp.concatenate([image_part.reshape(surface_size), tail])
    sent = jnp.pad(sent, (0, -sent.shape[0] % 1024)).reshape(-1, 128)
    got = from_all(sent)
    total = jnp.sum(got, axis=0).reshape(-1)
    peak_row, peak_lane = divmod(surface_size + 5, 128)
    peak = jnp.max(got[:, peak_row, peak_lane]) + 1e-06
    image = at_stations(total[:surface_size].reshape(surface_shape)) / peak
    change = level(image)
    moved = weight * (residual - trial_steps[:, None, None] * change)
    data_value = 0.5 * jnp.sum(moved * moved, axis=(1, 2))
    sums = total[surface_size : surface_size + 5]
    ratio = trial_steps / peak
    energy = sums[4]
    for order in (3, 2, 1, 0):
        energy = energy * ratio + sums[order]
    trial_values = (data_value + coupling * 0.5 * energy) / (2 * stations)
    weighted_residual = lax.dynamic_slice_in_dim(
        weighted, group * station_cell.shape[1], station_cell.shape[1], 1
    )
    return (data_gradient, cross_force, weighted_residual, trial_values)


def solution(mesh):
    placed = (
        P("gx", "gy", None),
        P("gx", "gy", None),
        P(None, "gx"),
        P(None, "gx"),
        P(None, "gx"),
        P(None, "gx"),
        P(),
    )
    return jax.shard_map(
        body,
        mesh=mesh,
        in_specs=placed,
        out_specs=(P(None, "gx", "gy", None), P(None, "gx", "gy", None), P(None, "gx"), P()),
        check_vma=False,
    )
```

time: 426 us -> 110 us (0.26)
  blocking collectives: 155 us -> 0 us
  matrix products: 140 us -> 10.2 us
  local copies, waits for them, and re-layouts: 15.6 us -> 40.7 us
  between operations: 26 us -> 3.57 us
  waiting for transfers between devices: 33.6 us -> 11.4 us
  other arithmetic: 28.7 us -> 12.4 us
  starting transfers between devices: 16 us -> 30.5 us
  loops' own time: 9.71 us -> 0 us
    dot_general x198 -> x9, matrix products: 140 us -> 10.2 us  [the longest x3 5 us: level(): jnp.einsum('fct,fts->fcs', parts_of(values), same, preferred_element_type...]
    psum x6 -> x0, blocking collectives: 95 us -> none  [the longest x1 40 us: body(): lax.psum(jnp.stack(shares), ('gx', 'gy')) / (2 * total_stations)]
    pmax x1 -> x0, blocking collectives: 39.4 us -> none  [body(): peak = lax.pmax(jnp.max(jnp.abs(gradient)), ('gx', 'gy')) + 1e-06]
    unnamed x2 -> x0, waiting for transfers between devices: 33.6 us -> none
    another operation x3 -> x53, local copies, waits for them, and re-layouts: 0.09 us -> 29 us  [the longest x46 29 us: adjoint(): jnp.stack([padded[:, i:i + span_x, j:j + span_y] for i in range(rows + 1)...]
    all_gather x2 -> x0, blocking collectives: 20.1 us -> none  [column_data(): lax.all_gather(fields, 'gx', axis=1, tiled=True)]
    all_to_all x0 -> x2, starting transfers between devices: none -> 15.1 us  [from_all(): return lax.all_to_all(copies, ('gx', 'gy'), 0, 0, tiled=True)]
    all_to_all x0 -> x2, waiting for transfers between devices: none -> 10.9 us  [from_all(): return lax.all_to_all(copies, ('gx', 'gy'), 0, 0, tiled=True)]
  transfers between devices with their start and end apart: 9 -> 9, of which waited for: 1 -> 2; matrix products, arithmetic and copies ran while one was open for 40% -> 8% of each run, Pallas kernels for 0% -> 0%
where the time goes in v1:
time: 110 us; the launch traced here: 109 us
  local copies, waits for them, and re-layouts  40.7 us (37%)
  starting transfers between devices  30.5 us (28%)
  other arithmetic  12.4 us (11%)
  waiting for transfers between devices  11.4 us (10%)
  matrix products  10.2 us (9%)
  between operations  3.57 us (3%)
    another operation x46, local copies, waits for them, and re-layouts, adjoint(): jnp.stack([padded[:, i:i + span_x, j:j + span_y] for i in range(rows + 1)...  29 us
    all_to_all x2, starting transfers between devices, from_all(): return lax.all_to_all(copies, ('gx', 'gy'), 0, 0, tiled=True)  15.1 us
    all_to_all x2, waiting for transfers between devices, from_all(): return lax.all_to_all(copies, ('gx', 'gy'), 0, 0, tiled=True)  10.9 us
    ppermute x2, starting transfers between devices, extended(): lax.ppermute(lax.slice_in_dim(block, size - low, None, axis=dim), axis, f...  7.76 us
    ppermute x3, starting transfers between devices, all_groups(): lax.ppermute(values, 'gx', [(i, (i + hop) % groups) for i in range(groups)])  5.07 us
    dot_general x3, matrix products, level(): jnp.einsum('fct,fts->fcs', parts_of(values), same, preferred_element_type...  5 us
    div x1, other arithmetic, body(): trial_values = (data_value + coupling * 0.5 * energy) / (2 * stations)  3.65 us
    dot_general x2, matrix products, forward(): jnp.einsum('fck,fpk->fcp', fields.reshape(2, rows * width, layers), flat,...  3.27 us
  transfers between devices with their start and end apart: 9, of which 2 were waited for; matrix products, arithmetic and copies ran while one was open for 8% of the time, Pallas kernels for 0%

profile of v1, /device:TPU:0, one launch (start us, length us, event | category | flops | bytes accessed | tf_op | source)
XLA Modules:
  0.0 108.9 jit_solution(9759950095160432573)
XLA Ops:
  2.7 4.0 %collective-permute-start.2 = (f32[8,256]{1,0:T(8,128)S(1)}, f32[8,256]{1,0:T(8,128)S(1)}, u32[]{:S(2)}, u32[]{:S(2)}) collective-permute-start(f32[8,256]{1,0:T(8,128)S(1)} %get-tuple-element.176), channel_id=1, source_target_pairs={{0,24},{8,0},{16,8},{24,16},{1,25},{9,1},{17,9},{25,17},{2,26},{10... | collective-permute-start | bytes 24584 | tf_op jit(solution)/shard_map/ppermute | solution.py:103
  8.4 1.6 %fusion.25 = f32[2,32,1600]{2,1,0:T(8,128)S(1)} fusion(f32[1,1600,128]{2,1,0:T(8,128)S(1)} %get-tuple-element.167, f32[1,1600,128]{2,1,0:T(8,128)S(1)} %get-tuple-element.166, f32[1,32,128]{2,1,0:T(8,128)S(1)} %bitcast.160, f32[1,32,128]{2,1,0:T(8,128)S(1)} %bitcast.161), kind=kOutput, calls=%fused_computation.28 | convolution fusion | flops 157704192 | bytes 2080768 | tf_op jit(solution)/shard_map/fck,fpk->fcp/dot_general | solution.py:171
  11.7 5.8 %all-to-all-start = ((f32[32,16,128]{2,1,0:T(8,128)}), f32[32,16,128]{2,1,0:T(8,128)S(1)}, u32[]{:S(2)}, u32[]{:S(2)}) async-start(f32[32,16,128]{2,1,0:T(8,128)} %broadcast_in_dim.16), calls=%async_computation | async-start | bytes 524288 | tf_op jit(solution)/shard_map/all_to_all | solution.py:90
  17.5 1.3 %collective-permute-start.4 = (f32[2,2,4,128]{3,1,2,0:T(2,128)S(1)}, f32[2,2,4,128]{3,1,2,0:T(2,128)S(1)}, u32[]{:S(2)}, u32[]{:S(2)}) collective-permute-start(f32[2,2,4,128]{3,1,2,0:T(2,128)S(1)} %pad_maximum_fusion.12), channel_id=1, source_target_pairs={{8,0},{16,8},{24,16},{9,1},{17,9},{25,17},{10,2},{18,10},{26,18},{... | collective-permute-start | bytes 24584 | tf_op jit(solution)/shard_map/ppermute | solution.py:23
  18.8 4.5 %collective-permute-start.3 = (f32[2,1,4,128]{3,1,2,0:T(1,128)S(1)}, f32[2,1,4,128]{3,1,2,0:T(1,128)S(1)}, u32[]{:S(2)}, u32[]{:S(2)}) collective-permute-start(f32[2,1,4,128]{3,1,2,0:T(1,128)S(1)} %pad_maximum_fusion.14), channel_id=1, source_target_pairs={{0,8},{8,16},{16,24},{1,9},{9,17},{17,25},{2,10},{10,18},{18,26},{... | collective-permute-start | bytes 12296 | tf_op jit(solution)/shard_map/ppermute | solution.py:20
  24.7 1.3 %collective-permute-start.6 = (f32[2,11,2,128]{3,1,2,0:T(8,128)S(1)}, f32[2,11,2,128]{3,1,2,0:T(8,128)S(1)}, u32[]{:S(2)}, u32[]{:S(2)}) collective-permute-start(f32[2,11,2,128]{3,1,2,0:T(8,128)S(1)} %pad_maximum_fusion.6), channel_id=1, source_target_pairs={{1,0},{2,1},{3,2},{4,3},{5,4},{6,5},{7,6},{9,8},{10,9},{11,10},{12... | collective-permute-start | bytes 67592 | tf_op jit(solution)/shard_map/ppermute | solution.py:23
  26.0 3.2 %collective-permute-start.5 = (f32[2,11,1,128]{3,1,2,0:T(8,128)S(1)}, f32[2,11,1,128]{3,1,2,0:T(8,128)S(1)}, u32[]{:S(2)}, u32[]{:S(2)}) collective-permute-start(f32[2,11,1,128]{3,1,2,0:T(8,128)S(1)} %pad_maximum_fusion.11), channel_id=1, source_target_pairs={{0,1},{1,2},{2,3},{3,4},{4,5},{5,6},{6,7},{8,9},{9,10},{10,11},{11... | collective-permute-start | bytes 33800 | tf_op jit(solution)/shard_map/ppermute | solution.py:20
  31.1 1.1 %convert_reduce_fusion = f32[2,1024]{1,0:T(2,128)S(1)} fusion(s32[2,1024]{1,0:T(2,128)S(1)} %get-tuple-element.154), kind=kLoop, calls=%fused_computation.7 | loop fusion | flops 8386560 | bytes 16384 | tf_op jit(solution)/shard_map/reduce_sum | solution.py:147
  32.2 1.7 %fusion.14 = f32[2,1024]{1,0:T(2,128)S(1)} fusion(s32[2,1024]{1,0:T(2,128)S(1)} %get-tuple-element.154, bf16[2,1,1024]{2,1,0:T(2,128)(2,1)S(1)} %copy.774, bf16[2,1,1024]{2,1,0:T(2,128)(2,1)S(1)} %copy.773, bf16[2,1,1024]{2,1,0:T(2,128)(2,1)S(1)} %copy.772), kind=kOutput, calls=%fused_computation.23 | convolution fusion | flops 14721024 | bytes 28672 | tf_op jit(solution)/shard_map/fct,fts->fcs/dot_general | solution.py:156
  34.5 1.7 %fusion.17 = f32[2,1024]{1,0:T(2,128)S(1)} fusion(s32[2,1024]{1,0:T(2,128)S(1)} %get-tuple-element.154, bf16[2,1,1024]{2,1,0:T(2,128)(2,1)S(1)} %copy.777, bf16[2,1,1024]{2,1,0:T(2,128)(2,1)S(1)} %copy.776, bf16[2,1,1024]{2,1,0:T(2,128)(2,1)S(1)} %copy.775), kind=kOutput, calls=%fused_computation.24 | convolution fusion | flops 14721024 | bytes 28672 | tf_op jit(solution)/shard_map/fct,fts->fcs/dot_general | solution.py:156
  37.4 0.9 pad_slice_fusion
  38.5 0.9 stack.311
  40.2 1.5 %stack.313 = f32[2,1,1600]{2,1,0:T(1,128)} reshape(f32[2,40,40]{2,1,0:T(8,128)} %get-tuple-element.111) | data formatting | bytes 25600 | tf_op jit(solution)/shard_map/stack | solution.py:187
  41.7 1.5 %stack.314 = f32[2,1,1600]{2,1,0:T(1,128)} reshape(f32[2,40,40]{2,1,0:T(8,128)} %get-tuple-element.112) | data formatting | bytes 25600 | tf_op jit(solution)/shard_map/stack | solution.py:187
  43.2 1.5 %stack.315 = f32[2,1,1600]{2,1,0:T(1,128)} reshape(f32[2,40,40]{2,1,0:T(8,128)} %get-tuple-element.113) | data formatting | bytes 25600 | tf_op jit(solution)/shard_map/stack | solution.py:187
  44.7 1.5 %stack.316 = f32[2,1,1600]{2,1,0:T(1,128)} reshape(f32[2,40,40]{2,1,0:T(8,128)} %get-tuple-element.114) | data formatting | bytes 25600 | tf_op jit(solution)/shard_map/stack | solution.py:187
  46.1 1.5 %stack.317 = f32[2,1,1600]{2,1,0:T(1,128)} reshape(f32[2,40,40]{2,1,0:T(8,128)} %get-tuple-element.115) | data formatting | bytes 25600 | tf_op jit(solution)/shard_map/stack | solution.py:187
  55.5 1.5 %stack.348 = f32[2,1,1600]{2,1,0:T(1,128)} reshape(f32[2,40,40]{2,1,0:T(8,128)} %get-tuple-element.148) | data formatting | bytes 25600 | tf_op jit(solution)/shard_map/stack | solution.py:187
  57.0 1.5 %stack.349 = f32[2,1,1600]{2,1,0:T(1,128)} reshape(f32[2,40,40]{2,1,0:T(8,128)} %get-tuple-element.149) | data formatting | bytes 25600 | tf_op jit(solution)/shard_map/stack | solution.py:187
  58.5 1.5 %stack.350 = f32[2,1,1600]{2,1,0:T(1,128)} reshape(f32[2,40,40]{2,1,0:T(8,128)} %get-tuple-element.150) | data formatting | bytes 25600 | tf_op jit(solution)/shard_map/stack | solution.py:187
  59.9 1.5 %stack.351 = f32[2,1,1600]{2,1,0:T(1,128)} reshape(f32[2,40,40]{2,1,0:T(8,128)} %get-tuple-element.151) | data formatting | bytes 25600 | tf_op jit(solution)/shard_map/stack | solution.py:187
  61.4 1.5 %stack.352 = f32[2,1,1600]{2,1,0:T(1,128)} reshape(f32[2,40,40]{2,1,0:T(8,128)} %get-tuple-element.152) | data formatting | bytes 25600 | tf_op jit(solution)/shard_map/stack | solution.py:187
  62.9 1.5 %stack.353 = f32[2,1,1600]{2,1,0:T(1,128)} reshape(f32[2,40,40]{2,1,0:T(8,128)} %get-tuple-element.147) | data formatting | bytes 25600 | tf_op jit(solution)/shard_map/stack | solution.py:187
  65.3 2.5 %stack.298 = f32[2,45,1600]{2,1,0:T(8,128)S(1)} concatenate(f32[2,1,1600]{2,1,0:T(1,128)S(1)} %stack.311, f32[2,1,1600]{2,1,0:T(1,128)S(1)} %stack.312, f32[2,1,1600]{2,1,0:T(1,128)S(1)} %copy-done.2, f32[2,1,1600]{2,1,0:T(1,128)S(1)} %copy-done.3, f32[2,1,1600]{2,1,0:T(1,128)S(1)} %copy-done.4, f32[2,1,1600]{2,1,0:T(1,128)S(1)} %copy-done.5, f32[2,1,1600]{2,1,0:T(1,128)S(1)} %copy-done.6, ...), dimensions={1} | concatenate | bytes 1152000 | tf_op jit(solution)/shard_map/stack | solution.py:187
  67.7 1.1 fusion.24
  69.5 1.6 %fusion.23 = f32[2,32,1600]{2,1,0:T(8,128)S(1)} fusion(f32[2,32,128]{2,1,0:T(8,128)S(1)} %bitcast.159, f32[1,1600,128]{2,1,0:T(8,128)S(1)} %get-tuple-element.167, f32[1,1600,128]{2,1,0:T(8,128)S(1)} %get-tuple-element.166), kind=kOutput, calls=%fused_computation.26 | convolution fusion | flops 157696000 | bytes 2080768 | tf_op jit(solution)/shard_map/fck,fpk->fcp/dot_general | solution.py:171
  74.7 2.6 %concatenate.46 = f32[2054]{0:T(1024)S(1)} concatenate(f32[2048]{0:T(1024)S(1)} %reshape.409, f32[1]{0:T(128)} %bitcast.48, f32[1]{0:T(128)} %bitcast.52, f32[1]{0:T(128)} %bitcast.53, f32[1]{0:T(128)} %bitcast.54, f32[1]{0:T(128)} %bitcast.55, f32[1]{0:T(128)} %bitcast.56), dimensions={0} | concatenate | bytes 16432 | tf_op jit(solution)/shard_map/concatenate | solution.py:251
  78.1 9.3 %all-to-all-start.1 = ((f32[32,24,128]{2,1,0:T(8,128)}), f32[32,24,128]{2,1,0:T(8,128)S(1)}, u32[]{:S(2)}, u32[]{:S(2)}) async-start(f32[32,24,128]{2,1,0:T(8,128)} %broadcast_in_dim.20), calls=%async_computation.1 | async-start | bytes 786432 | tf_op jit(solution)/shard_map/all_to_all | solution.py:90
  88.7 1.3 %constant_dynamic-slice_fusion = f32[2,256]{1,0:T(2,128)} fusion(f32[2,1024]{1,0:T(2,128)} %get-tuple-element.66, s32[]{:T(128)S(6)} %select_n.65), kind=kLoop, calls=%fused_computation.273 | loop fusion | bytes 4100 | tf_op jit(solution)/shard_map/dynamic_slice | solution.py:267
  89.9 10.9 %all-to-all-done.1 = f32[32,24,128]{2,1,0:T(8,128)S(1)} async-done(((f32[32,24,128]{2,1,0:T(8,128)}), f32[32,24,128]{2,1,0:T(8,128)S(1)}, u32[]{:S(2)}, u32[]{:S(2)}) %all-to-all-start.1) | async-done | bytes 393248 | tf_op jit(solution)/shard_map/all_to_all | solution.py:90
  102.7 1.7 %fusion.20 = f32[2,1024]{1,0:T(2,128)S(1)} fusion(s32[2,1024]{1,0:T(2,128)S(1)} %copy-done.20, bf16[2,1,1024]{2,1,0:T(2,128)(2,1)S(1)} %get-tuple-element.169, bf16[2,1,1024]{2,1,0:T(2,128)(2,1)S(1)} %get-tuple-element.170, bf16[2,1,1024]{2,1,0:T(2,128)(2,1)S(1)} %get-tuple-element.168), kind=kOutput, calls=%fused_computation.25 | convolution fusion | flops 14721024 | bytes 28672 | tf_op jit(solution)/shard_map/fct,fts->fcs/dot_general | solution.py:156
  105.3 3.7 %add_multiply_fusion = f32[8]{0:T(128)} fusion(f32[8]{0:T(128)S(1)} %copy-done.21, f32[8]{0:T(128)S(1)} %multiply_reduce_fusion, f32[]{:T(128)} %bitcast.63, f32[]{:T(128)} %bitcast.62, f32[]{:T(128)} %bitcast.61, f32[]{:T(128)} %bitcast.60, f32[]{:T(128)S(6)} %add.394, f32[]{:T(128)} %bitcast.59), kind=kLoop, calls=%fused_computation.276 | loop fusion | flops 104 | bytes 120 | tf_op jit(solution)/shard_map/div | solution.py:266
  (184 shorter events, 26.6 us)
Async XLA Ops:
  0.6 7.7 %copy-start = (f32[8,4,128]{2,1,0:T(4,128)S(1)}, f32[8,4,128]{2,1,0:T(4,128)}, u32[]{:S(2)}) copy-start(f32[8,4,128]{2,1,0:T(4,128)} %param.8) | copy-start | bytes 49156
  0.6 7.7 %copy-start.1 = (f32[8,4,128]{2,1,0:T(4,128)S(1)}, f32[8,4,128]{2,1,0:T(4,128)}, u32[]{:S(2)}) copy-start(f32[8,4,128]{2,1,0:T(4,128)} %param.7) | copy-start | bytes 49156
  2.7 26.5 %collective-permute-start.2 = (f32[8,256]{1,0:T(8,128)S(1)}, f32[8,256]{1,0:T(8,128)S(1)}, u32[]{:S(2)}, u32[]{:S(2)}) collective-permute-start(f32[8,256]{1,0:T(8,128)S(1)} %get-tuple-element.176), channel_id=1, source_target_pairs={{0,24},{8,0},{16,8},{24,16},{1,25},{9,1},{17,9},{25,17},{2,26},{10... | collective-permute-start | bytes 24584 | tf_op jit(solution)/shard_map/ppermute | solution.py:103
  6.7 22.5 %collective-permute-start.1 = (f32[8,256]{1,0:T(8,128)S(1)}, f32[8,256]{1,0:T(8,128)S(1)}, u32[]{:S(2)}, u32[]{:S(2)}) collective-permute-start(f32[8,256]{1,0:T(8,128)S(1)} %get-tuple-element.176), channel_id=1, source_target_pairs={{0,16},{8,24},{16,0},{24,8},{1,17},{9,25},{17,1},{25,9},{2,18},{10... | collective-permute-start | bytes 24584 | tf_op jit(solution)/shard_map/ppermute | solution.py:103
  7.2 22.1 %collective-permute-start = (f32[8,256]{1,0:T(8,128)S(1)}, f32[8,256]{1,0:T(8,128)S(1)}, u32[]{:S(2)}, u32[]{:S(2)}) collective-permute-start(f32[8,256]{1,0:T(8,128)S(1)} %get-tuple-element.176), channel_id=1, source_target_pairs={{0,8},{8,16},{16,24},{24,0},{1,9},{9,17},{17,25},{25,1},{2,10},{10... | collective-permute-start | bytes 24584 | tf_op jit(solution)/shard_map/ppermute | solution.py:103
  11.7 18.9 %all-to-all-start = ((f32[32,16,128]{2,1,0:T(8,128)}), f32[32,16,128]{2,1,0:T(8,128)S(1)}, u32[]{:S(2)}, u32[]{:S(2)}) async-start(f32[32,16,128]{2,1,0:T(8,128)} %broadcast_in_dim.16), calls=%async_computation | async-start | bytes 524288 | tf_op jit(solution)/shard_map/all_to_all | solution.py:90
  17.5 7.2 %collective-permute-start.4 = (f32[2,2,4,128]{3,1,2,0:T(2,128)S(1)}, f32[2,2,4,128]{3,1,2,0:T(2,128)S(1)}, u32[]{:S(2)}, u32[]{:S(2)}) collective-permute-start(f32[2,2,4,128]{3,1,2,0:T(2,128)S(1)} %pad_maximum_fusion.12), channel_id=1, source_target_pairs={{8,0},{16,8},{24,16},{9,1},{17,9},{25,17},{10,2},{18,10},{26,18},{... | collective-permute-start | bytes 24584 | tf_op jit(solution)/shard_map/ppermute | solution.py:23
  18.8 5.9 %collective-permute-start.3 = (f32[2,1,4,128]{3,1,2,0:T(1,128)S(1)}, f32[2,1,4,128]{3,1,2,0:T(1,128)S(1)}, u32[]{:S(2)}, u32[]{:S(2)}) collective-permute-start(f32[2,1,4,128]{3,1,2,0:T(1,128)S(1)} %pad_maximum_fusion.14), channel_id=1, source_target_pairs={{0,8},{8,16},{16,24},{1,9},{9,17},{17,25},{2,10},{10,18},{18,26},{... | collective-permute-start | bytes 12296 | tf_op jit(solution)/shard_map/ppermute | solution.py:20
  24.7 5.2 %collective-permute-start.6 = (f32[2,11,2,128]{3,1,2,0:T(8,128)S(1)}, f32[2,11,2,128]{3,1,2,0:T(8,128)S(1)}, u32[]{:S(2)}, u32[]{:S(2)}) collective-permute-start(f32[2,11,2,128]{3,1,2,0:T(8,128)S(1)} %pad_maximum_fusion.6), channel_id=1, source_target_pairs={{1,0},{2,1},{3,2},{4,3},{5,4},{6,5},{7,6},{9,8},{10,9},{11,10},{12... | collective-permute-start | bytes 67592 | tf_op jit(solution)/shard_map/ppermute | solution.py:23
  26.0 3.9 %collective-permute-start.5 = (f32[2,11,1,128]{3,1,2,0:T(8,128)S(1)}, f32[2,11,1,128]{3,1,2,0:T(8,128)S(1)}, u32[]{:S(2)}, u32[]{:S(2)}) collective-permute-start(f32[2,11,1,128]{3,1,2,0:T(8,128)S(1)} %pad_maximum_fusion.11), channel_id=1, source_target_pairs={{0,1},{1,2},{2,3},{3,4},{4,5},{5,6},{6,7},{8,9},{9,10},{10,11},{11... | collective-permute-start | bytes 33800 | tf_op jit(solution)/shard_map/ppermute | solution.py:20
  29.4 6.9 %copy-start.15 = (s32[2,1024]{1,0:T(2,128)}, s32[2,1024]{1,0:T(2,128)S(1)}, u32[]{:S(2)}) copy-start(s32[2,1024]{1,0:T(2,128)S(1)} %get-tuple-element.155) | copy-start | bytes 24580
  29.4 6.9 %copy-start.17 = (s32[2,1024]{1,0:T(2,128)}, s32[2,1024]{1,0:T(2,128)S(1)}, u32[]{:S(2)}) copy-start(s32[2,1024]{1,0:T(2,128)S(1)} %get-tuple-element.156) | copy-start | bytes 24580
  31.0 5.2 %copy-start.19 = (s32[2,1024]{1,0:T(2,128)}, s32[2,1024]{1,0:T(2,128)S(1)}, u32[]{:S(2)}) copy-start(s32[2,1024]{1,0:T(2,128)S(1)} %get-tuple-element.154) | copy-start | bytes 24580
  48.3 16.8 %copy-start.2 = (f32[2,1,1600]{2,1,0:T(1,128)S(1)}, f32[2,1,1600]{2,1,0:T(1,128)}, u32[]{:S(2)}) copy-start(f32[2,1,1600]{2,1,0:T(1,128)} %stack.313) | copy-start | bytes 38404
  48.3 16.9 %copy-start.3 = (f32[2,1,1600]{2,1,0:T(1,128)S(1)}, f32[2,1,1600]{2,1,0:T(1,128)}, u32[]{:S(2)}) copy-start(f32[2,1,1600]{2,1,0:T(1,128)} %stack.314) | copy-start | bytes 38404
  49.0 16.2 %copy-start.4 = (f32[2,1,1600]{2,1,0:T(1,128)S(1)}, f32[2,1,1600]{2,1,0:T(1,128)}, u32[]{:S(2)}) copy-start(f32[2,1,1600]{2,1,0:T(1,128)} %stack.315) | copy-start | bytes 38404
  49.0 16.2 %copy-start.5 = (f32[2,1,1600]{2,1,0:T(1,128)S(1)}, f32[2,1,1600]{2,1,0:T(1,128)}, u32[]{:S(2)}) copy-start(f32[2,1,1600]{2,1,0:T(1,128)} %stack.316) | copy-start | bytes 38404
  49.7 15.5 %copy-start.6 = (f32[2,1,1600]{2,1,0:T(1,128)S(1)}, f32[2,1,1600]{2,1,0:T(1,128)}, u32[]{:S(2)}) copy-start(f32[2,1,1600]{2,1,0:T(1,128)} %stack.317) | copy-start | bytes 38404
  49.7 15.5 %copy-start.7 = (f32[2,1,1600]{2,1,0:T(1,128)S(1)}, f32[2,1,1600]{2,1,0:T(1,128)}, u32[]{:S(2)}) copy-start(f32[2,1,1600]{2,1,0:T(1,128)} %stack.318) | copy-start | bytes 38404
  50.4 14.8 %copy-start.8 = (f32[2,1,1600]{2,1,0:T(1,128)S(1)}, f32[2,1,1600]{2,1,0:T(1,128)}, u32[]{:S(2)}) copy-start(f32[2,1,1600]{2,1,0:T(1,128)} %stack.319) | copy-start | bytes 38404
  50.4 14.8 %copy-start.9 = (f32[2,1,1600]{2,1,0:T(1,128)S(1)}, f32[2,1,1600]{2,1,0:T(1,128)}, u32[]{:S(2)}) copy-start(f32[2,1,1600]{2,1,0:T(1,128)} %stack.320) | copy-start | bytes 38404
  51.1 14.1 %copy-start.10 = (f32[2,1,1600]{2,1,0:T(1,128)S(1)}, f32[2,1,1600]{2,1,0:T(1,128)}, u32[]{:S(2)}) copy-start(f32[2,1,1600]{2,1,0:T(1,128)} %stack.321) | copy-start | bytes 38404
  51.1 14.1 %copy-start.11 = (f32[2,1,1600]{2,1,0:T(1,128)S(1)}, f32[2,1,1600]{2,1,0:T(1,128)}, u32[]{:S(2)}) copy-start(f32[2,1,1600]{2,1,0:T(1,128)} %stack.322) | copy-start | bytes 38404
  51.8 13.4 %copy-start.12 = (f32[2,1,1600]{2,1,0:T(1,128)S(1)}, f32[2,1,1600]{2,1,0:T(1,128)}, u32[]{:S(2)}) copy-start(f32[2,1,1600]{2,1,0:T(1,128)} %stack.323) | copy-start | bytes 38404
  71.8 0.7 copy-start.22
  72.5 28.4 %copy-start.16 = (s32[2,1024]{1,0:T(2,128)S(1)}, s32[2,1024]{1,0:T(2,128)}, u32[]{:S(2)}) copy-start(s32[2,1024]{1,0:T(2,128)} %copy-done.15) | copy-start | bytes 24580
  72.5 28.4 %copy-start.18 = (s32[2,1024]{1,0:T(2,128)S(1)}, s32[2,1024]{1,0:T(2,128)}, u32[]{:S(2)}) copy-start(s32[2,1024]{1,0:T(2,128)} %copy-done.17) | copy-start | bytes 24580
  72.6 30.0 %copy-start.20 = (s32[2,1024]{1,0:T(2,128)S(1)}, s32[2,1024]{1,0:T(2,128)}, u32[]{:S(2)}) copy-start(s32[2,1024]{1,0:T(2,128)} %copy-done.19) | copy-start | bytes 24580
  78.1 22.8 %all-to-all-start.1 = ((f32[32,24,128]{2,1,0:T(8,128)}), f32[32,24,128]{2,1,0:T(8,128)S(1)}, u32[]{:S(2)}, u32[]{:S(2)}) async-start(f32[32,24,128]{2,1,0:T(8,128)} %broadcast_in_dim.20), calls=%async_computation.1 | async-start | bytes 786432 | tf_op jit(solution)/shard_map/all_to_all | solution.py:90
  101.0 4.1 %copy-start.13 = (f32[2,1024]{1,0:T(2,128)S(1)}, f32[2,1024]{1,0:T(2,128)}, u32[]{:S(2)}) copy-start(f32[2,1024]{1,0:T(2,128)} %get-tuple-element.67) | copy-start | bytes 24580
  101.0 4.1 %copy-start.14 = (f32[2,1024]{1,0:T(2,128)S(1)}, f32[2,1024]{1,0:T(2,128)}, u32[]{:S(2)}) copy-start(f32[2,1024]{1,0:T(2,128)} %get-tuple-element.106) | copy-start | bytes 24580
  101.0 4.1 %copy-start.21 = (f32[8]{0:T(128)S(1)}, f32[8]{0:T(128)}, u32[]{:S(2)}) copy-start(f32[8]{0:T(128)} %param.13) | copy-start | bytes 100
  (1 other events, 0.7 us)

commit v2 on v1

--- a/solution.py
+++ b/solution.py
@@ -1,6 +1,10 @@
+import functools
+
 import jax
 import jax.numpy as jnp
 from jax import lax
+from jax.experimental import pallas as pl
+from jax.experimental.pallas import tpu as pltpu
 from jax.sharding import PartitionSpec as P
 
 LINES = 256
@@ -25,19 +29,100 @@
     return block
 
 
-def tables(first_x, first_y, rows, width, layers):
-    shape = (rows, width, layers)
-    gap_x = (first_x + lax.broadcasted_iota(jnp.int32, shape, 0)).astype(jnp.float32)
-    gap_y = (first_y + lax.broadcasted_iota(jnp.int32, shape, 1)).astype(jnp.float32)
+def block_tables(first_x, first_y, span_y, start, count, layers):
+    position = start + lax.broadcasted_iota(jnp.int32, (count, layers), 0)
+    gap_x = first_x + (position // span_y).astype(jnp.float32)
+    gap_y = first_y + (position % span_y).astype(jnp.float32)
     depth = (
-        lax.broadcasted_iota(jnp.int32, shape, 2).astype(jnp.float32) + 0.5
+        lax.broadcasted_iota(jnp.int32, (count, layers), 1).astype(jnp.float32) + 0.5
     ) * cell_depth + lift
     radius_sq = gap_x * gap_x + gap_y * gap_y + depth * depth
     inverse = lax.rsqrt(radius_sq)
     cube = inverse * inverse * inverse
     gravity = depth * cube
     magnetic = (3.0 * depth * depth - radius_sq) * cube * inverse * inverse
-    return jnp.stack([gravity, magnetic])
+    return (gravity, magnetic)
+
+
+def spread_rows(by_offset, out_ref, field, rows, width, span_y):
+    length = by_offset.shape[1]
+    over_y = None
+    for j in range(width):
+        piece = by_offset[j * rows : (j + 1) * rows]
+        piece = pltpu.roll(piece, (length - (width - j)) % length, 1)
+        over_y = piece if over_y is None else over_y + piece
+    total = None
+    for i in range(rows):
+        piece = pltpu.roll(over_y[i : i + 1], (length - (rows - i) * span_y) % length, 1)
+        total = piece if total is None else total + piece
+    chunks = out_ref.shape[0] // 2
+    for chunk in range(chunks):
+        row = field * chunks + chunk
+        out_ref[row : row + 1, :] = total[:, chunk * 128 : (chunk + 1) * 128]
+
+
+def project(columns, table):
+    return lax.dot_general(
+        columns, table, (((1,), (1,)), ((), ())),
+        precision=highest, preferred_element_type=jnp.float32,
+    )
+
+
+def first_kernel(sizes, first_ref, model_ref, table_ref, out_ref):
+    rows, width, span_y = sizes
+    length, layers = table_ref.shape[1:]
+    first_x = first_ref[0].astype(jnp.float32)
+    first_y = first_ref[1].astype(jnp.float32)
+    step = 128
+
+    def turn(index, carry):
+        start = pl.multiple_of(index * step, step)
+        pair = block_tables(first_x, first_y, span_y, start, step, layers)
+        table_ref[0, pl.ds(start, step), :] = pair[0]
+        table_ref[1, pl.ds(start, step), :] = pair[1]
+        return carry
+
+    lax.fori_loop(0, length // step, turn, 0)
+    for field in range(2):
+        spread_rows(
+            project(model_ref[field], table_ref[field]), out_ref, field, rows, width, span_y
+        )
+
+
+def middle_kernel(sizes, surface_ref, table_ref, force_ref, data_ref, out_ref, shift_ref, grad_ref):
+    rows, width, span_y = sizes
+    length, layers = table_ref.shape[1:]
+    chunks = surface_ref.shape[0] // 2
+    tall = -(-(rows + 1) // 8) * 8
+    shift_ref[...] = jnp.zeros_like(shift_ref)
+    for field in range(2):
+        pieces = [
+            surface_ref[field * chunks + chunk : field * chunks + chunk + 1, :]
+            for chunk in range(chunks)
+        ]
+        pieces.append(jnp.zeros((1, length - chunks * 128), jnp.float32))
+        flat = jnp.concatenate(pieces, axis=1)
+        for i in range(rows + 1):
+            amount = (rows - i) * span_y
+            shift_ref[i : i + 1, :] = pltpu.roll(flat, amount, 1) if amount else flat
+        base = shift_ref[0:tall, :]
+        for j in range(width):
+            shift_ref[j * tall : (j + 1) * tall, :] = pltpu.roll(base, width - j, 1)
+        shift_ref[width * tall : (width + 1) * tall, :] = base
+        wide = jnp.dot(
+            shift_ref[...], table_ref[field],
+            precision=highest, preferred_element_type=jnp.float32,
+        )
+        for j in range(width + 1):
+            for i in range(rows + 1):
+                data_ref[field, i, j : j + 1, :] = wide[j * tall + i : j * tall + i + 1]
+            if j < width:
+                grad_ref[j * rows : (j + 1) * rows, :] = (
+                    wide[j * tall : j * tall + rows] + force_ref[field, j]
+                )
+        spread_rows(
+            project(grad_ref[...], table_ref[field]), out_ref, field, rows, width, span_y
+        )
 
 
 def masks(rows, width, start_x, start_y, total_x, total_y):
@@ -140,7 +225,9 @@
     observed = packed[4:6]
     weight = packed[6:8]
     hot_x = (cells // total_y)[:, :, None] == jnp.arange(total_x, dtype=jnp.int32)
-    hot_y = (cells % total_y)[:, :, None] == jnp.arange(total_y, dtype=jnp.int32)
+    span_y = -(-(total_y + width) // 8) * 8
+    surface_shape = (2, total_x, span_y)
+    hot_y = (cells % total_y)[:, :, None] == jnp.arange(span_y, dtype=jnp.int32)
     hot_x = hot_x.astype(jnp.float32)
     hot_y = hot_y.astype(jnp.float32)
     same = (lines[:, :, None] == lines[:, None, :]).astype(jnp.bfloat16)
@@ -162,42 +249,24 @@
         picked = jnp.einsum("fsy,fxy->fsx", hot_y, surface, precision=highest)
         return jnp.sum(picked * hot_x, axis=2)
 
-    span_x = total_x + rows
-    span_y = -(-(total_y + width) // 8) * 8
-    table = tables(-rows - anchor_x, -width - anchor_y, span_x, span_y, layers)
-    flat = table.reshape(2, span_x * span_y, layers)
-
-    def forward(fields):
-        by_offset = jnp.einsum(
-            "fck,fpk->fcp", fields.reshape(2, rows * width, layers), flat, precision=highest
-        ).reshape(2, rows, width, span_x, span_y)
-        over_x = sum(
-            lax.slice_in_dim(by_offset[:, i], rows - i, rows - i + total_x, axis=2)
-            for i in range(rows)
-        )
-        return sum(
-            lax.slice_in_dim(over_x[:, j], width - j, width - j + total_y, axis=2)
-            for j in range(width)
-        )
-
-    def adjoint(surface):
-        padded = jnp.pad(
-            surface, ((0, 0), (rows, rows), (width, span_y - total_y))
-        )
-        shifted = jnp.stack(
-            [
-                padded[:, i : i + span_x, j : j + span_y]
-                for i in range(rows + 1)
-                for j in range(width + 1)
-            ],
-            axis=1,
-        )
-        return jnp.einsum(
-            "fcp,fpk->fck",
-            shifted.reshape(2, (rows + 1) * (width + 1), span_x * span_y),
-            flat,
-            precision=highest,
-        ).reshape(2, rows + 1, width + 1, layers)
+    sizes = (rows, width, span_y)
+    length = -(-(total_x + rows) // 16) * 16 * span_y
+    chunks = -(-total_x * span_y // 128)
+    vmem = pl.BlockSpec(memory_space=pltpu.VMEM)
+    surface_out = jax.ShapeDtypeStruct((2 * chunks, 128), jnp.float32)
+    table_out = jax.ShapeDtypeStruct((2, length, layers), jnp.float32)
+    wide_shape = (2, rows + 1, width + 1, layers)
+    tall = -(-(rows + 1) // 8) * 8
+    by_column = jnp.swapaxes(models, 1, 2).reshape(2, width * rows, layers)
+    table, predicted = pl.pallas_call(
+        functools.partial(first_kernel, sizes),
+        in_specs=[pl.BlockSpec(memory_space=pltpu.SMEM), vmem],
+        out_specs=(vmem, vmem),
+        out_shape=(table_out, surface_out),
+    )(jnp.stack([-rows - anchor_x, -width - anchor_y]), by_column)
+
+    def on_surface(sums):
+        return sums.reshape(2, chunks * 128)[:, : total_x * span_y].reshape(surface_shape)
 
     wide = extended(models, 1, 2)
     mask_x, mask_y, valid = masks(
@@ -215,20 +284,29 @@
         ]
     )
     cross_force = force[:, :rows, :width]
-
-    surface_shape = (2, total_x, total_y)
-    predicted = everywhere(forward(models).reshape(-1, 128)).reshape(surface_shape)
-    predicted = at_stations(predicted)
+    pulled = coupling * jnp.swapaxes(cross_force, 1, 2)
+
+    predicted = at_stations(on_surface(everywhere(predicted)))
     residual = level(predicted - observed)
     weighted = weight * residual
     source = level(weight * weighted)
     surface = jnp.einsum("fsx,fsy->fxy", hot_x * source[:, :, None], hot_y, precision=highest)
-    data_wide = adjoint(surface)
+    surface = surface.reshape(2, total_x * span_y)
+    surface = jnp.pad(surface, ((0, 0), (0, chunks * 128 - total_x * span_y)))
+    data_wide, image_part = pl.pallas_call(
+        functools.partial(middle_kernel, sizes),
+        in_specs=[vmem, vmem, vmem],
+        out_specs=(vmem, vmem),
+        out_shape=(jax.ShapeDtypeStruct(wide_shape, jnp.float32), surface_out),
+        scratch_shapes=[
+            pltpu.VMEM(((width + 1) * tall, length), jnp.float32),
+            pltpu.VMEM((width * rows, layers), jnp.float32),
+        ],
+    )(surface.reshape(2 * chunks, 128), table, pulled)
     data_gradient = data_wide[:, :rows, :width]
     gradient_wide = data_wide + coupling * force
     gradient = gradient_wide[:, :rows, :width]
 
-    image_part = forward(gradient)
     own_a = tuple(part[1:-1, 1:-1] for part in a)
     own_b = tuple(part[1:-1, 1:-1] for part in b)
     own_t = tuple(part[1:-1, 1:-1] for part in t)
@@ -246,19 +324,16 @@
             jnp.sum(inner(t2, t2)),
         ]
     )
-    surface_size = 2 * total_x * total_y
     tail = jnp.concatenate([powers, jnp.max(jnp.abs(gradient))[None]])
-    sent = jnp.concatenate([image_part.reshape(surface_size), tail])
-    sent = jnp.pad(sent, (0, -sent.shape[0] % 1024)).reshape(-1, 128)
-    got = from_all(sent)
-    total = jnp.sum(got, axis=0).reshape(-1)
-    peak_row, peak_lane = divmod(surface_size + 5, 128)
-    peak = jnp.max(got[:, peak_row, peak_lane]) + 1e-06
-    image = at_stations(total[:surface_size].reshape(surface_shape)) / peak
+    tail = jnp.broadcast_to(tail[:, None], (6, 128))
+    got = from_all(jnp.concatenate([image_part, jnp.pad(tail, ((0, 2), (0, 0)))]))
+    total = jnp.sum(got, axis=0)
+    peak = jnp.max(got[:, 2 * chunks + 5, 0]) + 1e-06
+    image = at_stations(on_surface(total[: 2 * chunks])) / peak
     change = level(image)
-    moved = weight * (residual - trial_steps[:, None, None] * change)
-    data_value = 0.5 * jnp.sum(moved * moved, axis=(1, 2))
-    sums = total[surface_size : surface_size + 5]
+    moved = weighted.reshape(1, -1) - trial_steps[:, None] * (weight * change).reshape(1, -1)
+    data_value = 0.5 * jnp.sum(moved * moved, axis=1)
+    sums = total[2 * chunks : 2 * chunks + 5, 0]
     ratio = trial_steps / peak
     energy = sums[4]
     for order in (3, 2, 1, 0):

time: 110 us -> 90.6 us (0.82)
  local copies, waits for them, and re-layouts: 40.7 us -> 10 us
  Pallas kernels: 0 us -> 11 us
  matrix products: 10.2 us -> 5.92 us
  waiting for transfers between devices: 11.4 us -> 15.3 us
  other arithmetic: 12.4 us -> 14 us
    another operation x46 -> x2, local copies, waits for them, and re-layouts: 29 us -> 0.16 us  [on_surface(): sums.reshape(2, chunks * 128)[:, :total_x * span_y].reshape(surface_shape)]
    pallas_call x0 -> x2, Pallas kernels: none -> 11 us  [the longest x1 6 us: body(): pl.pallas_call(functools.partial(middle_kernel, sizes), in_specs=[vmem, v...]
    dot_general x3 -> x0, matrix products: 4.36 us -> none  [the longest x2 3.27 us: forward(): jnp.einsum('fck,fpk->fcp', fields.reshape(2, rows * width, layers), flat,...]
    all_to_all x2, waiting for transfers between devices: 10.9 us -> 13.6 us  [from_all(): return lax.all_to_all(copies, ('gx', 'gy'), 0, 0, tiled=True)]
    slice x5 -> x1, local copies, waits for them, and re-layouts: 1.91 us -> 0.01 us  [body(): image = at_stations(on_surface(total[:2 * chunks])) / peak]
    slice x1, local copies, waits for them, and re-layouts: 0.01 us -> 1.46 us  [body(): data_gradient = data_wide[:, :rows, :width]]
    ppermute x2, waiting for transfers between devices: 0.5 us -> 1.7 us  [extended(): lax.ppermute(lax.slice_in_dim(block, size - low, None, axis=dim), axis, f...]
    broadcast_in_dim x4 -> x2, local copies, waits for them, and re-layouts: 1.57 us -> 2.35 us  [from_all(): copies = jnp.broadcast_to(values[None], (count,) + values.shape)]
  transfers between devices with their start and end apart: 9 -> 9, of which waited for: 2 -> 3; matrix products, arithmetic and copies ran while one was open for 8% -> 9% of each run, Pallas kernels for 0% -> 6%
where the time goes in v2:
time: 90.6 us; the launch traced here: 89.6 us
  starting transfers between devices  30.4 us (34%)
  waiting for transfers between devices  15.3 us (17%)
  other arithmetic  14 us (15%)
  Pallas kernels  11 us (12%)
  local copies, waits for them, and re-layouts  10 us (11%)
  matrix products  5.92 us (7%)
  between operations  3.02 us (3%)
    all_to_all x2, starting transfers between devices, from_all(): return lax.all_to_all(copies, ('gx', 'gy'), 0, 0, tiled=True)  15.1 us
    all_to_all x2, waiting for transfers between devices, from_all(): return lax.all_to_all(copies, ('gx', 'gy'), 0, 0, tiled=True)  13.6 us
    ppermute x2, starting transfers between devices, extended(): lax.ppermute(lax.slice_in_dim(block, size - low, None, axis=dim), axis, f...  7.58 us
    pallas_call x1, Pallas kernels, body(): pl.pallas_call(functools.partial(middle_kernel, sizes), in_specs=[vmem, v...  6 us
    ppermute x3, starting transfers between devices, all_groups(): lax.ppermute(values, 'gx', [(i, (i + hop) % groups) for i in range(groups)])  5.07 us
    dot_general x3, matrix products, level(): jnp.einsum('fct,fts->fcs', parts_of(values), same, preferred_element_type...  5 us
    pallas_call x1, Pallas kernels, body(): pl.pallas_call(functools.partial(first_kernel, sizes), in_specs=[pl.Block...  4.99 us
    div x1, other arithmetic, body(): trial_values = (data_value + coupling * 0.5 * energy) / (2 * stations)  3.65 us
  transfers between devices with their start and end apart: 9, of which 3 were waited for; matrix products, arithmetic and copies ran while one was open for 9% of the time, Pallas kernels for 6%

profile of v2, /device:TPU:0, one launch (start us, length us, event | category | flops | bytes accessed | tf_op | source)
XLA Modules:
  0.0 89.6 jit_solution(13165122536706816475)
XLA Ops:
  0.6 0.7 convert_element_type.51
  1.3 0.7 convert_element_type.50
  2.0 0.7 fusion.86
  2.7 4.0 %collective-permute-start.2 = (f32[8,256]{1,0:T(8,128)S(1)}, f32[8,256]{1,0:T(8,128)S(1)}, u32[]{:S(2)}, u32[]{:S(2)}) collective-permute-start(f32[8,256]{1,0:T(8,128)S(1)} %get-tuple-element.107), channel_id=1, source_target_pairs={{0,24},{8,0},{16,8},{24,16},{1,25},{9,1},{17,9},{25,17},{2,26},{10... | collective-permute-start | bytes 24584 | tf_op jit(solution)/shard_map/ppermute | solution.py:188
  8.4 0.7 copy_bitcast_fusion
  9.8 5.0 %shard_map.102 = (f32[2,1920,128]{2,1,0:T(8,128)}, f32[20,128]{1,0:T(8,128)}) custom-call(s32[2]{0:T(128)} %pad_add_fusion.first_ref, f32[2,32,128]{2,1,0:T(8,128)} %fusion.43.model_ref), custom_call_target="tpu_custom_call" | custom-call | tf_op jit(solution)/shard_map/pallas_call | solution.py:261
  14.7 1.5 %broadcast_in_dim.10 = f32[32,20,128]{2,1,0:T(8,128)} broadcast(f32[20,128]{1,0:T(8,128)} %get-tuple-element.8), dimensions={1,2} | broadcast | bytes 337920 | tf_op jit(solution)/shard_map/broadcast_in_dim | solution.py:174
  16.2 5.8 %all-to-all-start = ((f32[32,20,128]{2,1,0:T(8,128)}), f32[32,20,128]{2,1,0:T(8,128)S(1)}, u32[]{:S(2)}, u32[]{:S(2)}) async-start(f32[32,20,128]{2,1,0:T(8,128)} %broadcast_in_dim.10), calls=%async_computation | async-start | bytes 786432 | tf_op jit(solution)/shard_map/all_to_all | solution.py:175
  22.1 1.3 %collective-permute-start.4 = (f32[2,2,4,128]{3,1,2,0:T(2,128)S(1)}, f32[2,2,4,128]{3,1,2,0:T(2,128)S(1)}, u32[]{:S(2)}, u32[]{:S(2)}) collective-permute-start(f32[2,2,4,128]{3,1,2,0:T(2,128)S(1)} %fusion.68), channel_id=1, source_target_pairs={{8,0},{16,8},{24,16},{9,1},{17,9},{25,17},{10,2},{18,10},{26,18},{... | collective-permute-start | bytes 24584 | tf_op jit(solution)/shard_map/ppermute | solution.py:27
  23.4 4.5 %collective-permute-start.3 = (f32[2,1,4,128]{3,1,2,0:T(1,128)S(1)}, f32[2,1,4,128]{3,1,2,0:T(1,128)S(1)}, u32[]{:S(2)}, u32[]{:S(2)}) collective-permute-start(f32[2,1,4,128]{3,1,2,0:T(1,128)S(1)} %fusion.72), channel_id=1, source_target_pairs={{0,8},{8,16},{16,24},{1,9},{9,17},{17,25},{2,10},{10,18},{18,26},{... | collective-permute-start | bytes 12296 | tf_op jit(solution)/shard_map/ppermute | solution.py:24
  28.2 1.0 %collective-permute-done.3 = f32[2,1,4,128]{3,1,2,0:T(1,128)S(1)} collective-permute-done((f32[2,1,4,128]{3,1,2,0:T(1,128)S(1)}, f32[2,1,4,128]{3,1,2,0:T(1,128)S(1)}, u32[]{:S(2)}, u32[]{:S(2)}) %collective-permute-start.3) | collective-permute-done | bytes 4128 | tf_op jit(solution)/shard_map/ppermute | solution.py:24
  29.2 1.3 %collective-permute-start.6 = (f32[2,11,2,128]{3,1,2,0:T(8,128)S(1)}, f32[2,11,2,128]{3,1,2,0:T(8,128)S(1)}, u32[]{:S(2)}, u32[]{:S(2)}) collective-permute-start(f32[2,11,2,128]{3,1,2,0:T(8,128)S(1)} %pad_maximum_fusion.3), channel_id=1, source_target_pairs={{1,0},{2,1},{3,2},{4,3},{5,4},{6,5},{7,6},{9,8},{10,9},{11,10},{12... | collective-permute-start | bytes 67592 | tf_op jit(solution)/shard_map/ppermute | solution.py:27
  30.6 3.0 %collective-permute-start.5 = (f32[2,11,1,128]{3,1,2,0:T(8,128)S(1)}, f32[2,11,1,128]{3,1,2,0:T(8,128)S(1)}, u32[]{:S(2)}, u32[]{:S(2)}) collective-permute-start(f32[2,11,1,128]{3,1,2,0:T(8,128)S(1)} %pad_maximum_fusion.8), channel_id=1, source_target_pairs={{0,1},{1,2},{2,3},{3,4},{4,5},{5,6},{6,7},{8,9},{9,10},{10,11},{11... | collective-permute-start | bytes 33800 | tf_op jit(solution)/shard_map/ppermute | solution.py:24
  33.7 0.7 collective-permute-done.5
  35.1 0.6 multiply_bitcast_fusion
  36.2 1.1 %convert_reduce_fusion = f32[2,1024]{1,0:T(2,128)S(1)} fusion(s32[2,1024]{1,0:T(2,128)S(1)} %get-tuple-element.87), kind=kLoop, calls=%fused_computation.7 | loop fusion | flops 8386560 | bytes 16384 | tf_op jit(solution)/shard_map/reduce_sum | solution.py:234
  37.4 1.7 %fusion.14 = f32[2,1024]{1,0:T(2,128)S(1)} fusion(s32[2,1024]{1,0:T(2,128)S(1)} %get-tuple-element.87, bf16[2,1,1024]{2,1,0:T(2,128)(2,1)S(1)} %copy.89, bf16[2,1,1024]{2,1,0:T(2,128)(2,1)S(1)} %copy.88, bf16[2,1,1024]{2,1,0:T(2,128)(2,1)S(1)} %copy.87), kind=kOutput, calls=%fused_computation.18 | convolution fusion | flops 14721024 | bytes 28672 | tf_op jit(solution)/shard_map/fct,fts->fcs/dot_general | solution.py:243
  39.1 1.7 %fusion.17 = f32[2,1024]{1,0:T(2,128)S(1)} fusion(s32[2,1024]{1,0:T(2,128)S(1)} %get-tuple-element.87, bf16[2,1,1024]{2,1,0:T(2,128)(2,1)S(1)} %copy.92, bf16[2,1,1024]{2,1,0:T(2,128)(2,1)S(1)} %copy.91, bf16[2,1,1024]{2,1,0:T(2,128)(2,1)S(1)} %copy.90), kind=kOutput, calls=%fused_computation.19 | convolution fusion | flops 14721024 | bytes 28672 | tf_op jit(solution)/shard_map/fct,fts->fcs/dot_general | solution.py:243
  41.2 0.7 reshape.171.surface_ref
  41.8 6.0 %shard_map.103 = (f32[2,9,5,128]{3,2,1,0:T(8,128)}, f32[20,128]{1,0:T(8,128)}) custom-call(f32[20,128]{1,0:T(8,128)} %reshape.171.surface_ref, f32[2,1920,128]{2,1,0:T(8,128)} %get-tuple-element.9.table_ref, f32[2,4,8,128]{3,2,1,0:T(8,128)} %get-tuple-element.59.force_ref), custom_call_target="tpu_custom_call" | custom-call | tf_op jit(solution)/shard_map/pallas_call | solution.py:296
  47.8 0.9 %fusion.32 = f32[2,9,5,128]{3,1,2,0:T(8,128)S(1)} fusion(f32[1,9,5,128]{3,1,2,0:T(8,128)S(1)} %fusion.38, f32[1,9,5,128]{3,1,2,0:T(8,128)S(1)} %fusion.41, f32[2,9,5,128]{3,2,1,0:T(8,128)} %get-tuple-element.10), kind=kLoop, calls=%fused_computation.36 | loop fusion | flops 34560 | bytes 138240 | tf_op jit(solution)/shard_map/add | solution.py:307
  49.7 0.7 add_reduce_fusion.2
  51.7 2.6 %concatenate.46 = f32[6]{0:T(128)S(1)} concatenate(f32[1]{0:T(128)} %bitcast.25, f32[1]{0:T(128)} %bitcast.29, f32[1]{0:T(128)} %bitcast.30, f32[1]{0:T(128)} %bitcast.31, f32[1]{0:T(128)} %bitcast.32, f32[1]{0:T(128)} %bitcast.33), dimensions={0} | concatenate | bytes 48 | tf_op jit(solution)/shard_map/concatenate | solution.py:327
  54.4 0.8 pad_maximum_fusion.9
  55.2 0.9 broadcast_in_dim.13
  56.0 9.3 %all-to-all-start.1 = ((f32[32,28,128]{2,1,0:T(8,128)}), f32[32,28,128]{2,1,0:T(8,128)S(1)}, u32[]{:S(2)}, u32[]{:S(2)}) async-start(f32[32,28,128]{2,1,0:T(8,128)} %broadcast_in_dim.13), calls=%async_computation.1 | async-start | bytes 1048576 | tf_op jit(solution)/shard_map/all_to_all | solution.py:175
  65.4 0.6 copy.96
  66.0 1.5 %slice.249 = f32[2,8,4,128]{3,2,1,0:T(4,128)} slice(f32[2,9,5,128]{3,2,1,0:T(8,128)} %get-tuple-element.10), slice={[0:2], [0:8], [0:4], [0:128]} | slice | bytes 65536 | tf_op jit(solution)/shard_map/slice | solution.py:306
  68.1 13.6 %all-to-all-done.1 = f32[32,28,128]{2,1,0:T(8,128)S(1)} async-done(((f32[32,28,128]{2,1,0:T(8,128)}), f32[32,28,128]{2,1,0:T(8,128)S(1)}, u32[]{:S(2)}, u32[]{:S(2)}) %all-to-all-start.1) | async-done | bytes 458784 | tf_op jit(solution)/shard_map/all_to_all | solution.py:175
  82.7 0.6 slice_reduce_fusion
  84.0 1.7 %fusion.20 = f32[2,1024]{1,0:T(2,128)S(1)} fusion(s32[2,1024]{1,0:T(2,128)S(1)} %get-tuple-element.87, bf16[2,1,1024]{2,1,0:T(2,128)(2,1)S(1)} %get-tuple-element.100, bf16[2,1,1024]{2,1,0:T(2,128)(2,1)S(1)} %get-tuple-element.101, bf16[2,1,1024]{2,1,0:T(2,128)(2,1)S(1)} %get-tuple-element.99), kind=kOutput, calls=%fused_computation.20 | convolution fusion | flops 14721024 | bytes 28672 | tf_op jit(solution)/shard_map/fct,fts->fcs/dot_general | solution.py:243
  85.9 3.6 %add_multiply_fusion = f32[8]{0:T(128)} fusion(f32[8]{0:T(128)S(1)} %copy-done, f32[8]{0:T(128)S(1)} %multiply_reduce_fusion, f32[]{:T(128)} %bitcast.38, f32[]{:T(128)} %bitcast.37, f32[]{:T(128)} %bitcast.36, f32[]{:T(128)} %bitcast.35, f32[]{:T(128)S(6)} %add.227, f32[]{:T(128)} %bitcast.34), kind=kLoop, calls=%fused_computation.185 | loop fusion | flops 104 | bytes 120 | tf_op jit(solution)/shard_map/div | solution.py:341
  (73 shorter events, 7.1 us)
Async XLA Ops:
  2.7 30.9 %collective-permute-start.2 = (f32[8,256]{1,0:T(8,128)S(1)}, f32[8,256]{1,0:T(8,128)S(1)}, u32[]{:S(2)}, u32[]{:S(2)}) collective-permute-start(f32[8,256]{1,0:T(8,128)S(1)} %get-tuple-element.107), channel_id=1, source_target_pairs={{0,24},{8,0},{16,8},{24,16},{1,25},{9,1},{17,9},{25,17},{2,26},{10... | collective-permute-start | bytes 24584 | tf_op jit(solution)/shard_map/ppermute | solution.py:188
  6.7 26.9 %collective-permute-start.1 = (f32[8,256]{1,0:T(8,128)S(1)}, f32[8,256]{1,0:T(8,128)S(1)}, u32[]{:S(2)}, u32[]{:S(2)}) collective-permute-start(f32[8,256]{1,0:T(8,128)S(1)} %get-tuple-element.107), channel_id=1, source_target_pairs={{0,16},{8,24},{16,0},{24,8},{1,17},{9,25},{17,1},{25,9},{2,18},{10... | collective-permute-start | bytes 24584 | tf_op jit(solution)/shard_map/ppermute | solution.py:188
  7.2 26.4 %collective-permute-start = (f32[8,256]{1,0:T(8,128)S(1)}, f32[8,256]{1,0:T(8,128)S(1)}, u32[]{:S(2)}, u32[]{:S(2)}) collective-permute-start(f32[8,256]{1,0:T(8,128)S(1)} %get-tuple-element.107), channel_id=1, source_target_pairs={{0,8},{8,16},{16,24},{24,0},{1,9},{9,17},{17,25},{25,1},{2,10},{10... | collective-permute-start | bytes 24584 | tf_op jit(solution)/shard_map/ppermute | solution.py:188
  16.2 19.5 %all-to-all-start = ((f32[32,20,128]{2,1,0:T(8,128)}), f32[32,20,128]{2,1,0:T(8,128)S(1)}, u32[]{:S(2)}, u32[]{:S(2)}) async-start(f32[32,20,128]{2,1,0:T(8,128)} %broadcast_in_dim.10), calls=%async_computation | async-start | bytes 786432 | tf_op jit(solution)/shard_map/all_to_all | solution.py:175
  22.1 7.2 %collective-permute-start.4 = (f32[2,2,4,128]{3,1,2,0:T(2,128)S(1)}, f32[2,2,4,128]{3,1,2,0:T(2,128)S(1)}, u32[]{:S(2)}, u32[]{:S(2)}) collective-permute-start(f32[2,2,4,128]{3,1,2,0:T(2,128)S(1)} %fusion.68), channel_id=1, source_target_pairs={{8,0},{16,8},{24,16},{9,1},{17,9},{25,17},{10,2},{18,10},{26,18},{... | collective-permute-start | bytes 24584 | tf_op jit(solution)/shard_map/ppermute | solution.py:27
  23.4 5.9 %collective-permute-start.3 = (f32[2,1,4,128]{3,1,2,0:T(1,128)S(1)}, f32[2,1,4,128]{3,1,2,0:T(1,128)S(1)}, u32[]{:S(2)}, u32[]{:S(2)}) collective-permute-start(f32[2,1,4,128]{3,1,2,0:T(1,128)S(1)} %fusion.72), channel_id=1, source_target_pairs={{0,8},{8,16},{16,24},{1,9},{9,17},{17,25},{2,10},{10,18},{18,26},{... | collective-permute-start | bytes 12296 | tf_op jit(solution)/shard_map/ppermute | solution.py:24
  29.2 5.2 %collective-permute-start.6 = (f32[2,11,2,128]{3,1,2,0:T(8,128)S(1)}, f32[2,11,2,128]{3,1,2,0:T(8,128)S(1)}, u32[]{:S(2)}, u32[]{:S(2)}) collective-permute-start(f32[2,11,2,128]{3,1,2,0:T(8,128)S(1)} %pad_maximum_fusion.3), channel_id=1, source_target_pairs={{1,0},{2,1},{3,2},{4,3},{5,4},{6,5},{7,6},{9,8},{10,9},{11,10},{12... | collective-permute-start | bytes 67592 | tf_op jit(solution)/shard_map/ppermute | solution.py:27
  30.6 3.9 %collective-permute-start.5 = (f32[2,11,1,128]{3,1,2,0:T(8,128)S(1)}, f32[2,11,1,128]{3,1,2,0:T(8,128)S(1)}, u32[]{:S(2)}, u32[]{:S(2)}) collective-permute-start(f32[2,11,1,128]{3,1,2,0:T(8,128)S(1)} %pad_maximum_fusion.8), channel_id=1, source_target_pairs={{0,1},{1,2},{2,3},{3,4},{4,5},{5,6},{6,7},{8,9},{9,10},{10,11},{11... | collective-permute-start | bytes 33800 | tf_op jit(solution)/shard_map/ppermute | solution.py:24
  56.0 25.6 %all-to-all-start.1 = ((f32[32,28,128]{2,1,0:T(8,128)}), f32[32,28,128]{2,1,0:T(8,128)S(1)}, u32[]{:S(2)}, u32[]{:S(2)}) async-start(f32[32,28,128]{2,1,0:T(8,128)} %broadcast_in_dim.13), calls=%async_computation.1 | async-start | bytes 1048576 | tf_op jit(solution)/shard_map/all_to_all | solution.py:175
  65.4 20.3 %copy-start = (f32[8]{0:T(128)S(1)}, f32[8]{0:T(128)}, u32[]{:S(2)}) copy-start(f32[8]{0:T(128)} %param.13) | copy-start | bytes 100

commit v3 on v2

--- a/solution.py
+++ b/solution.py
@@ -125,6 +125,79 @@
         )
 
 
+def parts_of(values):
+    first = values.astype(jnp.bfloat16)
+    rest = values - first.astype(jnp.float32)
+    second = rest.astype(jnp.bfloat16)
+    third = (rest - second.astype(jnp.float32)).astype(jnp.bfloat16)
+    return jnp.concatenate([first, second, third], axis=0)
+
+
+def hot_rows(indices, size, kind=jnp.float32):
+    labels = lax.broadcasted_iota(jnp.int32, (size, indices.shape[1]), 0)
+    return (labels == indices).astype(jnp.float32).astype(kind)
+
+
+def leveller(lines):
+    hot = hot_rows(lines, LINES, jnp.bfloat16)
+    over = (((1,), (1,)), ((), ()))
+    ones = jnp.ones((8, lines.shape[1]), jnp.bfloat16)
+    counts = lax.dot_general(ones, hot, over, preferred_element_type=jnp.float32)[0:1]
+    counts = jnp.maximum(counts, 1.0)
+
+    def level(values):
+        sums = lax.dot_general(parts_of(values), hot, over, preferred_element_type=jnp.float32)
+        means = jnp.sum(sums, axis=0, keepdims=True) / counts
+        spread = jnp.dot(parts_of(means), hot, preferred_element_type=jnp.float32)
+        return values - jnp.sum(spread, axis=0, keepdims=True)
+
+    return level
+
+
+def places(cells, total_y, surface):
+    hot_x = hot_rows(cells // total_y, surface.shape[0])
+    hot_y = hot_rows(cells % total_y, surface.shape[1])
+    return hot_x, hot_y
+
+
+def at_stations(surface, hot_x, hot_y):
+    picked = jnp.dot(surface, hot_y, precision=highest, preferred_element_type=jnp.float32)
+    return jnp.sum(picked * hot_x, axis=0, keepdims=True)
+
+
+def source_kernel(total_y, surface_ref, packed_ref, weighted_ref, source_ref):
+    for field in range(2):
+        cells = packed_ref[field : field + 1, :].astype(jnp.int32)
+        level = leveller(packed_ref[2 + field : 3 + field, :].astype(jnp.int32))
+        weight = packed_ref[6 + field : 7 + field, :]
+        hot_x, hot_y = places(cells, total_y, surface_ref[field])
+        predicted = at_stations(surface_ref[field], hot_x, hot_y)
+        weighted = weight * level(predicted - packed_ref[4 + field : 5 + field, :])
+        weighted_ref[field : field + 1, :] = weighted
+        source = level(weight * weighted)
+        source_ref[field] = project(hot_x * source, hot_y)
+
+
+def trial_kernel(total_y, coupling, image_ref, tail_ref, packed_ref, weighted_ref, step_ref, out_ref):
+    peak = jnp.max(tail_ref[5:6, :], axis=1, keepdims=True) + 1e-06
+    steps = step_ref[...]
+    ratio = steps / peak
+    energy = jnp.sum(tail_ref[4:5, :], axis=1, keepdims=True)
+    for order in (3, 2, 1, 0):
+        energy = energy * ratio + jnp.sum(tail_ref[order : order + 1, :], axis=1, keepdims=True)
+    value = coupling * energy
+    for field in range(2):
+        cells = packed_ref[field : field + 1, :].astype(jnp.int32)
+        level = leveller(packed_ref[2 + field : 3 + field, :].astype(jnp.int32))
+        hot_x, hot_y = places(cells, total_y, image_ref[field])
+        image = at_stations(image_ref[field], hot_x, hot_y) / peak
+        change = packed_ref[6 + field : 7 + field, :] * level(image)
+        moved = weighted_ref[field : field + 1, :] - steps * change
+        value = value + jnp.sum(moved * moved, axis=1, keepdims=True)
+    stations = 2 * packed_ref.shape[1]
+    out_ref[...] = 0.5 * value / stations
+
+
 def masks(rows, width, start_x, start_y, total_x, total_y):
     global_x = start_x + jnp.arange(rows, dtype=jnp.int32)
     global_y = start_y + jnp.arange(width, dtype=jnp.int32)
@@ -177,6 +250,18 @@
 
 def everywhere(values):
     return jnp.sum(from_all(values), axis=0)
+
+
+def doubled(values, largest):
+    is_largest = lax.broadcasted_iota(jnp.int32, values.shape, 0) == largest
+    for axis in ("gy", "gx"):
+        count = lax.axis_size(axis)
+        hop = 1
+        while hop < count:
+            other = lax.ppermute(values, axis, [(i, i ^ hop) for i in range(count)])
+            values = jnp.where(is_largest, jnp.maximum(values, other), values + other)
+            hop *= 2
+    return values
 
 
 def all_groups(values):
@@ -220,35 +305,8 @@
         ]
     )
     packed = all_groups(packed)
-    cells = packed[0:2].astype(jnp.int32)
-    lines = packed[2:4].astype(jnp.int32)
-    observed = packed[4:6]
-    weight = packed[6:8]
-    hot_x = (cells // total_y)[:, :, None] == jnp.arange(total_x, dtype=jnp.int32)
     span_y = -(-(total_y + width) // 8) * 8
     surface_shape = (2, total_x, span_y)
-    hot_y = (cells % total_y)[:, :, None] == jnp.arange(span_y, dtype=jnp.int32)
-    hot_x = hot_x.astype(jnp.float32)
-    hot_y = hot_y.astype(jnp.float32)
-    same = (lines[:, :, None] == lines[:, None, :]).astype(jnp.bfloat16)
-    counts = jnp.sum(same.astype(jnp.float32), axis=2)
-
-    def parts_of(values):
-        first = lax.reduce_precision(values, 8, 7)
-        rest = values - first
-        second = lax.reduce_precision(rest, 8, 7)
-        return jnp.stack([first, second, rest - second], axis=1).astype(jnp.bfloat16)
-
-    def level(values):
-        sums = jnp.einsum(
-            "fct,fts->fcs", parts_of(values), same, preferred_element_type=jnp.float32
-        )
-        return values - jnp.sum(sums, axis=1) / jnp.maximum(counts, 1.0)
-
-    def at_stations(surface):
-        picked = jnp.einsum("fsy,fxy->fsx", hot_y, surface, precision=highest)
-        return jnp.sum(picked * hot_x, axis=2)
-
     sizes = (rows, width, span_y)
     length = -(-(total_x + rows) // 16) * 16 * span_y
     chunks = -(-total_x * span_y // 128)
@@ -286,11 +344,15 @@
     cross_force = force[:, :rows, :width]
     pulled = coupling * jnp.swapaxes(cross_force, 1, 2)
 
-    predicted = at_stations(on_surface(everywhere(predicted)))
-    residual = level(predicted - observed)
-    weighted = weight * residual
-    source = level(weight * weighted)
-    surface = jnp.einsum("fsx,fsy->fxy", hot_x * source[:, :, None], hot_y, precision=highest)
+    weighted, surface = pl.pallas_call(
+        functools.partial(source_kernel, total_y),
+        in_specs=[vmem, vmem],
+        out_specs=(vmem, vmem),
+        out_shape=(
+            jax.ShapeDtypeStruct((2, stations), jnp.float32),
+            jax.ShapeDtypeStruct(surface_shape, jnp.float32),
+        ),
+    )(on_surface(everywhere(predicted)), packed)
     surface = surface.reshape(2, total_x * span_y)
     surface = jnp.pad(surface, ((0, 0), (0, chunks * 128 - total_x * span_y)))
     data_wide, image_part = pl.pallas_call(
@@ -315,30 +377,31 @@
     db = differences(gradient_wide[1], *own_mask)
     t1 = tuple(-(p + q) for p, q in zip(cross(da, own_b), cross(own_a, db)))
     t2 = cross(da, db)
-    powers = jnp.stack(
-        [
-            jnp.sum(inner(own_t, own_t)),
-            2.0 * jnp.sum(inner(own_t, t1)),
-            jnp.sum(inner(t1, t1) + 2.0 * inner(own_t, t2)),
-            2.0 * jnp.sum(inner(t1, t2)),
-            jnp.sum(inner(t2, t2)),
-        ]
-    )
-    tail = jnp.concatenate([powers, jnp.max(jnp.abs(gradient))[None]])
-    tail = jnp.broadcast_to(tail[:, None], (6, 128))
-    got = from_all(jnp.concatenate([image_part, jnp.pad(tail, ((0, 2), (0, 0)))]))
-    total = jnp.sum(got, axis=0)
-    peak = jnp.max(got[:, 2 * chunks + 5, 0]) + 1e-06
-    image = at_stations(on_surface(total[: 2 * chunks])) / peak
-    change = level(image)
-    moved = weighted.reshape(1, -1) - trial_steps[:, None] * (weight * change).reshape(1, -1)
-    data_value = 0.5 * jnp.sum(moved * moved, axis=1)
-    sums = total[2 * chunks : 2 * chunks + 5, 0]
-    ratio = trial_steps / peak
-    energy = sums[4]
-    for order in (3, 2, 1, 0):
-        energy = energy * ratio + sums[order]
-    trial_values = (data_value + coupling * 0.5 * energy) / (2 * stations)
+    def lanes(values):
+        return jnp.sum(values, axis=(0, 1))[None]
+
+    tail = (
+        lanes(inner(own_t, own_t)),
+        lanes(2.0 * inner(own_t, t1)),
+        lanes(inner(t1, t1) + 2.0 * inner(own_t, t2)),
+        lanes(2.0 * inner(t1, t2)),
+        lanes(inner(t2, t2)),
+        jnp.max(jnp.abs(gradient), axis=(0, 1, 2))[None],
+        jnp.zeros((2, layers), jnp.float32),
+    )
+    total = doubled(jnp.concatenate((image_part,) + tail), 2 * chunks + 5)
+    trial_values = pl.pallas_call(
+        functools.partial(trial_kernel, total_y, coupling),
+        in_specs=[vmem] * 5,
+        out_specs=vmem,
+        out_shape=jax.ShapeDtypeStruct((trial_steps.shape[0], 1), jnp.float32),
+    )(
+        on_surface(total[: 2 * chunks]),
+        total[2 * chunks :],
+        packed,
+        weighted,
+        trial_steps[:, None],
+    )[:, 0]
     weighted_residual = lax.dynamic_slice_in_dim(
         weighted, group * station_cell.shape[1], station_cell.shape[1], 1
     )

time: 90.6 us -> 79.3 us (0.88)
  waiting for transfers between devices: 15.3 us -> 5.85 us
  Pallas kernels: 11 us -> 18.7 us
  matrix products: 5.92 us -> 0 us
  other arithmetic: 14 us -> 8.37 us
  starting transfers between devices: 30.4 us -> 34.1 us
  between operations: 3.02 us -> 0.88 us
    all_to_all x2 -> x1, waiting for transfers between devices: 13.6 us -> 0.01 us  [from_all(): return lax.all_to_all(copies, ('gx', 'gy'), 0, 0, tiled=True)]
    ppermute x0 -> x5, starting transfers between devices: none -> 13 us  [doubled(): other = lax.ppermute(values, axis, [(i, i ^ hop) for i in range(count)])]
    all_to_all x2 -> x1, starting transfers between devices: 15.1 us -> 5.79 us  [from_all(): return lax.all_to_all(copies, ('gx', 'gy'), 0, 0, tiled=True)]
    pallas_call x0 -> x2, Pallas kernels: none -> 7.67 us  [the longest x1 4.91 us: body(): pl.pallas_call(functools.partial(source_kernel, total_y), in_specs=[vmem,...]
    dot_general x6 -> x0, matrix products: 5.92 us -> none  [the longest x3 5 us: level(): jnp.einsum('fct,fts->fcs', parts_of(values), same, preferred_element_type...]
    ppermute x0 -> x5, waiting for transfers between devices: none -> 4.69 us  [doubled(): other = lax.ppermute(values, axis, [(i, i ^ hop) for i in range(count)])]
    div x2 -> x0, other arithmetic: 3.66 us -> none  [the longest x1 3.65 us: body(): trial_values = (data_value + coupling * 0.5 * energy) / (2 * stations)]
    reduce_sum x4 -> x1, other arithmetic: 2.08 us -> 0.05 us  [lanes(): return jnp.sum(values, axis=(0, 1))[None]]
  transfers between devices with their start and end apart: 9 -> 13, of which waited for: 3 -> 6; matrix products, arithmetic and copies ran while one was open for 9% -> 12% of each run, Pallas kernels for 6% -> 6%
where the time goes in v3:
time: 79.3 us; the launch traced here: 78.3 us
  starting transfers between devices  34.1 us (43%)
  Pallas kernels  18.7 us (24%)
  local copies, waits for them, and re-layouts  10.5 us (13%)
  other arithmetic  8.37 us (11%)
  waiting for transfers between devices  5.85 us (7%)
  between operations  0.88 us (1%)
    ppermute x5, starting transfers between devices, doubled(): other = lax.ppermute(values, axis, [(i, i ^ hop) for i in range(count)])  13 us
    ppermute x2, starting transfers between devices, extended(): lax.ppermute(lax.slice_in_dim(block, size - low, None, axis=dim), axis, f...  7.58 us
    pallas_call x1, Pallas kernels, body(): pl.pallas_call(functools.partial(middle_kernel, sizes), in_specs=[vmem, v...  6 us
    all_to_all x1, starting transfers between devices, from_all(): return lax.all_to_all(copies, ('gx', 'gy'), 0, 0, tiled=True)  5.79 us
    ppermute x3, starting transfers between devices, all_groups(): lax.ppermute(values, 'gx', [(i, (i + hop) % groups) for i in range(groups)])  5.07 us
    pallas_call x1, Pallas kernels, body(): pl.pallas_call(functools.partial(first_kernel, sizes), in_specs=[pl.Block...  4.98 us
    pallas_call x1, Pallas kernels, body(): pl.pallas_call(functools.partial(source_kernel, total_y), in_specs=[vmem,...  4.91 us
    ppermute x5, waiting for transfers between devices, doubled(): other = lax.ppermute(values, axis, [(i, i ^ hop) for i in range(count)])  4.69 us
  transfers between devices with their start and end apart: 13, of which 6 were waited for; matrix products, arithmetic and copies ran while one was open for 12% of the time, Pallas kernels for 6%

profile of v3, /device:TPU:0, one launch (start us, length us, event | category | flops | bytes accessed | tf_op | source)
XLA Modules:
  0.0 78.3 jit_solution(3762307777722473137)
XLA Ops:
  0.6 0.7 convert_element_type.32
  1.3 0.7 convert_element_type.31
  2.0 0.7 fusion.26
  2.7 4.0 %collective-permute-start.2 = (f32[8,256]{1,0:T(8,128)S(1)}, f32[8,256]{1,0:T(8,128)S(1)}, u32[]{:S(2)}, u32[]{:S(2)}) collective-permute-start(f32[8,256]{1,0:T(8,128)S(1)} %get-tuple-element.71), channel_id=1, source_target_pairs={{0,24},{8,0},{16,8},{24,16},{1,25},{9,1},{17,9},{25,17},{2,26},{10... | collective-permute-start | bytes 24584 | tf_op jit(solution)/shard_map/ppermute | solution.py:273
  8.4 0.7 copy_bitcast_fusion
  9.7 5.0 %shard_map.102 = (f32[2,1920,128]{2,1,0:T(8,128)}, f32[20,128]{1,0:T(8,128)}) custom-call(s32[2]{0:T(128)} %pad_add_fusion.first_ref, f32[2,32,128]{2,1,0:T(8,128)} %fusion.12.model_ref), custom_call_target="tpu_custom_call" | custom-call | tf_op jit(solution)/shard_map/pallas_call | solution.py:319
  14.7 1.5 %broadcast_in_dim.42 = f32[32,20,128]{2,1,0:T(8,128)} broadcast(f32[20,128]{1,0:T(8,128)} %get-tuple-element.10), dimensions={1,2} | broadcast | bytes 337920 | tf_op jit(solution)/shard_map/broadcast_in_dim | solution.py:247
  16.2 5.8 %all-to-all-start = ((f32[32,20,128]{2,1,0:T(8,128)}), f32[32,20,128]{2,1,0:T(8,128)S(1)}, u32[]{:S(2)}, u32[]{:S(2)}) async-start(f32[32,20,128]{2,1,0:T(8,128)} %broadcast_in_dim.42), calls=%async_computation | async-start | bytes 786432 | tf_op jit(solution)/shard_map/all_to_all | solution.py:248
  22.0 1.3 %collective-permute-start.4 = (f32[2,2,4,128]{3,1,2,0:T(2,128)S(1)}, f32[2,2,4,128]{3,1,2,0:T(2,128)S(1)}, u32[]{:S(2)}, u32[]{:S(2)}) collective-permute-start(f32[2,2,4,128]{3,1,2,0:T(2,128)S(1)} %fusion.19), channel_id=1, source_target_pairs={{8,0},{16,8},{24,16},{9,1},{17,9},{25,17},{10,2},{18,10},{26,18},{... | collective-permute-start | bytes 24584 | tf_op jit(solution)/shard_map/ppermute | solution.py:27
  23.3 4.5 %collective-permute-start.3 = (f32[2,1,4,128]{3,1,2,0:T(1,128)S(1)}, f32[2,1,4,128]{3,1,2,0:T(1,128)S(1)}, u32[]{:S(2)}, u32[]{:S(2)}) collective-permute-start(f32[2,1,4,128]{3,1,2,0:T(1,128)S(1)} %fusion.20), channel_id=1, source_target_pairs={{0,8},{8,16},{16,24},{1,9},{9,17},{17,25},{2,10},{10,18},{18,26},{... | collective-permute-start | bytes 12296 | tf_op jit(solution)/shard_map/ppermute | solution.py:24
  28.2 1.0 %collective-permute-done.3 = f32[2,1,4,128]{3,1,2,0:T(1,128)S(1)} collective-permute-done((f32[2,1,4,128]{3,1,2,0:T(1,128)S(1)}, f32[2,1,4,128]{3,1,2,0:T(1,128)S(1)}, u32[]{:S(2)}, u32[]{:S(2)}) %collective-permute-start.3) | collective-permute-done | bytes 4128 | tf_op jit(solution)/shard_map/ppermute | solution.py:24
  29.2 1.3 %collective-permute-start.6 = (f32[2,11,2,128]{3,1,2,0:T(8,128)S(1)}, f32[2,11,2,128]{3,1,2,0:T(8,128)S(1)}, u32[]{:S(2)}, u32[]{:S(2)}) collective-permute-start(f32[2,11,2,128]{3,1,2,0:T(8,128)S(1)} %pad_maximum_fusion.3), channel_id=1, source_target_pairs={{1,0},{2,1},{3,2},{4,3},{5,4},{6,5},{7,6},{9,8},{10,9},{11,10},{12... | collective-permute-start | bytes 67592 | tf_op jit(solution)/shard_map/ppermute | solution.py:27
  30.5 3.0 %collective-permute-start.5 = (f32[2,11,1,128]{3,1,2,0:T(8,128)S(1)}, f32[2,11,1,128]{3,1,2,0:T(8,128)S(1)}, u32[]{:S(2)}, u32[]{:S(2)}) collective-permute-start(f32[2,11,1,128]{3,1,2,0:T(8,128)S(1)} %pad_maximum_fusion.8), channel_id=1, source_target_pairs={{0,1},{1,2},{2,3},{3,4},{4,5},{5,6},{6,7},{8,9},{9,10},{10,11},{11... | collective-permute-start | bytes 33800 | tf_op jit(solution)/shard_map/ppermute | solution.py:24
  35.7 0.7 reshape_reshape.6.surface_ref
  36.4 4.9 %shard_map.103 = (f32[2,1024]{1,0:T(2,128)}, f32[2,32,40]{2,1,0:T(8,128)}) custom-call(f32[2,32,40]{2,1,0:T(8,128)} %reshape_reshape.6.surface_ref, f32[8,1024]{1,0:T(8,128)} %pad_maximum_fusion.7.packed_ref), custom_call_target="tpu_custom_call" | custom-call | tf_op jit(solution)/shard_map/pallas_call | solution.py:347
  41.3 1.4 %reshape.120.surface_ref = f32[20,128]{1,0:T(8,128)} reshape(f32[2,32,40]{2,1,0:T(8,128)} %get-tuple-element.11) | data formatting | bytes 20480 | tf_op jit(solution)/shard_map/reshape | solution.py:367
  42.8 6.0 %shard_map.104 = (f32[2,9,5,128]{3,2,1,0:T(8,128)}, f32[20,128]{1,0:T(8,128)}) custom-call(f32[20,128]{1,0:T(8,128)} %reshape.120.surface_ref, f32[2,1920,128]{2,1,0:T(8,128)} %get-tuple-element.12.table_ref, f32[2,4,8,128]{3,2,1,0:T(8,128)} %get-tuple-element.43.force_ref), custom_call_target="tpu_custom_call" | custom-call | tf_op jit(solution)/shard_map/pallas_call | solution.py:358
  48.8 0.9 %fusion.1 = f32[2,9,5,128]{3,1,2,0:T(8,128)S(1)} fusion(f32[1,9,5,128]{3,1,2,0:T(8,128)S(1)} %fusion.7, f32[1,9,5,128]{3,1,2,0:T(8,128)S(1)} %fusion.10, f32[2,9,5,128]{3,2,1,0:T(8,128)} %get-tuple-element.13), kind=kLoop, calls=%fused_computation.5 | loop fusion | flops 34560 | bytes 138240 | tf_op jit(solution)/shard_map/add | solution.py:369
  50.1 0.8 concatenate.43
  50.9 1.5 %collective-permute-start.7 = (f32[28,128]{1,0:T(8,128)S(1)}, f32[28,128]{1,0:T(8,128)S(1)}, u32[]{:S(2)}, u32[]{:S(2)}) collective-permute-start(f32[28,128]{1,0:T(8,128)S(1)} %concatenate.43), channel_id=1, source_target_pairs={{0,1},{1,0},{2,3},{3,2},{4,5},{5,4},{6,7},{7,6},{8,9},{9,8},{10,11... | collective-permute-start | bytes 43016 | tf_op jit(solution)/shard_map/ppermute | solution.py:261
  52.3 0.8 %collective-permute-done.7 = f32[28,128]{1,0:T(8,128)S(1)} collective-permute-done((f32[28,128]{1,0:T(8,128)S(1)}, f32[28,128]{1,0:T(8,128)S(1)}, u32[]{:S(2)}, u32[]{:S(2)}) %collective-permute-start.7) | collective-permute-done | bytes 14368 | tf_op jit(solution)/shard_map/ppermute | solution.py:261
  53.2 2.5 %collective-permute-start.8 = (f32[28,128]{1,0:T(8,128)S(1)}, f32[28,128]{1,0:T(8,128)S(1)}, u32[]{:S(2)}, u32[]{:S(2)}) collective-permute-start(f32[28,128]{1,0:T(8,128)S(1)} %add_select_fusion.4), channel_id=1, source_target_pairs={{0,2},{1,3},{2,0},{3,1},{4,6},{5,7},{6,4},{7,5},{8,10},{9,11},{10,... | collective-permute-start | bytes 43016 | tf_op jit(solution)/shard_map/ppermute | solution.py:261
  55.8 1.7 %collective-permute-done.8 = f32[28,128]{1,0:T(8,128)S(1)} collective-permute-done((f32[28,128]{1,0:T(8,128)S(1)}, f32[28,128]{1,0:T(8,128)S(1)}, u32[]{:S(2)}, u32[]{:S(2)}) %collective-permute-start.8) | collective-permute-done | bytes 14368 | tf_op jit(solution)/shard_map/ppermute | solution.py:261
  57.6 2.9 %collective-permute-start.9 = (f32[28,128]{1,0:T(8,128)S(1)}, f32[28,128]{1,0:T(8,128)S(1)}, u32[]{:S(2)}, u32[]{:S(2)}) collective-permute-start(f32[28,128]{1,0:T(8,128)S(1)} %add_select_fusion.3), channel_id=1, source_target_pairs={{0,4},{1,5},{2,6},{3,7},{4,0},{5,1},{6,2},{7,3},{8,12},{9,13},{10,... | collective-permute-start | bytes 43016 | tf_op jit(solution)/shard_map/ppermute | solution.py:261
  60.5 1.7 %collective-permute-done.9 = f32[28,128]{1,0:T(8,128)S(1)} collective-permute-done((f32[28,128]{1,0:T(8,128)S(1)}, f32[28,128]{1,0:T(8,128)S(1)}, u32[]{:S(2)}, u32[]{:S(2)}) %collective-permute-start.9) | collective-permute-done | bytes 14368 | tf_op jit(solution)/shard_map/ppermute | solution.py:261
  62.3 2.4 %collective-permute-start.10 = (f32[28,128]{1,0:T(8,128)S(1)}, f32[28,128]{1,0:T(8,128)S(1)}, u32[]{:S(2)}, u32[]{:S(2)}) collective-permute-start(f32[28,128]{1,0:T(8,128)S(1)} %add_select_fusion.2), channel_id=1, source_target_pairs={{0,8},{8,0},{16,24},{24,16},{1,9},{9,1},{17,25},{25,17},{2,10},{10... | collective-permute-start | bytes 43016 | tf_op jit(solution)/shard_map/ppermute | solution.py:261
  66.4 3.7 %collective-permute-start.11 = (f32[28,128]{1,0:T(8,128)S(1)}, f32[28,128]{1,0:T(8,128)S(1)}, u32[]{:S(2)}, u32[]{:S(2)}) collective-permute-start(f32[28,128]{1,0:T(8,128)S(1)} %add_select_fusion.1), channel_id=1, source_target_pairs={{0,16},{8,24},{16,0},{24,8},{1,17},{9,25},{17,1},{25,9},{2,18},{10... | collective-permute-start | bytes 43016 | tf_op jit(solution)/shard_map/ppermute | solution.py:261
  70.2 1.2 %constant_dynamic-slice_fusion = f32[2,256]{1,0:T(2,128)} fusion(f32[2,1024]{1,0:T(2,128)} %get-tuple-element.14.weighted_ref, s32[]{:T(128)S(6)} %select_n.68), kind=kLoop, calls=%fused_computation.99 | loop fusion | bytes 4100 | tf_op jit(solution)/shard_map/dynamic_slice | solution.py:405
  71.4 1.5 %slice.207 = f32[2,8,4,128]{3,2,1,0:T(4,128)} slice(f32[2,9,5,128]{3,2,1,0:T(8,128)} %get-tuple-element.13), slice={[0:2], [0:8], [0:4], [0:128]} | slice | bytes 65536 | tf_op jit(solution)/shard_map/slice | solution.py:368
  73.6 0.7 reshape_reshape.7.image_ref
  74.3 2.8 %shard_map.105 = f32[8,1]{1,0:T(8,128)} custom-call(f32[2,32,40]{2,1,0:T(8,128)} %reshape_reshape.7.image_ref, f32[8,128]{1,0:T(8,128)} %slice.285.tail_ref, f32[8,1024]{1,0:T(8,128)} %pad_maximum_fusion.7.packed_ref, f32[2,1024]{1,0:T(2,128)} %get-tuple-element.14.weighted_ref, f32[8,1]{1,0:T(8,128)} %copy.30.step_ref), custom_call_target="tpu_custom_call" | custom-call | tf_op jit(solution)/shard_map/pallas_call | solution.py:393
  77.0 1.3 %reduce = f32[8]{0:T(128)} reduce(f32[8,1]{1,0:T(8,128)} %shard_map.105, f32[]{:T(128)} %constant.103), dimensions={1}, to_apply=%pallas_call.27.reduce_sub_computation | reduce | bytes 68 | tf_op jit(solution)/shard_map/pallas_call | solution.py:393
  (61 shorter events, 7.8 us)
Async XLA Ops:
  2.7 30.9 %collective-permute-start.2 = (f32[8,256]{1,0:T(8,128)S(1)}, f32[8,256]{1,0:T(8,128)S(1)}, u32[]{:S(2)}, u32[]{:S(2)}) collective-permute-start(f32[8,256]{1,0:T(8,128)S(1)} %get-tuple-element.71), channel_id=1, source_target_pairs={{0,24},{8,0},{16,8},{24,16},{1,25},{9,1},{17,9},{25,17},{2,26},{10... | collective-permute-start | bytes 24584 | tf_op jit(solution)/shard_map/ppermute | solution.py:273
  6.7 26.9 %collective-permute-start.1 = (f32[8,256]{1,0:T(8,128)S(1)}, f32[8,256]{1,0:T(8,128)S(1)}, u32[]{:S(2)}, u32[]{:S(2)}) collective-permute-start(f32[8,256]{1,0:T(8,128)S(1)} %get-tuple-element.71), channel_id=1, source_target_pairs={{0,16},{8,24},{16,0},{24,8},{1,17},{9,25},{17,1},{25,9},{2,18},{10... | collective-permute-start | bytes 24584 | tf_op jit(solution)/shard_map/ppermute | solution.py:273
  7.2 26.4 %collective-permute-start = (f32[8,256]{1,0:T(8,128)S(1)}, f32[8,256]{1,0:T(8,128)S(1)}, u32[]{:S(2)}, u32[]{:S(2)}) collective-permute-start(f32[8,256]{1,0:T(8,128)S(1)} %get-tuple-element.71), channel_id=1, source_target_pairs={{0,8},{8,16},{16,24},{24,0},{1,9},{9,17},{17,25},{25,1},{2,10},{10... | collective-permute-start | bytes 24584 | tf_op jit(solution)/shard_map/ppermute | solution.py:273
  16.2 19.5 %all-to-all-start = ((f32[32,20,128]{2,1,0:T(8,128)}), f32[32,20,128]{2,1,0:T(8,128)S(1)}, u32[]{:S(2)}, u32[]{:S(2)}) async-start(f32[32,20,128]{2,1,0:T(8,128)} %broadcast_in_dim.42), calls=%async_computation | async-start | bytes 786432 | tf_op jit(solution)/shard_map/all_to_all | solution.py:248
  22.0 7.2 %collective-permute-start.4 = (f32[2,2,4,128]{3,1,2,0:T(2,128)S(1)}, f32[2,2,4,128]{3,1,2,0:T(2,128)S(1)}, u32[]{:S(2)}, u32[]{:S(2)}) collective-permute-start(f32[2,2,4,128]{3,1,2,0:T(2,128)S(1)} %fusion.19), channel_id=1, source_target_pairs={{8,0},{16,8},{24,16},{9,1},{17,9},{25,17},{10,2},{18,10},{26,18},{... | collective-permute-start | bytes 24584 | tf_op jit(solution)/shard_map/ppermute | solution.py:27
  23.3 5.9 %collective-permute-start.3 = (f32[2,1,4,128]{3,1,2,0:T(1,128)S(1)}, f32[2,1,4,128]{3,1,2,0:T(1,128)S(1)}, u32[]{:S(2)}, u32[]{:S(2)}) collective-permute-start(f32[2,1,4,128]{3,1,2,0:T(1,128)S(1)} %fusion.20), channel_id=1, source_target_pairs={{0,8},{8,16},{16,24},{1,9},{9,17},{17,25},{2,10},{10,18},{18,26},{... | collective-permute-start | bytes 12296 | tf_op jit(solution)/shard_map/ppermute | solution.py:24
  29.2 5.2 %collective-permute-start.6 = (f32[2,11,2,128]{3,1,2,0:T(8,128)S(1)}, f32[2,11,2,128]{3,1,2,0:T(8,128)S(1)}, u32[]{:S(2)}, u32[]{:S(2)}) collective-permute-start(f32[2,11,2,128]{3,1,2,0:T(8,128)S(1)} %pad_maximum_fusion.3), channel_id=1, source_target_pairs={{1,0},{2,1},{3,2},{4,3},{5,4},{6,5},{7,6},{9,8},{10,9},{11,10},{12... | collective-permute-start | bytes 67592 | tf_op jit(solution)/shard_map/ppermute | solution.py:27
  30.5 3.9 %collective-permute-start.5 = (f32[2,11,1,128]{3,1,2,0:T(8,128)S(1)}, f32[2,11,1,128]{3,1,2,0:T(8,128)S(1)}, u32[]{:S(2)}, u32[]{:S(2)}) collective-permute-start(f32[2,11,1,128]{3,1,2,0:T(8,128)S(1)} %pad_maximum_fusion.8), channel_id=1, source_target_pairs={{0,1},{1,2},{2,3},{3,4},{4,5},{5,6},{6,7},{8,9},{9,10},{10,11},{11... | collective-permute-start | bytes 33800 | tf_op jit(solution)/shard_map/ppermute | solution.py:24
  35.7 28.9 %copy-start = (f32[8]{0:T(128)S(1)}, f32[8]{0:T(128)}, u32[]{:S(2)}) copy-start(f32[8]{0:T(128)} %param.13) | copy-start | bytes 100
  50.9 2.3 %collective-permute-start.7 = (f32[28,128]{1,0:T(8,128)S(1)}, f32[28,128]{1,0:T(8,128)S(1)}, u32[]{:S(2)}, u32[]{:S(2)}) collective-permute-start(f32[28,128]{1,0:T(8,128)S(1)} %concatenate.43), channel_id=1, source_target_pairs={{0,1},{1,0},{2,3},{3,2},{4,5},{5,4},{6,7},{7,6},{8,9},{9,8},{10,11... | collective-permute-start | bytes 43016 | tf_op jit(solution)/shard_map/ppermute | solution.py:261
  53.2 4.2 %collective-permute-start.8 = (f32[28,128]{1,0:T(8,128)S(1)}, f32[28,128]{1,0:T(8,128)S(1)}, u32[]{:S(2)}, u32[]{:S(2)}) collective-permute-start(f32[28,128]{1,0:T(8,128)S(1)} %add_select_fusion.4), channel_id=1, source_target_pairs={{0,2},{1,3},{2,0},{3,1},{4,6},{5,7},{6,4},{7,5},{8,10},{9,11},{10,... | collective-permute-start | bytes 43016 | tf_op jit(solution)/shard_map/ppermute | solution.py:261
  57.6 4.6 %collective-permute-start.9 = (f32[28,128]{1,0:T(8,128)S(1)}, f32[28,128]{1,0:T(8,128)S(1)}, u32[]{:S(2)}, u32[]{:S(2)}) collective-permute-start(f32[28,128]{1,0:T(8,128)S(1)} %add_select_fusion.3), channel_id=1, source_target_pairs={{0,4},{1,5},{2,6},{3,7},{4,0},{5,1},{6,2},{7,3},{8,12},{9,13},{10,... | collective-permute-start | bytes 43016 | tf_op jit(solution)/shard_map/ppermute | solution.py:261
  62.3 4.1 %collective-permute-start.10 = (f32[28,128]{1,0:T(8,128)S(1)}, f32[28,128]{1,0:T(8,128)S(1)}, u32[]{:S(2)}, u32[]{:S(2)}) collective-permute-start(f32[28,128]{1,0:T(8,128)S(1)} %add_select_fusion.2), channel_id=1, source_target_pairs={{0,8},{8,0},{16,24},{24,16},{1,9},{9,1},{17,25},{25,17},{2,10},{10... | collective-permute-start | bytes 43016 | tf_op jit(solution)/shard_map/ppermute | solution.py:261
  66.4 6.5 %collective-permute-start.11 = (f32[28,128]{1,0:T(8,128)S(1)}, f32[28,128]{1,0:T(8,128)S(1)}, u32[]{:S(2)}, u32[]{:S(2)}) collective-permute-start(f32[28,128]{1,0:T(8,128)S(1)} %add_select_fusion.1), channel_id=1, source_target_pairs={{0,16},{8,24},{16,0},{24,8},{1,17},{9,25},{17,1},{25,9},{2,18},{10... | collective-permute-start | bytes 43016 | tf_op jit(solution)/shard_map/ppermute | solution.py:261

commit v4 on v3

--- a/solution.py
+++ b/solution.py
@@ -92,15 +92,12 @@
 def middle_kernel(sizes, surface_ref, table_ref, force_ref, data_ref, out_ref, shift_ref, grad_ref):
     rows, width, span_y = sizes
     length, layers = table_ref.shape[1:]
-    chunks = surface_ref.shape[0] // 2
     tall = -(-(rows + 1) // 8) * 8
     shift_ref[...] = jnp.zeros_like(shift_ref)
     for field in range(2):
-        pieces = [
-            surface_ref[field * chunks + chunk : field * chunks + chunk + 1, :]
-            for chunk in range(chunks)
-        ]
-        pieces.append(jnp.zeros((1, length - chunks * 128), jnp.float32))
+        surface = surface_ref[field]
+        pieces = [surface[row : row + 1, :] for row in range(surface.shape[0])]
+        pieces.append(jnp.zeros((1, length - surface.size), jnp.float32))
         flat = jnp.concatenate(pieces, axis=1)
         for i in range(rows + 1):
             amount = (rows - i) * span_y
@@ -161,41 +158,74 @@
 
 
 def at_stations(surface, hot_x, hot_y):
-    picked = jnp.dot(surface, hot_y, precision=highest, preferred_element_type=jnp.float32)
+    count = surface.shape[0]
+    parts = jnp.dot(
+        parts_of(surface), hot_y.astype(jnp.bfloat16), preferred_element_type=jnp.float32
+    )
+    picked = parts[:count] + parts[count : 2 * count] + parts[2 * count :]
     return jnp.sum(picked * hot_x, axis=0, keepdims=True)
 
 
-def source_kernel(total_y, surface_ref, packed_ref, weighted_ref, source_ref):
+def to_surface(values, hot_x, hot_y):
+    count = hot_x.shape[0]
+    parts = lax.dot_general(
+        parts_of(hot_x * values), hot_y.astype(jnp.bfloat16), (((1,), (1,)), ((), ())),
+        preferred_element_type=jnp.float32,
+    )
+    return parts[:count] + parts[count : 2 * count] + parts[2 * count :]
+
+
+def unpacked(flat_ref, field, chunks, surface_ref):
+    pieces = [
+        flat_ref[field * chunks + chunk : field * chunks + chunk + 1, :]
+        for chunk in range(chunks)
+    ]
+    flat = jnp.concatenate(pieces, axis=1)
+    rows, span_y = surface_ref.shape
+    for row in range(rows):
+        surface_ref[row : row + 1, :] = flat[:, row * span_y : (row + 1) * span_y]
+    return surface_ref[...]
+
+
+def source_kernel(total_y, surface_ref, packed_ref, weighted_ref, source_ref, hold_ref):
     for field in range(2):
         cells = packed_ref[field : field + 1, :].astype(jnp.int32)
         level = leveller(packed_ref[2 + field : 3 + field, :].astype(jnp.int32))
         weight = packed_ref[6 + field : 7 + field, :]
-        hot_x, hot_y = places(cells, total_y, surface_ref[field])
-        predicted = at_stations(surface_ref[field], hot_x, hot_y)
+        surface = unpacked(surface_ref, field, surface_ref.shape[0] // 2, hold_ref)
+        hot_x, hot_y = places(cells, total_y, surface)
+        predicted = at_stations(surface, hot_x, hot_y)
         weighted = weight * level(predicted - packed_ref[4 + field : 5 + field, :])
         weighted_ref[field : field + 1, :] = weighted
         source = level(weight * weighted)
-        source_ref[field] = project(hot_x * source, hot_y)
-
-
-def trial_kernel(total_y, coupling, image_ref, tail_ref, packed_ref, weighted_ref, step_ref, out_ref):
-    peak = jnp.max(tail_ref[5:6, :], axis=1, keepdims=True) + 1e-06
+        source_ref[field] = to_surface(source, hot_x, hot_y)
+
+
+def trial_kernel(total_y, coupling, total_ref, packed_ref, weighted_ref, step_ref, out_ref, hold_ref):
+    chunks = total_ref.shape[0] // 2 - 4
+    tail = total_ref[2 * chunks :, :]
+    peak = jnp.max(tail[5:6, :], axis=1, keepdims=True) + 1e-06
     steps = step_ref[...]
     ratio = steps / peak
-    energy = jnp.sum(tail_ref[4:5, :], axis=1, keepdims=True)
+    energy = jnp.sum(tail[4:5, :], axis=1, keepdims=True)
     for order in (3, 2, 1, 0):
-        energy = energy * ratio + jnp.sum(tail_ref[order : order + 1, :], axis=1, keepdims=True)
+        energy = energy * ratio + jnp.sum(tail[order : order + 1, :], axis=1, keepdims=True)
     value = coupling * energy
     for field in range(2):
         cells = packed_ref[field : field + 1, :].astype(jnp.int32)
         level = leveller(packed_ref[2 + field : 3 + field, :].astype(jnp.int32))
-        hot_x, hot_y = places(cells, total_y, image_ref[field])
-        image = at_stations(image_ref[field], hot_x, hot_y) / peak
+        surface = unpacked(total_ref, field, chunks, hold_ref)
+        hot_x, hot_y = places(cells, total_y, surface)
+        image = at_stations(surface, hot_x, hot_y) / peak
         change = packed_ref[6 + field : 7 + field, :] * level(image)
         moved = weighted_ref[field : field + 1, :] - steps * change
         value = value + jnp.sum(moved * moved, axis=1, keepdims=True)
     stations = 2 * packed_ref.shape[1]
-    out_ref[...] = 0.5 * value / stations
+    count = value.shape[0]
+    here = lax.broadcasted_iota(jnp.int32, (count, count), 0) == lax.broadcasted_iota(
+        jnp.int32, (count, count), 1
+    )
+    out_ref[...] = jnp.sum(jnp.where(here, 0.5 * value / stations, 0.0), axis=0, keepdims=True)
 
 
 def masks(rows, width, start_x, start_y, total_x, total_y):
@@ -323,9 +353,6 @@
         out_shape=(table_out, surface_out),
     )(jnp.stack([-rows - anchor_x, -width - anchor_y]), by_column)
 
-    def on_surface(sums):
-        return sums.reshape(2, chunks * 128)[:, : total_x * span_y].reshape(surface_shape)
-
     wide = extended(models, 1, 2)
     mask_x, mask_y, valid = masks(
         rows + 2, width + 2, anchor_x - 1, anchor_y - 1, total_x, total_y
@@ -352,9 +379,8 @@
             jax.ShapeDtypeStruct((2, stations), jnp.float32),
             jax.ShapeDtypeStruct(surface_shape, jnp.float32),
         ),
-    )(on_surface(everywhere(predicted)), packed)
-    surface = surface.reshape(2, total_x * span_y)
-    surface = jnp.pad(surface, ((0, 0), (0, chunks * 128 - total_x * span_y)))
+        scratch_shapes=[pltpu.VMEM(surface_shape[1:], jnp.float32)],
+    )(everywhere(predicted), packed)
     data_wide, image_part = pl.pallas_call(
         functools.partial(middle_kernel, sizes),
         in_specs=[vmem, vmem, vmem],
@@ -364,7 +390,7 @@
             pltpu.VMEM(((width + 1) * tall, length), jnp.float32),
             pltpu.VMEM((width * rows, layers), jnp.float32),
         ],
-    )(surface.reshape(2 * chunks, 128), table, pulled)
+    )(surface, table, pulled)
     data_gradient = data_wide[:, :rows, :width]
     gradient_wide = data_wide + coupling * force
     gradient = gradient_wide[:, :rows, :width]
@@ -392,16 +418,12 @@
     total = doubled(jnp.concatenate((image_part,) + tail), 2 * chunks + 5)
     trial_values = pl.pallas_call(
         functools.partial(trial_kernel, total_y, coupling),
-        in_specs=[vmem] * 5,
+        in_specs=[vmem] * 4,
         out_specs=vmem,
-        out_shape=jax.ShapeDtypeStruct((trial_steps.shape[0], 1), jnp.float32),
-    )(
-        on_surface(total[: 2 * chunks]),
-        total[2 * chunks :],
-        packed,
-        weighted,
-        trial_steps[:, None],
-    )[:, 0]
+        out_shape=jax.ShapeDtypeStruct((1, trial_steps.shape[0]), jnp.float32),
+        scratch_shapes=[pltpu.VMEM(surface_shape[1:], jnp.float32)],
+    )(total, packed, weighted, trial_steps[:, None])
+    trial_values = trial_values.reshape(-1)
     weighted_residual = lax.dynamic_slice_in_dim(
         weighted, group * station_cell.shape[1], station_cell.shape[1], 1
     )

time: 79.3 us -> 75.3 us (0.950)
  local copies, waits for them, and re-layouts: 10.5 us -> 7.08 us
    reshape x1 -> x0, local copies, waits for them, and re-layouts: 1.44 us -> none  [body(): surface.reshape(2 * chunks, 128)]
    another operation x2 -> x0, local copies, waits for them, and re-layouts: 1.39 us -> none  [on_surface(): sums.reshape(2, chunks * 128)[:, :total_x * span_y].reshape(surface_shape)]
    pallas_call x1 -> x0, other arithmetic: 1.31 us -> none  [body(): pl.pallas_call(functools.partial(trial_kernel, total_y, coupling), in_spe...]
  transfers between devices with their start and end apart: 13 -> 13, of which waited for: 6 -> 6; matrix products, arithmetic and copies ran while one was open for 12% -> 13% of each run, Pallas kernels for 6% -> 7%
where the time goes in v4:
time: 75.3 us; the launch traced here: 74.4 us
  starting transfers between devices  34.1 us (45%)
  Pallas kernels  18.3 us (24%)
  other arithmetic  8.27 us (11%)
  local copies, waits for them, and re-layouts  7.08 us (9%)
  waiting for transfers between devices  5.85 us (8%)
  between operations  0.87 us (1%)
    ppermute x5, starting transfers between devices, doubled(): other = lax.ppermute(values, axis, [(i, i ^ hop) for i in range(count)])  13 us
    ppermute x2, starting transfers between devices, extended(): lax.ppermute(lax.slice_in_dim(block, size - low, None, axis=dim), axis, f...  7.58 us
    pallas_call x1, Pallas kernels, body(): pl.pallas_call(functools.partial(middle_kernel, sizes), in_specs=[vmem, v...  6.08 us
    all_to_all x1, starting transfers between devices, from_all(): return lax.all_to_all(copies, ('gx', 'gy'), 0, 0, tiled=True)  5.79 us
    ppermute x3, starting transfers between devices, all_groups(): lax.ppermute(values, 'gx', [(i, (i + hop) % groups) for i in range(groups)])  5.07 us
    pallas_call x1, Pallas kernels, body(): pl.pallas_call(functools.partial(first_kernel, sizes), in_specs=[pl.Block...  4.98 us
    ppermute x5, waiting for transfers between devices, doubled(): other = lax.ppermute(values, axis, [(i, i ^ hop) for i in range(count)])  4.69 us
    pallas_call x1, Pallas kernels, body(): pl.pallas_call(functools.partial(source_kernel, total_y), in_specs=[vmem,...  4.33 us
  transfers between devices with their start and end apart: 13, of which 6 were waited for; matrix products, arithmetic and copies ran while one was open for 13% of the time, Pallas kernels for 7%

profile of v4, /device:TPU:0, one launch (start us, length us, event | category | flops | bytes accessed | tf_op | source)
XLA Modules:
  0.0 74.4 jit_solution(1008206267543457028)
XLA Ops:
  0.6 0.7 convert_element_type.32
  1.3 0.7 convert_element_type.31
  2.0 0.7 fusion.26
  2.7 4.0 %collective-permute-start.2 = (f32[8,256]{1,0:T(8,128)S(1)}, f32[8,256]{1,0:T(8,128)S(1)}, u32[]{:S(2)}, u32[]{:S(2)}) collective-permute-start(f32[8,256]{1,0:T(8,128)S(1)} %get-tuple-element.67), channel_id=1, source_target_pairs={{0,24},{8,0},{16,8},{24,16},{1,25},{9,1},{17,9},{25,17},{2,26},{10... | collective-permute-start | bytes 24584 | tf_op jit(solution)/shard_map/ppermute | solution.py:303
  8.4 0.7 copy_bitcast_fusion
  9.7 5.0 %shard_map.102 = (f32[2,1920,128]{2,1,0:T(8,128)}, f32[20,128]{1,0:T(8,128)}) custom-call(s32[2]{0:T(128)} %pad_add_fusion.first_ref, f32[2,32,128]{2,1,0:T(8,128)} %fusion.12.model_ref), custom_call_target="tpu_custom_call" | custom-call | tf_op jit(solution)/shard_map/pallas_call | solution.py:349
  14.7 1.5 %broadcast_in_dim.42 = f32[32,20,128]{2,1,0:T(8,128)} broadcast(f32[20,128]{1,0:T(8,128)} %get-tuple-element.10), dimensions={1,2} | broadcast | bytes 337920 | tf_op jit(solution)/shard_map/broadcast_in_dim | solution.py:277
  16.2 5.8 %all-to-all-start = ((f32[32,20,128]{2,1,0:T(8,128)}), f32[32,20,128]{2,1,0:T(8,128)S(1)}, u32[]{:S(2)}, u32[]{:S(2)}) async-start(f32[32,20,128]{2,1,0:T(8,128)} %broadcast_in_dim.42), calls=%async_computation | async-start | bytes 786432 | tf_op jit(solution)/shard_map/all_to_all | solution.py:278
  22.0 1.3 %collective-permute-start.4 = (f32[2,2,4,128]{3,1,2,0:T(2,128)S(1)}, f32[2,2,4,128]{3,1,2,0:T(2,128)S(1)}, u32[]{:S(2)}, u32[]{:S(2)}) collective-permute-start(f32[2,2,4,128]{3,1,2,0:T(2,128)S(1)} %fusion.19), channel_id=1, source_target_pairs={{8,0},{16,8},{24,16},{9,1},{17,9},{25,17},{10,2},{18,10},{26,18},{... | collective-permute-start | bytes 24584 | tf_op jit(solution)/shard_map/ppermute | solution.py:27
  23.3 4.5 %collective-permute-start.3 = (f32[2,1,4,128]{3,1,2,0:T(1,128)S(1)}, f32[2,1,4,128]{3,1,2,0:T(1,128)S(1)}, u32[]{:S(2)}, u32[]{:S(2)}) collective-permute-start(f32[2,1,4,128]{3,1,2,0:T(1,128)S(1)} %fusion.20), channel_id=1, source_target_pairs={{0,8},{8,16},{16,24},{1,9},{9,17},{17,25},{2,10},{10,18},{18,26},{... | collective-permute-start | bytes 12296 | tf_op jit(solution)/shard_map/ppermute | solution.py:24
  28.2 1.0 %collective-permute-done.3 = f32[2,1,4,128]{3,1,2,0:T(1,128)S(1)} collective-permute-done((f32[2,1,4,128]{3,1,2,0:T(1,128)S(1)}, f32[2,1,4,128]{3,1,2,0:T(1,128)S(1)}, u32[]{:S(2)}, u32[]{:S(2)}) %collective-permute-start.3) | collective-permute-done | bytes 4128 | tf_op jit(solution)/shard_map/ppermute | solution.py:24
  29.2 1.3 %collective-permute-start.6 = (f32[2,11,2,128]{3,1,2,0:T(8,128)S(1)}, f32[2,11,2,128]{3,1,2,0:T(8,128)S(1)}, u32[]{:S(2)}, u32[]{:S(2)}) collective-permute-start(f32[2,11,2,128]{3,1,2,0:T(8,128)S(1)} %pad_maximum_fusion.3), channel_id=1, source_target_pairs={{1,0},{2,1},{3,2},{4,3},{5,4},{6,5},{7,6},{9,8},{10,9},{11,10},{12... | collective-permute-start | bytes 67592 | tf_op jit(solution)/shard_map/ppermute | solution.py:27
  30.5 3.0 %collective-permute-start.5 = (f32[2,11,1,128]{3,1,2,0:T(8,128)S(1)}, f32[2,11,1,128]{3,1,2,0:T(8,128)S(1)}, u32[]{:S(2)}, u32[]{:S(2)}) collective-permute-start(f32[2,11,1,128]{3,1,2,0:T(8,128)S(1)} %pad_maximum_fusion.8), channel_id=1, source_target_pairs={{0,1},{1,2},{2,3},{3,4},{4,5},{5,6},{6,7},{8,9},{9,10},{10,11},{11... | collective-permute-start | bytes 33800 | tf_op jit(solution)/shard_map/ppermute | solution.py:24
  35.7 0.6 reduce_sum.54.surface_ref
  36.3 4.3 %shard_map.103 = (f32[2,1024]{1,0:T(2,128)}, f32[2,32,40]{2,1,0:T(8,128)}) custom-call(f32[20,128]{1,0:T(8,128)} %reduce_sum.54.surface_ref, f32[8,1024]{1,0:T(8,128)} %pad_maximum_fusion.7.packed_ref), custom_call_target="tpu_custom_call" | custom-call | tf_op jit(solution)/shard_map/pallas_call | solution.py:374
  40.6 6.1 %shard_map.104 = (f32[2,9,5,128]{3,2,1,0:T(8,128)}, f32[20,128]{1,0:T(8,128)}) custom-call(f32[2,32,40]{2,1,0:T(8,128)} %get-tuple-element.11.surface_ref, f32[2,1920,128]{2,1,0:T(8,128)} %get-tuple-element.12.table_ref, f32[2,4,8,128]{3,2,1,0:T(8,128)} %get-tuple-element.39.force_ref), custom_call_target="tpu_custom_call" | custom-call | tf_op jit(solution)/shard_map/pallas_call | solution.py:384
  46.7 0.9 %fusion.1 = f32[2,9,5,128]{3,1,2,0:T(8,128)S(1)} fusion(f32[1,9,5,128]{3,1,2,0:T(8,128)S(1)} %fusion.7, f32[1,9,5,128]{3,1,2,0:T(8,128)S(1)} %fusion.10, f32[2,9,5,128]{3,2,1,0:T(8,128)} %get-tuple-element.13), kind=kLoop, calls=%fused_computation.5 | loop fusion | flops 34560 | bytes 138240 | tf_op jit(solution)/shard_map/add | solution.py:395
  48.0 0.8 %concatenate.43 = f32[28,128]{1,0:T(8,128)S(1)} concatenate(f32[20,128]{1,0:T(8,128)} %get-tuple-element.15, f32[1,128]{1,0:T(1,128)S(1)} %bitcast.57, f32[1,128]{1,0:T(1,128)S(1)} %bitcast.56, f32[1,128]{1,0:T(1,128)S(1)} %bitcast.55, f32[1,128]{1,0:T(1,128)S(1)} %bitcast.58, f32[1,128]{1,0:T(1,128)S(1)} %bitcast.59, f32[1,128]{1,0:T(1,128)S(1)} %bitcast.54, ...), dimensions={0} | concatenate | bytes 28672 | tf_op jit(solution)/shard_map/concatenate | solution.py:418
  48.8 1.5 %collective-permute-start.7 = (f32[28,128]{1,0:T(8,128)S(1)}, f32[28,128]{1,0:T(8,128)S(1)}, u32[]{:S(2)}, u32[]{:S(2)}) collective-permute-start(f32[28,128]{1,0:T(8,128)S(1)} %concatenate.43), channel_id=1, source_target_pairs={{0,1},{1,0},{2,3},{3,2},{4,5},{5,4},{6,7},{7,6},{8,9},{9,8},{10,11... | collective-permute-start | bytes 43016 | tf_op jit(solution)/shard_map/ppermute | solution.py:291
  50.3 0.8 %collective-permute-done.7 = f32[28,128]{1,0:T(8,128)S(1)} collective-permute-done((f32[28,128]{1,0:T(8,128)S(1)}, f32[28,128]{1,0:T(8,128)S(1)}, u32[]{:S(2)}, u32[]{:S(2)}) %collective-permute-start.7) | collective-permute-done | bytes 14368 | tf_op jit(solution)/shard_map/ppermute | solution.py:291
  51.2 2.5 %collective-permute-start.8 = (f32[28,128]{1,0:T(8,128)S(1)}, f32[28,128]{1,0:T(8,128)S(1)}, u32[]{:S(2)}, u32[]{:S(2)}) collective-permute-start(f32[28,128]{1,0:T(8,128)S(1)} %add_select_fusion.4), channel_id=1, source_target_pairs={{0,2},{1,3},{2,0},{3,1},{4,6},{5,7},{6,4},{7,5},{8,10},{9,11},{10,... | collective-permute-start | bytes 43016 | tf_op jit(solution)/shard_map/ppermute | solution.py:291
  53.7 1.7 %collective-permute-done.8 = f32[28,128]{1,0:T(8,128)S(1)} collective-permute-done((f32[28,128]{1,0:T(8,128)S(1)}, f32[28,128]{1,0:T(8,128)S(1)}, u32[]{:S(2)}, u32[]{:S(2)}) %collective-permute-start.8) | collective-permute-done | bytes 14368 | tf_op jit(solution)/shard_map/ppermute | solution.py:291
  55.5 2.9 %collective-permute-start.9 = (f32[28,128]{1,0:T(8,128)S(1)}, f32[28,128]{1,0:T(8,128)S(1)}, u32[]{:S(2)}, u32[]{:S(2)}) collective-permute-start(f32[28,128]{1,0:T(8,128)S(1)} %add_select_fusion.3), channel_id=1, source_target_pairs={{0,4},{1,5},{2,6},{3,7},{4,0},{5,1},{6,2},{7,3},{8,12},{9,13},{10,... | collective-permute-start | bytes 43016 | tf_op jit(solution)/shard_map/ppermute | solution.py:291
  58.4 1.7 %collective-permute-done.9 = f32[28,128]{1,0:T(8,128)S(1)} collective-permute-done((f32[28,128]{1,0:T(8,128)S(1)}, f32[28,128]{1,0:T(8,128)S(1)}, u32[]{:S(2)}, u32[]{:S(2)}) %collective-permute-start.9) | collective-permute-done | bytes 14368 | tf_op jit(solution)/shard_map/ppermute | solution.py:291
  60.2 2.4 %collective-permute-start.10 = (f32[28,128]{1,0:T(8,128)S(1)}, f32[28,128]{1,0:T(8,128)S(1)}, u32[]{:S(2)}, u32[]{:S(2)}) collective-permute-start(f32[28,128]{1,0:T(8,128)S(1)} %add_select_fusion.2), channel_id=1, source_target_pairs={{0,8},{8,0},{16,24},{24,16},{1,9},{9,1},{17,25},{25,17},{2,10},{10... | collective-permute-start | bytes 43016 | tf_op jit(solution)/shard_map/ppermute | solution.py:291
  62.6 0.7 copy.25.step_ref
  63.3 0.6 copy.26
  64.4 3.7 %collective-permute-start.11 = (f32[28,128]{1,0:T(8,128)S(1)}, f32[28,128]{1,0:T(8,128)S(1)}, u32[]{:S(2)}, u32[]{:S(2)}) collective-permute-start(f32[28,128]{1,0:T(8,128)S(1)} %add_select_fusion.1), channel_id=1, source_target_pairs={{0,16},{8,24},{16,0},{24,8},{1,17},{9,25},{17,1},{25,9},{2,18},{10... | collective-permute-start | bytes 43016 | tf_op jit(solution)/shard_map/ppermute | solution.py:291
  68.1 1.3 %constant_dynamic-slice_fusion = f32[2,256]{1,0:T(2,128)} fusion(f32[2,1024]{1,0:T(2,128)} %get-tuple-element.14.weighted_ref, s32[]{:T(128)S(6)} %select_n.68), kind=kLoop, calls=%fused_computation.99 | loop fusion | bytes 4100 | tf_op jit(solution)/shard_map/dynamic_slice | solution.py:427
  69.4 1.5 %slice.201 = f32[2,8,4,128]{3,2,1,0:T(4,128)} slice(f32[2,9,5,128]{3,2,1,0:T(8,128)} %get-tuple-element.13), slice={[0:2], [0:8], [0:4], [0:128]} | slice | bytes 65536 | tf_op jit(solution)/shard_map/slice | solution.py:394
  70.8 0.7 add_select_fusion.total_ref
  71.5 2.9 %shard_map.105 = f32[1,8]{1,0:T(1,128)} custom-call(f32[28,128]{1,0:T(8,128)} %add_select_fusion.total_ref, f32[8,1024]{1,0:T(8,128)} %pad_maximum_fusion.7.packed_ref, f32[2,1024]{1,0:T(2,128)} %get-tuple-element.14.weighted_ref, f32[8,1]{1,0:T(8,128)} %copy.25.step_ref), custom_call_target="tpu_custom_call" | custom-call | tf_op jit(solution)/shard_map/pallas_call | solution.py:419
  (55 shorter events, 5.8 us)
Async XLA Ops:
  2.7 30.8 %collective-permute-start.2 = (f32[8,256]{1,0:T(8,128)S(1)}, f32[8,256]{1,0:T(8,128)S(1)}, u32[]{:S(2)}, u32[]{:S(2)}) collective-permute-start(f32[8,256]{1,0:T(8,128)S(1)} %get-tuple-element.67), channel_id=1, source_target_pairs={{0,24},{8,0},{16,8},{24,16},{1,25},{9,1},{17,9},{25,17},{2,26},{10... | collective-permute-start | bytes 24584 | tf_op jit(solution)/shard_map/ppermute | solution.py:303
  6.7 26.9 %collective-permute-start.1 = (f32[8,256]{1,0:T(8,128)S(1)}, f32[8,256]{1,0:T(8,128)S(1)}, u32[]{:S(2)}, u32[]{:S(2)}) collective-permute-start(f32[8,256]{1,0:T(8,128)S(1)} %get-tuple-element.67), channel_id=1, source_target_pairs={{0,16},{8,24},{16,0},{24,8},{1,17},{9,25},{17,1},{25,9},{2,18},{10... | collective-permute-start | bytes 24584 | tf_op jit(solution)/shard_map/ppermute | solution.py:303
  7.2 26.4 %collective-permute-start = (f32[8,256]{1,0:T(8,128)S(1)}, f32[8,256]{1,0:T(8,128)S(1)}, u32[]{:S(2)}, u32[]{:S(2)}) collective-permute-start(f32[8,256]{1,0:T(8,128)S(1)} %get-tuple-element.67), channel_id=1, source_target_pairs={{0,8},{8,16},{16,24},{24,0},{1,9},{9,17},{17,25},{25,1},{2,10},{10... | collective-permute-start | bytes 24584 | tf_op jit(solution)/shard_map/ppermute | solution.py:303
  16.2 19.5 %all-to-all-start = ((f32[32,20,128]{2,1,0:T(8,128)}), f32[32,20,128]{2,1,0:T(8,128)S(1)}, u32[]{:S(2)}, u32[]{:S(2)}) async-start(f32[32,20,128]{2,1,0:T(8,128)} %broadcast_in_dim.42), calls=%async_computation | async-start | bytes 786432 | tf_op jit(solution)/shard_map/all_to_all | solution.py:278
  22.0 7.2 %collective-permute-start.4 = (f32[2,2,4,128]{3,1,2,0:T(2,128)S(1)}, f32[2,2,4,128]{3,1,2,0:T(2,128)S(1)}, u32[]{:S(2)}, u32[]{:S(2)}) collective-permute-start(f32[2,2,4,128]{3,1,2,0:T(2,128)S(1)} %fusion.19), channel_id=1, source_target_pairs={{8,0},{16,8},{24,16},{9,1},{17,9},{25,17},{10,2},{18,10},{26,18},{... | collective-permute-start | bytes 24584 | tf_op jit(solution)/shard_map/ppermute | solution.py:27
  23.3 5.9 %collective-permute-start.3 = (f32[2,1,4,128]{3,1,2,0:T(1,128)S(1)}, f32[2,1,4,128]{3,1,2,0:T(1,128)S(1)}, u32[]{:S(2)}, u32[]{:S(2)}) collective-permute-start(f32[2,1,4,128]{3,1,2,0:T(1,128)S(1)} %fusion.20), channel_id=1, source_target_pairs={{0,8},{8,16},{16,24},{1,9},{9,17},{17,25},{2,10},{10,18},{18,26},{... | collective-permute-start | bytes 12296 | tf_op jit(solution)/shard_map/ppermute | solution.py:24
  29.2 5.2 %collective-permute-start.6 = (f32[2,11,2,128]{3,1,2,0:T(8,128)S(1)}, f32[2,11,2,128]{3,1,2,0:T(8,128)S(1)}, u32[]{:S(2)}, u32[]{:S(2)}) collective-permute-start(f32[2,11,2,128]{3,1,2,0:T(8,128)S(1)} %pad_maximum_fusion.3), channel_id=1, source_target_pairs={{1,0},{2,1},{3,2},{4,3},{5,4},{6,5},{7,6},{9,8},{10,9},{11,10},{12... | collective-permute-start | bytes 67592 | tf_op jit(solution)/shard_map/ppermute | solution.py:27
  30.5 3.9 %collective-permute-start.5 = (f32[2,11,1,128]{3,1,2,0:T(8,128)S(1)}, f32[2,11,1,128]{3,1,2,0:T(8,128)S(1)}, u32[]{:S(2)}, u32[]{:S(2)}) collective-permute-start(f32[2,11,1,128]{3,1,2,0:T(8,128)S(1)} %pad_maximum_fusion.8), channel_id=1, source_target_pairs={{0,1},{1,2},{2,3},{3,4},{4,5},{5,6},{6,7},{8,9},{9,10},{10,11},{11... | collective-permute-start | bytes 33800 | tf_op jit(solution)/shard_map/ppermute | solution.py:24
  36.3 26.3 %copy-start = (f32[8]{0:T(128)S(1)}, f32[8]{0:T(128)}, u32[]{:S(2)}) copy-start(f32[8]{0:T(128)} %param.13) | copy-start | bytes 100
  48.8 2.3 %collective-permute-start.7 = (f32[28,128]{1,0:T(8,128)S(1)}, f32[28,128]{1,0:T(8,128)S(1)}, u32[]{:S(2)}, u32[]{:S(2)}) collective-permute-start(f32[28,128]{1,0:T(8,128)S(1)} %concatenate.43), channel_id=1, source_target_pairs={{0,1},{1,0},{2,3},{3,2},{4,5},{5,4},{6,7},{7,6},{8,9},{9,8},{10,11... | collective-permute-start | bytes 43016 | tf_op jit(solution)/shard_map/ppermute | solution.py:291
  51.2 4.2 %collective-permute-start.8 = (f32[28,128]{1,0:T(8,128)S(1)}, f32[28,128]{1,0:T(8,128)S(1)}, u32[]{:S(2)}, u32[]{:S(2)}) collective-permute-start(f32[28,128]{1,0:T(8,128)S(1)} %add_select_fusion.4), channel_id=1, source_target_pairs={{0,2},{1,3},{2,0},{3,1},{4,6},{5,7},{6,4},{7,5},{8,10},{9,11},{10,... | collective-permute-start | bytes 43016 | tf_op jit(solution)/shard_map/ppermute | solution.py:291
  55.5 4.6 %collective-permute-start.9 = (f32[28,128]{1,0:T(8,128)S(1)}, f32[28,128]{1,0:T(8,128)S(1)}, u32[]{:S(2)}, u32[]{:S(2)}) collective-permute-start(f32[28,128]{1,0:T(8,128)S(1)} %add_select_fusion.3), channel_id=1, source_target_pairs={{0,4},{1,5},{2,6},{3,7},{4,0},{5,1},{6,2},{7,3},{8,12},{9,13},{10,... | collective-permute-start | bytes 43016 | tf_op jit(solution)/shard_map/ppermute | solution.py:291
  60.2 4.1 %collective-permute-start.10 = (f32[28,128]{1,0:T(8,128)S(1)}, f32[28,128]{1,0:T(8,128)S(1)}, u32[]{:S(2)}, u32[]{:S(2)}) collective-permute-start(f32[28,128]{1,0:T(8,128)S(1)} %add_select_fusion.2), channel_id=1, source_target_pairs={{0,8},{8,0},{16,24},{24,16},{1,9},{9,1},{17,25},{25,17},{2,10},{10... | collective-permute-start | bytes 43016 | tf_op jit(solution)/shard_map/ppermute | solution.py:291
  64.4 6.5 %collective-permute-start.11 = (f32[28,128]{1,0:T(8,128)S(1)}, f32[28,128]{1,0:T(8,128)S(1)}, u32[]{:S(2)}, u32[]{:S(2)}) collective-permute-start(f32[28,128]{1,0:T(8,128)S(1)} %add_select_fusion.1), channel_id=1, source_target_pairs={{0,16},{8,24},{16,0},{24,8},{1,17},{9,25},{17,1},{25,9},{2,18},{10... | collective-permute-start | bytes 43016 | tf_op jit(solution)/shard_map/ppermute | solution.py:291

commit v5 on v4

--- a/solution.py
+++ b/solution.py
@@ -12,7 +12,6 @@
 cell_depth = 2.0
 lift = 1.0
 coupling_scale = 0.05
-highest = lax.Precision.HIGHEST
 
 
 def extended(block, low, high):
@@ -61,11 +60,26 @@
         out_ref[row : row + 1, :] = total[:, chunk * 128 : (chunk + 1) * 128]
 
 
+def two_parts(values):
+    first = values.astype(jnp.bfloat16)
+    return first, (values - first.astype(jnp.float32)).astype(jnp.bfloat16)
+
+
+def product(left, right, side):
+    high, low = two_parts(left)
+    count = left.shape[0]
+    right_high, right_low = two_parts(right)
+    dims = (((1,), (side,)), ((), ()))
+    both = lax.dot_general(
+        jnp.concatenate([high, low], axis=0), right_high, dims,
+        preferred_element_type=jnp.float32,
+    )
+    rest = lax.dot_general(high, right_low, dims, preferred_element_type=jnp.float32)
+    return both[:count] + (both[count:] + rest)
+
+
 def project(columns, table):
-    return lax.dot_general(
-        columns, table, (((1,), (1,)), ((), ())),
-        precision=highest, preferred_element_type=jnp.float32,
-    )
+    return product(columns, table, 1)
 
 
 def first_kernel(sizes, first_ref, model_ref, table_ref, out_ref):
@@ -106,10 +120,7 @@
         for j in range(width):
             shift_ref[j * tall : (j + 1) * tall, :] = pltpu.roll(base, width - j, 1)
         shift_ref[width * tall : (width + 1) * tall, :] = base
-        wide = jnp.dot(
-            shift_ref[...], table_ref[field],
-            precision=highest, preferred_element_type=jnp.float32,
-        )
+        wide = product(shift_ref[...], table_ref[field], 0)
         for j in range(width + 1):
             for i in range(rows + 1):
                 data_ref[field, i, j : j + 1, :] = wide[j * tall + i : j * tall + i + 1]

time: 75.3 us -> 72.2 us (0.959)
  Pallas kernels: 18.3 us -> 15.2 us
    pallas_call x1, Pallas kernels: 6.08 us -> 4.14 us  [body(): pl.pallas_call(functools.partial(middle_kernel, sizes), in_specs=[vmem, v...]
    pallas_call x1, Pallas kernels: 4.98 us -> 3.84 us  [body(): pl.pallas_call(functools.partial(first_kernel, sizes), in_specs=[pl.Block...]
  transfers between devices with their start and end apart: 13 -> 13, of which waited for: 6 -> 6; matrix products, arithmetic and copies ran while one was open for 13% -> 13% of each run, Pallas kernels for 7% -> 5%
where the time goes in v5:
time: 72.2 us; the launch traced here: 71.3 us
  starting transfers between devices  34.1 us (47%)
  Pallas kernels  15.2 us (21%)
  other arithmetic  8.27 us (11%)
  local copies, waits for them, and re-layouts  7.08 us (10%)
  waiting for transfers between devices  5.85 us (8%)
  between operations  0.87 us (1%)
    ppermute x5, starting transfers between devices, doubled(): other = lax.ppermute(values, axis, [(i, i ^ hop) for i in range(count)])  13 us
    ppermute x2, starting transfers between devices, extended(): lax.ppermute(lax.slice_in_dim(block, size - low, None, axis=dim), axis, f...  7.58 us
    all_to_all x1, starting transfers between devices, from_all(): return lax.all_to_all(copies, ('gx', 'gy'), 0, 0, tiled=True)  5.79 us
    ppermute x3, starting transfers between devices, all_groups(): lax.ppermute(values, 'gx', [(i, (i + hop) % groups) for i in range(groups)])  5.07 us
    ppermute x5, waiting for transfers between devices, doubled(): other = lax.ppermute(values, axis, [(i, i ^ hop) for i in range(count)])  4.69 us
    pallas_call x1, Pallas kernels, body(): pl.pallas_call(functools.partial(source_kernel, total_y), in_specs=[vmem,...  4.33 us
    pallas_call x1, Pallas kernels, body(): pl.pallas_call(functools.partial(middle_kernel, sizes), in_specs=[vmem, v...  4.14 us
    pallas_call x1, Pallas kernels, body(): pl.pallas_call(functools.partial(first_kernel, sizes), in_specs=[pl.Block...  3.84 us
  transfers between devices with their start and end apart: 13, of which 6 were waited for; matrix products, arithmetic and copies ran while one was open for 13% of the time, Pallas kernels for 5%

profile of v5, /device:TPU:0, one launch (start us, length us, event | category | flops | bytes accessed | tf_op | source)
XLA Modules:
  0.0 71.3 jit_solution(2219105050881758015)
XLA Ops:
  0.6 0.7 convert_element_type.32
  1.3 0.7 convert_element_type.31
  2.0 0.7 fusion.26
  2.7 4.0 %collective-permute-start.2 = (f32[8,256]{1,0:T(8,128)S(1)}, f32[8,256]{1,0:T(8,128)S(1)}, u32[]{:S(2)}, u32[]{:S(2)}) collective-permute-start(f32[8,256]{1,0:T(8,128)S(1)} %get-tuple-element.67), channel_id=1, source_target_pairs={{0,24},{8,0},{16,8},{24,16},{1,25},{9,1},{17,9},{25,17},{2,26},{10... | collective-permute-start | bytes 24584 | tf_op jit(solution)/shard_map/ppermute | solution.py:314
  8.4 0.7 %copy_bitcast_fusion = (f32[1,8,4,128]{3,1,2,0:T(8,128)S(1)}, f32[1,8,4,128]{3,1,2,0:T(8,128)S(1)}) fusion(f32[8,4,128]{2,1,0:T(4,128)} %param.8, f32[8,4,128]{2,1,0:T(4,128)} %param.7), kind=kLoop, calls=%fused_computation.69 | loop fusion | bytes 65536 | tf_op jit(solution)/shard_map/stack | solution.py:338
  9.7 3.8 %shard_map.102 = (f32[2,1920,128]{2,1,0:T(8,128)}, f32[20,128]{1,0:T(8,128)}) custom-call(s32[2]{0:T(128)} %pad_add_fusion.first_ref, f32[2,32,128]{2,1,0:T(8,128)} %fusion.12.model_ref), custom_call_target="tpu_custom_call" | custom-call | tf_op jit(solution)/shard_map/pallas_call | solution.py:360
  13.6 1.5 %broadcast_in_dim.42 = f32[32,20,128]{2,1,0:T(8,128)} broadcast(f32[20,128]{1,0:T(8,128)} %get-tuple-element.10), dimensions={1,2} | broadcast | bytes 337920 | tf_op jit(solution)/shard_map/broadcast_in_dim | solution.py:288
  15.0 5.8 %all-to-all-start = ((f32[32,20,128]{2,1,0:T(8,128)}), f32[32,20,128]{2,1,0:T(8,128)S(1)}, u32[]{:S(2)}, u32[]{:S(2)}) async-start(f32[32,20,128]{2,1,0:T(8,128)} %broadcast_in_dim.42), calls=%async_computation | async-start | bytes 786432 | tf_op jit(solution)/shard_map/all_to_all | solution.py:289
  20.9 1.3 %collective-permute-start.4 = (f32[2,2,4,128]{3,1,2,0:T(2,128)S(1)}, f32[2,2,4,128]{3,1,2,0:T(2,128)S(1)}, u32[]{:S(2)}, u32[]{:S(2)}) collective-permute-start(f32[2,2,4,128]{3,1,2,0:T(2,128)S(1)} %fusion.19), channel_id=1, source_target_pairs={{8,0},{16,8},{24,16},{9,1},{17,9},{25,17},{10,2},{18,10},{26,18},{... | collective-permute-start | bytes 24584 | tf_op jit(solution)/shard_map/ppermute | solution.py:26
  22.2 4.5 %collective-permute-start.3 = (f32[2,1,4,128]{3,1,2,0:T(1,128)S(1)}, f32[2,1,4,128]{3,1,2,0:T(1,128)S(1)}, u32[]{:S(2)}, u32[]{:S(2)}) collective-permute-start(f32[2,1,4,128]{3,1,2,0:T(1,128)S(1)} %fusion.20), channel_id=1, source_target_pairs={{0,8},{8,16},{16,24},{1,9},{9,17},{17,25},{2,10},{10,18},{18,26},{... | collective-permute-start | bytes 12296 | tf_op jit(solution)/shard_map/ppermute | solution.py:23
  27.0 1.0 %collective-permute-done.3 = f32[2,1,4,128]{3,1,2,0:T(1,128)S(1)} collective-permute-done((f32[2,1,4,128]{3,1,2,0:T(1,128)S(1)}, f32[2,1,4,128]{3,1,2,0:T(1,128)S(1)}, u32[]{:S(2)}, u32[]{:S(2)}) %collective-permute-start.3) | collective-permute-done | bytes 4128 | tf_op jit(solution)/shard_map/ppermute | solution.py:23
  28.1 1.3 %collective-permute-start.6 = (f32[2,11,2,128]{3,1,2,0:T(8,128)S(1)}, f32[2,11,2,128]{3,1,2,0:T(8,128)S(1)}, u32[]{:S(2)}, u32[]{:S(2)}) collective-permute-start(f32[2,11,2,128]{3,1,2,0:T(8,128)S(1)} %pad_maximum_fusion.3), channel_id=1, source_target_pairs={{1,0},{2,1},{3,2},{4,3},{5,4},{6,5},{7,6},{9,8},{10,9},{11,10},{12... | collective-permute-start | bytes 67592 | tf_op jit(solution)/shard_map/ppermute | solution.py:26
  29.4 3.0 %collective-permute-start.5 = (f32[2,11,1,128]{3,1,2,0:T(8,128)S(1)}, f32[2,11,1,128]{3,1,2,0:T(8,128)S(1)}, u32[]{:S(2)}, u32[]{:S(2)}) collective-permute-start(f32[2,11,1,128]{3,1,2,0:T(8,128)S(1)} %pad_maximum_fusion.8), channel_id=1, source_target_pairs={{0,1},{1,2},{2,3},{3,4},{4,5},{5,6},{6,7},{8,9},{9,10},{10,11},{11... | collective-permute-start | bytes 33800 | tf_op jit(solution)/shard_map/ppermute | solution.py:23
  34.5 0.6 reduce_sum.54.surface_ref
  35.2 4.3 %shard_map.103 = (f32[2,1024]{1,0:T(2,128)}, f32[2,32,40]{2,1,0:T(8,128)}) custom-call(f32[20,128]{1,0:T(8,128)} %reduce_sum.54.surface_ref, f32[8,1024]{1,0:T(8,128)} %pad_maximum_fusion.7.packed_ref), custom_call_target="tpu_custom_call" | custom-call | tf_op jit(solution)/shard_map/pallas_call | solution.py:385
  39.5 4.1 %shard_map.104 = (f32[2,9,5,128]{3,2,1,0:T(8,128)}, f32[20,128]{1,0:T(8,128)}) custom-call(f32[2,32,40]{2,1,0:T(8,128)} %get-tuple-element.11.surface_ref, f32[2,1920,128]{2,1,0:T(8,128)} %get-tuple-element.12.table_ref, f32[2,4,8,128]{3,2,1,0:T(8,128)} %get-tuple-element.39.force_ref), custom_call_target="tpu_custom_call" | custom-call | tf_op jit(solution)/shard_map/pallas_call | solution.py:395
  43.6 0.9 %fusion.1 = f32[2,9,5,128]{3,1,2,0:T(8,128)S(1)} fusion(f32[1,9,5,128]{3,1,2,0:T(8,128)S(1)} %fusion.7, f32[1,9,5,128]{3,1,2,0:T(8,128)S(1)} %fusion.10, f32[2,9,5,128]{3,2,1,0:T(8,128)} %get-tuple-element.13), kind=kLoop, calls=%fused_computation.5 | loop fusion | flops 34560 | bytes 138240 | tf_op jit(solution)/shard_map/add | solution.py:406
  45.0 0.8 %concatenate.43 = f32[28,128]{1,0:T(8,128)S(1)} concatenate(f32[20,128]{1,0:T(8,128)} %get-tuple-element.15, f32[1,128]{1,0:T(1,128)S(1)} %bitcast.57, f32[1,128]{1,0:T(1,128)S(1)} %bitcast.56, f32[1,128]{1,0:T(1,128)S(1)} %bitcast.55, f32[1,128]{1,0:T(1,128)S(1)} %bitcast.58, f32[1,128]{1,0:T(1,128)S(1)} %bitcast.59, f32[1,128]{1,0:T(1,128)S(1)} %bitcast.54, ...), dimensions={0} | concatenate | bytes 28672 | tf_op jit(solution)/shard_map/concatenate | solution.py:429
  45.7 1.5 %collective-permute-start.7 = (f32[28,128]{1,0:T(8,128)S(1)}, f32[28,128]{1,0:T(8,128)S(1)}, u32[]{:S(2)}, u32[]{:S(2)}) collective-permute-start(f32[28,128]{1,0:T(8,128)S(1)} %concatenate.43), channel_id=1, source_target_pairs={{0,1},{1,0},{2,3},{3,2},{4,5},{5,4},{6,7},{7,6},{8,9},{9,8},{10,11... | collective-permute-start | bytes 43016 | tf_op jit(solution)/shard_map/ppermute | solution.py:302
  47.2 0.8 %collective-permute-done.7 = f32[28,128]{1,0:T(8,128)S(1)} collective-permute-done((f32[28,128]{1,0:T(8,128)S(1)}, f32[28,128]{1,0:T(8,128)S(1)}, u32[]{:S(2)}, u32[]{:S(2)}) %collective-permute-start.7) | collective-permute-done | bytes 14368 | tf_op jit(solution)/shard_map/ppermute | solution.py:302
  48.1 2.5 %collective-permute-start.8 = (f32[28,128]{1,0:T(8,128)S(1)}, f32[28,128]{1,0:T(8,128)S(1)}, u32[]{:S(2)}, u32[]{:S(2)}) collective-permute-start(f32[28,128]{1,0:T(8,128)S(1)} %add_select_fusion.4), channel_id=1, source_target_pairs={{0,2},{1,3},{2,0},{3,1},{4,6},{5,7},{6,4},{7,5},{8,10},{9,11},{10,... | collective-permute-start | bytes 43016 | tf_op jit(solution)/shard_map/ppermute | solution.py:302
  50.6 1.7 %collective-permute-done.8 = f32[28,128]{1,0:T(8,128)S(1)} collective-permute-done((f32[28,128]{1,0:T(8,128)S(1)}, f32[28,128]{1,0:T(8,128)S(1)}, u32[]{:S(2)}, u32[]{:S(2)}) %collective-permute-start.8) | collective-permute-done | bytes 14368 | tf_op jit(solution)/shard_map/ppermute | solution.py:302
  52.4 2.9 %collective-permute-start.9 = (f32[28,128]{1,0:T(8,128)S(1)}, f32[28,128]{1,0:T(8,128)S(1)}, u32[]{:S(2)}, u32[]{:S(2)}) collective-permute-start(f32[28,128]{1,0:T(8,128)S(1)} %add_select_fusion.3), channel_id=1, source_target_pairs={{0,4},{1,5},{2,6},{3,7},{4,0},{5,1},{6,2},{7,3},{8,12},{9,13},{10,... | collective-permute-start | bytes 43016 | tf_op jit(solution)/shard_map/ppermute | solution.py:302
  55.4 1.7 %collective-permute-done.9 = f32[28,128]{1,0:T(8,128)S(1)} collective-permute-done((f32[28,128]{1,0:T(8,128)S(1)}, f32[28,128]{1,0:T(8,128)S(1)}, u32[]{:S(2)}, u32[]{:S(2)}) %collective-permute-start.9) | collective-permute-done | bytes 14368 | tf_op jit(solution)/shard_map/ppermute | solution.py:302
  57.1 2.4 %collective-permute-start.10 = (f32[28,128]{1,0:T(8,128)S(1)}, f32[28,128]{1,0:T(8,128)S(1)}, u32[]{:S(2)}, u32[]{:S(2)}) collective-permute-start(f32[28,128]{1,0:T(8,128)S(1)} %add_select_fusion.2), channel_id=1, source_target_pairs={{0,8},{8,0},{16,24},{24,16},{1,9},{9,1},{17,25},{25,17},{2,10},{10... | collective-permute-start | bytes 43016 | tf_op jit(solution)/shard_map/ppermute | solution.py:302
  59.5 0.7 copy.25.step_ref
  60.2 0.6 copy.26
  61.3 3.7 %collective-permute-start.11 = (f32[28,128]{1,0:T(8,128)S(1)}, f32[28,128]{1,0:T(8,128)S(1)}, u32[]{:S(2)}, u32[]{:S(2)}) collective-permute-start(f32[28,128]{1,0:T(8,128)S(1)} %add_select_fusion.1), channel_id=1, source_target_pairs={{0,16},{8,24},{16,0},{24,8},{1,17},{9,25},{17,1},{25,9},{2,18},{10... | collective-permute-start | bytes 43016 | tf_op jit(solution)/shard_map/ppermute | solution.py:302
  65.0 1.3 %constant_dynamic-slice_fusion = f32[2,256]{1,0:T(2,128)} fusion(f32[2,1024]{1,0:T(2,128)} %get-tuple-element.14.weighted_ref, s32[]{:T(128)S(6)} %select_n.68), kind=kLoop, calls=%fused_computation.99 | loop fusion | bytes 4100 | tf_op jit(solution)/shard_map/dynamic_slice | solution.py:438
  66.3 1.5 %slice.201 = f32[2,8,4,128]{3,2,1,0:T(4,128)} slice(f32[2,9,5,128]{3,2,1,0:T(8,128)} %get-tuple-element.13), slice={[0:2], [0:8], [0:4], [0:128]} | slice | bytes 65536 | tf_op jit(solution)/shard_map/slice | solution.py:405
  67.8 0.7 add_select_fusion.total_ref
  68.4 2.9 %shard_map.105 = f32[1,8]{1,0:T(1,128)} custom-call(f32[28,128]{1,0:T(8,128)} %add_select_fusion.total_ref, f32[8,1024]{1,0:T(8,128)} %pad_maximum_fusion.7.packed_ref, f32[2,1024]{1,0:T(2,128)} %get-tuple-element.14.weighted_ref, f32[8,1]{1,0:T(8,128)} %copy.25.step_ref), custom_call_target="tpu_custom_call" | custom-call | tf_op jit(solution)/shard_map/pallas_call | solution.py:430
  (55 shorter events, 5.8 us)
Async XLA Ops:
  2.7 29.7 %collective-permute-start.2 = (f32[8,256]{1,0:T(8,128)S(1)}, f32[8,256]{1,0:T(8,128)S(1)}, u32[]{:S(2)}, u32[]{:S(2)}) collective-permute-start(f32[8,256]{1,0:T(8,128)S(1)} %get-tuple-element.67), channel_id=1, source_target_pairs={{0,24},{8,0},{16,8},{24,16},{1,25},{9,1},{17,9},{25,17},{2,26},{10... | collective-permute-start | bytes 24584 | tf_op jit(solution)/shard_map/ppermute | solution.py:314
  6.7 25.7 %collective-permute-start.1 = (f32[8,256]{1,0:T(8,128)S(1)}, f32[8,256]{1,0:T(8,128)S(1)}, u32[]{:S(2)}, u32[]{:S(2)}) collective-permute-start(f32[8,256]{1,0:T(8,128)S(1)} %get-tuple-element.67), channel_id=1, source_target_pairs={{0,16},{8,24},{16,0},{24,8},{1,17},{9,25},{17,1},{25,9},{2,18},{10... | collective-permute-start | bytes 24584 | tf_op jit(solution)/shard_map/ppermute | solution.py:314
  7.2 25.2 %collective-permute-start = (f32[8,256]{1,0:T(8,128)S(1)}, f32[8,256]{1,0:T(8,128)S(1)}, u32[]{:S(2)}, u32[]{:S(2)}) collective-permute-start(f32[8,256]{1,0:T(8,128)S(1)} %get-tuple-element.67), channel_id=1, source_target_pairs={{0,8},{8,16},{16,24},{24,0},{1,9},{9,17},{17,25},{25,1},{2,10},{10... | collective-permute-start | bytes 24584 | tf_op jit(solution)/shard_map/ppermute | solution.py:314
  15.0 19.5 %all-to-all-start = ((f32[32,20,128]{2,1,0:T(8,128)}), f32[32,20,128]{2,1,0:T(8,128)S(1)}, u32[]{:S(2)}, u32[]{:S(2)}) async-start(f32[32,20,128]{2,1,0:T(8,128)} %broadcast_in_dim.42), calls=%async_computation | async-start | bytes 786432 | tf_op jit(solution)/shard_map/all_to_all | solution.py:289
  20.9 7.2 %collective-permute-start.4 = (f32[2,2,4,128]{3,1,2,0:T(2,128)S(1)}, f32[2,2,4,128]{3,1,2,0:T(2,128)S(1)}, u32[]{:S(2)}, u32[]{:S(2)}) collective-permute-start(f32[2,2,4,128]{3,1,2,0:T(2,128)S(1)} %fusion.19), channel_id=1, source_target_pairs={{8,0},{16,8},{24,16},{9,1},{17,9},{25,17},{10,2},{18,10},{26,18},{... | collective-permute-start | bytes 24584 | tf_op jit(solution)/shard_map/ppermute | solution.py:26
  22.2 5.9 %collective-permute-start.3 = (f32[2,1,4,128]{3,1,2,0:T(1,128)S(1)}, f32[2,1,4,128]{3,1,2,0:T(1,128)S(1)}, u32[]{:S(2)}, u32[]{:S(2)}) collective-permute-start(f32[2,1,4,128]{3,1,2,0:T(1,128)S(1)} %fusion.20), channel_id=1, source_target_pairs={{0,8},{8,16},{16,24},{1,9},{9,17},{17,25},{2,10},{10,18},{18,26},{... | collective-permute-start | bytes 12296 | tf_op jit(solution)/shard_map/ppermute | solution.py:23
  28.1 5.2 %collective-permute-start.6 = (f32[2,11,2,128]{3,1,2,0:T(8,128)S(1)}, f32[2,11,2,128]{3,1,2,0:T(8,128)S(1)}, u32[]{:S(2)}, u32[]{:S(2)}) collective-permute-start(f32[2,11,2,128]{3,1,2,0:T(8,128)S(1)} %pad_maximum_fusion.3), channel_id=1, source_target_pairs={{1,0},{2,1},{3,2},{4,3},{5,4},{6,5},{7,6},{9,8},{10,9},{11,10},{12... | collective-permute-start | bytes 67592 | tf_op jit(solution)/shard_map/ppermute | solution.py:26
  29.4 3.9 %collective-permute-start.5 = (f32[2,11,1,128]{3,1,2,0:T(8,128)S(1)}, f32[2,11,1,128]{3,1,2,0:T(8,128)S(1)}, u32[]{:S(2)}, u32[]{:S(2)}) collective-permute-start(f32[2,11,1,128]{3,1,2,0:T(8,128)S(1)} %pad_maximum_fusion.8), channel_id=1, source_target_pairs={{0,1},{1,2},{2,3},{3,4},{4,5},{5,6},{6,7},{8,9},{9,10},{10,11},{11... | collective-permute-start | bytes 33800 | tf_op jit(solution)/shard_map/ppermute | solution.py:23
  35.2 24.3 %copy-start = (f32[8]{0:T(128)S(1)}, f32[8]{0:T(128)}, u32[]{:S(2)}) copy-start(f32[8]{0:T(128)} %param.13) | copy-start | bytes 100
  45.7 2.3 %collective-permute-start.7 = (f32[28,128]{1,0:T(8,128)S(1)}, f32[28,128]{1,0:T(8,128)S(1)}, u32[]{:S(2)}, u32[]{:S(2)}) collective-permute-start(f32[28,128]{1,0:T(8,128)S(1)} %concatenate.43), channel_id=1, source_target_pairs={{0,1},{1,0},{2,3},{3,2},{4,5},{5,4},{6,7},{7,6},{8,9},{9,8},{10,11... | collective-permute-start | bytes 43016 | tf_op jit(solution)/shard_map/ppermute | solution.py:302
  48.1 4.2 %collective-permute-start.8 = (f32[28,128]{1,0:T(8,128)S(1)}, f32[28,128]{1,0:T(8,128)S(1)}, u32[]{:S(2)}, u32[]{:S(2)}) collective-permute-start(f32[28,128]{1,0:T(8,128)S(1)} %add_select_fusion.4), channel_id=1, source_target_pairs={{0,2},{1,3},{2,0},{3,1},{4,6},{5,7},{6,4},{7,5},{8,10},{9,11},{10,... | collective-permute-start | bytes 43016 | tf_op jit(solution)/shard_map/ppermute | solution.py:302
  52.4 4.6 %collective-permute-start.9 = (f32[28,128]{1,0:T(8,128)S(1)}, f32[28,128]{1,0:T(8,128)S(1)}, u32[]{:S(2)}, u32[]{:S(2)}) collective-permute-start(f32[28,128]{1,0:T(8,128)S(1)} %add_select_fusion.3), channel_id=1, source_target_pairs={{0,4},{1,5},{2,6},{3,7},{4,0},{5,1},{6,2},{7,3},{8,12},{9,13},{10,... | collective-permute-start | bytes 43016 | tf_op jit(solution)/shard_map/ppermute | solution.py:302
  57.1 4.1 %collective-permute-start.10 = (f32[28,128]{1,0:T(8,128)S(1)}, f32[28,128]{1,0:T(8,128)S(1)}, u32[]{:S(2)}, u32[]{:S(2)}) collective-permute-start(f32[28,128]{1,0:T(8,128)S(1)} %add_select_fusion.2), channel_id=1, source_target_pairs={{0,8},{8,0},{16,24},{24,16},{1,9},{9,1},{17,25},{25,17},{2,10},{10... | collective-permute-start | bytes 43016 | tf_op jit(solution)/shard_map/ppermute | solution.py:302
  61.3 6.5 %collective-permute-start.11 = (f32[28,128]{1,0:T(8,128)S(1)}, f32[28,128]{1,0:T(8,128)S(1)}, u32[]{:S(2)}, u32[]{:S(2)}) collective-permute-start(f32[28,128]{1,0:T(8,128)S(1)} %add_select_fusion.1), channel_id=1, source_target_pairs={{0,16},{8,24},{16,0},{24,8},{1,17},{9,25},{17,1},{25,9},{2,18},{10... | collective-permute-start | bytes 43016 | tf_op jit(solution)/shard_map/ppermute | solution.py:302
